TPU v7x, 32 devices: a whole 2x2x4 slice. The times are simulated.
32 devices in a mesh: slab: 4 (over y, x), point: 2 (over core), win: 4 (over z).
Axes of the slice: x: 2, y: 2, z: 4, core: 2. Of those that a mesh axis runs over, the one named last changes fastest.
Arguments:
- diag_blocks: float32 [4, 2, 256, 256], P('slab'), as said below
- couplings: float32 [4, 2, 256, 256], P('slab'), may hold values from -0.25 to 0.25
- subspace: float32 [8, 4, 2, 256, 128], P('win', 'slab'), may hold values from -6 to 6
- widths: int32 [8], P('win'), may hold values from 32 to 128, as said below
- owner_order: int32 [8], replicated, may hold values from 0 to 7, each once
- centers: float32 [8], P('win'), may hold values from -2.5 to 2.5
- radii: float32 [8], P('win'), may hold values from 0.6 to 1.5
Outputs:
- filtered: float32 [8, 4, 2, 256, 128], P('win', 'slab', None, 'point')
Inputs may be any that keep to these rules, and one draw needn't show every extreme that they name: `widths`: columns in use of each window; some window uses all 128. `owner_order`: a permutation of the windows. `diag_blocks`: each diagonal block is Hermitian: index 0 symmetric, index 1 antisymmetric.
All inputs are finite; a program needn't handle non-finite values.
Results may differ from a plain program's by a relative error of at most 0.0003.
Values sent between devices are 32-bit elements; how exact they have to be, the bound alone decides.
No kernel may reach another device: no remote copies, remote signals or barrier semaphores. Data moves between devices by JAX's collectives and lax.ppermute only.
A program may use at most 128 MiB of HBM per device.

v0:
```python
import math

import jax
import jax.numpy as jnp
from jax import lax
from jax.sharding import PartitionSpec as P

HIGHEST_PRECISION = lax.Precision.HIGHEST


def from_behind(value, axis, steps):
    count = lax.axis_size(axis)
    first, last = (max(0, -steps), min(count, count - steps))
    return lax.ppermute(value, axis, [(source, source + steps) for source in range(first, last)])


def complex_product(left, right):
    real_part = jnp.dot(
        left[0], right[0], precision=HIGHEST_PRECISION, preferred_element_type=jnp.float32
    ) - jnp.dot(left[1], right[1], precision=HIGHEST_PRECISION, preferred_element_type=jnp.float32)
    imag_part = jnp.dot(
        left[0], right[1], precision=HIGHEST_PRECISION, preferred_element_type=jnp.float32
    ) + jnp.dot(left[1], right[0], precision=HIGHEST_PRECISION, preferred_element_type=jnp.float32)
    return jnp.stack([real_part, imag_part])


def adjoint(matrix):
    return jnp.stack([matrix[0].T, -matrix[1].T])


def plain_dot(left, right):
    return jnp.dot(left, right, precision=HIGHEST_PRECISION, preferred_element_type=jnp.float32)


def normal_solve(system, rhs_block):
    sys_real = system[0]
    sys_imag = system[1]
    gram_real = plain_dot(sys_real.T, sys_real) + plain_dot(sys_imag.T, sys_imag)
    gram_imag = plain_dot(sys_real.T, sys_imag) - plain_dot(sys_imag.T, sys_real)
    stacked = jnp.concatenate(
        [jnp.concatenate([gram_real, -gram_imag], 1), jnp.concatenate([gram_imag, gram_real], 1)], 0
    )
    factor = jnp.linalg.cholesky(stacked)
    proj_real = plain_dot(sys_real.T, rhs_block[0]) + plain_dot(sys_imag.T, rhs_block[1])
    proj_imag = plain_dot(sys_real.T, rhs_block[1]) - plain_dot(sys_imag.T, rhs_block[0])
    solved = jax.scipy.linalg.cho_solve((factor, True), jnp.concatenate([proj_real, proj_imag], 0))
    order = sys_real.shape[0]
    return jnp.stack([solved[:order], solved[order:]])


def halving_solve(shifted, link, source, slab_index, slab_count):
    order = shifted.shape[1]
    columns = source.shape[2]
    levels = slab_count.bit_length() - 1
    from_lower = from_behind(link, "slab", 1)
    lower_link = -adjoint(from_lower)
    upper_link = -link
    diagonal = shifted
    loaded = source
    stored = jnp.zeros((2, order, 2 * order + columns), jnp.float32)
    for level in range(levels):
        stride = 1 << level
        eliminate = slab_index % (2 * stride) == stride
        retained = slab_index % (2 * stride) == 0

        def reduce_row(operands):
            return normal_solve(
                operands[0], jnp.concatenate([operands[1], operands[2], operands[3]], axis=2)
            )

        def skip_row(operands):
            return jnp.zeros((2, order, 2 * order + columns), jnp.float32)

        packed = lax.cond(
            eliminate, reduce_row, skip_row, (diagonal, upper_link, lower_link, loaded)
        )
        stored = jnp.where(eliminate, packed, stored)
        from_below = from_behind(packed, "slab", stride)
        from_above = from_behind(packed, "slab", -stride)

        def merge_rows(operands):
            diag_now, upper_now, lower_now, loaded_now, below_now, above_now = operands
            via_lower = complex_product(lower_now, below_now)
            via_upper = complex_product(upper_now, above_now)
            new_diag = diag_now - via_lower[:, :, :order] - via_upper[:, :, order : 2 * order]
            new_upper = -via_upper[:, :, :order]
            new_lower = -via_lower[:, :, order : 2 * order]
            new_loaded = loaded_now - via_lower[:, :, 2 * order :] - via_upper[:, :, 2 * order :]
            return (new_diag, new_upper, new_lower, new_loaded)

        def keep_rows(operands):
            return (operands[0], operands[1], operands[2], operands[3])

        diagonal, upper_link, lower_link, loaded = lax.cond(
            retained,
            merge_rows,
            keep_rows,
            (diagonal, upper_link, lower_link, loaded, from_below, from_above),
        )

    def root_solve(operands):
        return normal_solve(operands[0], operands[1])

    def no_root(operands):
        return jnp.zeros((2, order, columns), jnp.float32)

    solution = lax.cond(slab_index == 0, root_solve, no_root, (diagonal, loaded))
    for level in range(levels - 1, -1, -1):
        stride = 1 << level
        eliminate = slab_index % (2 * stride) == stride
        below_known = from_behind(solution, "slab", stride)
        above_known = from_behind(solution, "slab", -stride)

        def finish_row(operands):
            kept_now, below_now, above_now, current = operands
            return (
                kept_now[:, :, 2 * order :]
                - complex_product(kept_now[:, :, :order], above_now)
                - complex_product(kept_now[:, :, order : 2 * order], below_now)
            )

        def leave_row(operands):
            return operands[3]

        solution = lax.cond(
            eliminate, finish_row, leave_row, (stored, below_known, above_known, solution)
        )
    return solution


def per_device(diag_blocks, couplings, subspace, widths, owner_order, centers, radii):
    slab_index = lax.axis_index("slab")
    slab_count = lax.axis_size("slab")
    point_index = lax.axis_index("point")
    point_count = lax.axis_size("point")
    win_index = lax.axis_index("win")
    win_count = lax.axis_size("win")
    order = diag_blocks.shape[2]
    columns = subspace.shape[4]
    local_count = subspace.shape[0]
    angle = 2.0 * math.pi * (point_index.astype(jnp.float32) + 0.5) / point_count
    identity = jnp.eye(order, dtype=jnp.float32)
    keep_link = (slab_index < slab_count - 1).astype(jnp.float32)
    link = couplings[0] * keep_link
    weighted_all = []
    for local in range(local_count):
        center = centers[local]
        radius = radii[local]
        zeta_re = center + radius * jnp.cos(angle)
        zeta_im = radius * jnp.sin(angle)
        shifted = jnp.stack(
            [zeta_re * identity - diag_blocks[0, 0], zeta_im * identity - diag_blocks[0, 1]]
        )
        live = (jnp.arange(columns, dtype=jnp.int32) < widths[local]).astype(jnp.float32)
        source = subspace[local, 0] * live
        solution = halving_solve(shifted, link, source, slab_index, slab_count)
        weight_re = radius * jnp.cos(angle) / point_count
        weight_im = radius * jnp.sin(angle) / point_count
        weighted_all.append(
            jnp.stack(
                [
                    weight_re * solution[0] - weight_im * solution[1],
                    weight_re * solution[1] + weight_im * solution[0],
                ]
            )
        )
    weighted = jnp.stack(weighted_all)
    rows_part = order // point_count
    total_windows = local_count * win_count
    mine = win_index * local_count + jnp.arange(local_count, dtype=jnp.int32)
    slot_hit = (owner_order[:, None] == mine[None, :]).astype(jnp.float32)
    slot_terms_all = jnp.einsum("sj,jabc->sabc", slot_hit, weighted, precision=HIGHEST_PRECISION)
    arranged = slot_terms_all.reshape(win_count, local_count, 2, point_count, rows_part, columns)
    term_all = jnp.transpose(arranged, (3, 0, 1, 2, 4, 5)).reshape(
        point_count * total_windows * 2 * rows_part, columns
    )
    share = lax.psum_scatter(term_all, ("point", "win"), scatter_dimension=0, tiled=True)
    return share.reshape(local_count, 1, 2, rows_part, columns)


def solution(mesh):
    placed = (
        P("slab", None, None, None),
        P("slab", None, None, None),
        P("win", "slab", None, None, None),
        P("win"),
        P(),
        P("win"),
        P("win"),
    )
    return jax.shard_map(
        per_device,
        mesh=mesh,
        in_specs=placed,
        out_specs=P("win", "slab", None, "point", None),
        check_vma=False,
    )
```

profile of v0, /device:TPU:1, one launch (start us, length us, event | category | flops | bytes accessed | tf_op | source)
XLA Modules:
  0.0 1240.6 jit_solution(505564558138150097)
XLA Ops:
  7.8 4.7 collective-permute-start
  19.2 3.2 collective-permute-done
  24.2 10.1 conditional.14
  34.3 167.8 %collective-permute-start.1 = (f32[2,256,640]{2,1,0:T(8,128)}, f32[2,256,640]{2,1,0:T(8,128)}, u32[]{:S(2)}, u32[]{:S(2)}) collective-permute-start(f32[2,256,640]{2,1,0:T(8,128)} %get-tuple-element.994), channel_id=1, source_target_pairs={{0,8},{8,16},{16,24},{1,9},{9,17},{17,25},{2,10},{10,18},{18,26},{... | collective-permute-start | bytes 3932168 | tf_op jit(solution)/shard_map/ppermute | solution.py:14
  204.0 7.1 conditional.21
  212.4 160.7 %collective-permute-start.9 = (f32[2,256,640]{2,1,0:T(8,128)}, f32[2,256,640]{2,1,0:T(8,128)}, u32[]{:S(2)}, u32[]{:S(2)}) collective-permute-start(f32[2,256,640]{2,1,0:T(8,128)} %get-tuple-element.1000), channel_id=1, source_target_pairs={{0,8},{8,16},{16,24},{1,9},{9,17},{17,25},{2,10},{10,18},{18,26},{... | collective-permute-start | bytes 3932168 | tf_op jit(solution)/shard_map/ppermute | solution.py:14
  374.3 18.1 %conditional.15 = (f32[2,256,256]{2,1,0:T(8,128)S(1)}, f32[2,256,256]{2,1,0:T(8,128)}, f32[2,256,256]{2,1,0:T(8,128)}, f32[2,256,128]{2,1,0:T(8,128)S(1)}) conditional(s32[]{:T(128)} %convert_element_type.51, (f32[2,256,256]{2,1,0:T(8,128)S(1)}, f32[2,256,256]{2,1,0:T(8,128)S(1)}, f32[2,256,256]{1,2,0:T(8,128)S(1)}, ...), branch_computations={%region_10.13_spmd, %region_11.14_spmd} | conditional | flops 4028497920 | bytes 28311640 | solution.py:94
  377.2 2.1 fusion.2
  392.3 6.9 conditional.16
  399.2 165.5 %collective-permute-start.3 = (f32[2,256,640]{2,1,0:T(8,128)}, f32[2,256,640]{2,1,0:T(8,128)}, u32[]{:S(2)}, u32[]{:S(2)}) collective-permute-start(f32[2,256,640]{2,1,0:T(8,128)} %get-tuple-element.995), channel_id=1, source_target_pairs={{0,16},{8,24},{1,17},{9,25},{2,18},{10,26},{3,19},{11,27},{4,20},{... | collective-permute-start | bytes 3932168 | tf_op jit(solution)/shard_map/ppermute | solution.py:14
  566.1 17.2 %conditional.22 = (f32[2,256,256]{2,1,0:T(8,128)S(1)}, f32[2,256,256]{2,1,0:T(8,128)S(1)}, f32[2,256,256]{2,1,0:T(8,128)}, f32[2,256,128]{2,1,0:T(8,128)S(1)}) conditional(s32[]{:T(128)} %convert_element_type.51, (f32[2,256,256]{2,1,0:T(8,128)S(1)}, f32[2,256,256]{2,1,0:T(8,128)S(1)}, f32[2,256,256]{1,2,0:T(8,128)S(1)}, ...), branch_computations={%region_24.28_spmd, %region_25.29_spmd} | conditional | flops 4028497920 | bytes 26214460 | solution.py:94
  566.3 2.1 fusion.176
  572.3 2.0 fusion.169
  583.3 6.5 conditional.23
  589.7 162.9 %collective-permute-start.11 = (f32[2,256,640]{2,1,0:T(8,128)}, f32[2,256,640]{2,1,0:T(8,128)}, u32[]{:S(2)}, u32[]{:S(2)}) collective-permute-start(f32[2,256,640]{2,1,0:T(8,128)} %get-tuple-element.1001), channel_id=1, source_target_pairs={{0,16},{8,24},{1,17},{9,25},{2,18},{10,26},{3,19},{11,27},{4,20},{... | collective-permute-start | bytes 3932168 | tf_op jit(solution)/shard_map/ppermute | solution.py:14
  754.1 16.4 %conditional.17 = ((f32[2,256,256]{2,1,0:T(8,128)S(1)}, f32[2,256,128]{2,1,0:T(8,128)S(1)})) conditional(s32[]{:T(128)} %convert_element_type.50, (f32[2,256,256]{2,1,0:T(8,128)S(1)}, f32[2,256,128]{2,1,0:T(8,128)S(1)}) %tuple.137, (f32[2,256,256]{2,1,0:T(8,128)}, f32[2,256,640]{2,1,0:T(8,128)}, f32[2,256,256]{2,1,0:T(8,128)S(1)}, ...), branch_computations={%region_14.17_spmd, %region_15.18_spmd} | conditional | flops 4027973632 | bytes 22020120 | solution.py:94
  754.1 2.0 fusion.46
  756.1 2.0 fusion.42
  758.1 2.0 fusion.50
  760.1 2.0 fusion.43
  762.1 2.0 fusion.52
  764.1 2.0 fusion.44
  766.1 2.0 fusion.56
  768.1 2.0 fusion.45
  770.5 174.0 %conditional.18 = (f32[2,256,128]{2,1,0:T(8,128)}) conditional(s32[]{:T(128)} %convert_element_type.49, () %tuple.132, (f32[2,256,256]{2,1,0:T(8,128)S(1)}, f32[2,256,128]{2,1,0:T(8,128)S(1)}) %get-tuple-element.996), branch_computations={%region_16.19_spmd, %region_17.21_spmd} | conditional | flops 2118222336 | bytes 38148012 | solution.py:107
  775.2 2.5 copy.21
  780.4 11.7 cholesky.782
  793.3 9.8 custom-call.57
  807.0 11.9 cholesky.801
  821.3 9.8 custom-call.58
  835.0 13.2 %cholesky.822 = f32[128,128]{1,0:T(8,128)} custom-call(f32[128,128]{1,0:T(8,128)} %cholesky.1088), custom_call_target="Cholesky" | custom-call | tf_op jit(solution)/shard_map/cond/branch_1_fun/jit(cholesky)/cholesky | solution.py:43
  851.0 11.3 custom-call.59
  865.4 11.9 cholesky.839
  879.2 2.3 select_select_fusion.1
  881.6 13.7 %while.14 = (s32[]{:T(128)}, f32[512,512]{1,0:T(8,128)}, s32[4,2]{0,1:T(2,128)S(1)}, f32[4,128,128]{2,1,0:T(8,128)}, s32[]{:T(128)}) while((s32[]{:T(128)}, f32[512,512]{1,0:T(8,128)}, s32[4,2]{0,1:T(2,128)S(1)}, f32[4,128,128]{2,1,0:T(8,128)}, s32[]{:T(128)}) %tuple.332), condition=%wide.while_cond.1, body=%wide.while_body.1.sunk | while | flops 2 | bytes 132705 | solution.py:46
  882.2 2.8 bitcast_dynamic-update-slice_fusion.15
  885.7 2.8 bitcast_dynamic-update-slice_fusion.15
  889.1 2.8 bitcast_dynamic-update-slice_fusion.15
  892.5 2.8 bitcast_dynamic-update-slice_fusion.15
  895.3 40.7 %custom-call.60 = f32[4,128,128]{1,2,0:T(8,128)} custom-call(f32[4,128,128]{2,1,0:T(8,128)} %get-tuple-element.432), custom_call_target="InvertDiagBlocksLowerTriangular" | custom-call | tf_op jit(solution)/shard_map/cond/branch_1_fun/jit(_cho_solve)/triangular_solve | solution.py:46
  945.8 5.4 collective-permute-start.6
  951.2 16.1 %conditional.24 = ((f32[2,256,256]{2,1,0:T(8,128)S(1)}, f32[2,256,128]{2,1,0:T(8,128)S(1)})) conditional(s32[]{:T(128)} %convert_element_type.50, (f32[2,256,256]{2,1,0:T(8,128)S(1)}, f32[2,256,128]{2,1,0:T(8,128)S(1)}) %tuple.147, (f32[2,256,256]{2,1,0:T(8,128)}, f32[2,256,640]{2,1,0:T(8,128)}, f32[2,256,256]{2,1,0:T(8,128)S(1)}, ...), branch_computations={%region_28.32_spmd, %region_29.33_spmd} | conditional | flops 4027973632 | bytes 22020120 | solution.py:94
  958.9 2.0 fusion.218
  960.8 2.0 fusion.210
  964.8 2.0 fusion.211
  967.3 157.7 %conditional.25 = (f32[2,256,128]{2,1,0:T(8,128)}) conditional(s32[]{:T(128)} %convert_element_type.49, () %tuple.142, (f32[2,256,256]{2,1,0:T(8,128)S(1)}, f32[2,256,128]{2,1,0:T(8,128)S(1)}) %get-tuple-element.1002), branch_computations={%region_30.34_spmd, %region_31.35_spmd} | conditional | flops 2118222336 | bytes 35264344 | solution.py:107
  974.6 11.7 cholesky.998
  986.5 9.8 custom-call.69
  998.8 11.9 cholesky.1017
  1012.8 9.8 custom-call.70
  1024.2 11.7 cholesky.1038
  1037.2 9.8 custom-call.71
  1048.5 12.1 cholesky.1055
  1063.0 14.4 %while.17 = (s32[]{:T(128)}, f32[512,512]{1,0:T(8,128)}, s32[4,2]{0,1:T(2,128)S(1)}, f32[4,128,128]{2,1,0:T(8,128)}, s32[]{:T(128)}) while((s32[]{:T(128)}, f32[512,512]{1,0:T(8,128)}, s32[4,2]{0,1:T(2,128)S(1)}, f32[4,128,128]{2,1,0:T(8,128)}, s32[]{:T(128)}) %tuple.323), condition=%wide.while_cond.1.clone, body=%wide.while_body.1.clone.sunk | while | flops 2 | bytes 132705 | solution.py:46
  1063.7 2.9 bitcast_dynamic-update-slice_fusion.12
  1067.3 2.9 bitcast_dynamic-update-slice_fusion.12
  1070.9 2.9 bitcast_dynamic-update-slice_fusion.12
  1074.6 2.9 bitcast_dynamic-update-slice_fusion.12
  1077.4 40.2 %custom-call.72 = f32[4,128,128]{1,2,0:T(8,128)S(1)} custom-call(f32[4,128,128]{2,1,0:T(8,128)} %get-tuple-element.435), custom_call_target="InvertDiagBlocksLowerTriangular" | custom-call | tf_op jit(solution)/shard_map/cond/branch_1_fun/jit(_cho_solve)/triangular_solve | solution.py:46
  1126.3 4.7 collective-permute-start.14
  1132.5 4.0 collective-permute-start.8
  1137.8 14.0 %collective-permute-start.16 = (f32[2,256,128]{2,1,0:T(8,128)}, f32[2,256,128]{2,1,0:T(8,128)}, u32[]{:S(2)}, u32[]{:S(2)}) collective-permute-start(f32[2,256,128]{2,1,0:T(8,128)} %get-tuple-element.1004), channel_id=1, source_target_pairs={{0,8},{8,16},{16,24},{1,9},{9,17},{17,25},{2,10},{10,18},{18,26},{... | collective-permute-start | bytes 786440 | tf_op jit(solution)/shard_map/ppermute | solution.py:14
  1151.9 3.2 collective-permute-done.15
  1160.9 72.6 %reduce-scatter.2.cloned.1.call-done = f32[512,128]{1,0:T(8,128)} async-done(((f32[4096,128]{1,0:T(8,128)}), f32[512,128]{1,0:T(8,128)}) %reduce-scatter.2.cloned.1.call-update) | async-done | bytes 262160 | tf_op jit(solution)/shard_map/reduce_scatter | solution.py:177
  (240 shorter events, 127.5 us)
Async XLA Ops:
  6.5 6.1 copy-start.38
  6.5 6.7 copy-start.39
  6.5 7.3 copy-start.40
  6.5 12.5 %copy-start.28 = (f32[1,2,256,256]{3,2,1,0:T(8,128)S(1)}, f32[1,2,256,256]{3,2,1,0:T(8,128)}, u32[]{:S(2)}) copy-start(f32[1,2,256,256]{3,2,1,0:T(8,128)} %param.40) | copy-start | bytes 1572868
  6.5 1226.9 %reduce-scatter.2.cloned.1.call-start = ((), (), s32[]{:S(2)}) async-start(), calls=%async_computation.1 | async-start | bytes 2359296 | tf_op jit(solution)/shard_map/reduce_scatter | solution.py:177
  6.6 12.5 %copy-start.37 = (f32[2,1,2,256,128]{4,3,2,1,0:T(8,128)S(1)}, f32[2,1,2,256,128]{4,3,2,1,0:T(8,128)}, u32[]{:S(2)}) copy-start(f32[2,1,2,256,128]{4,3,2,1,0:T(8,128)} %param.42) | copy-start | bytes 1572868
  7.8 14.5 %collective-permute-start = (f32[2,256,256]{2,1,0:T(8,128)S(1)}, f32[2,256,256]{2,1,0:T(8,128)}, u32[]{:S(2)}, u32[]{:S(2)}) collective-permute-start(f32[2,256,256]{2,1,0:T(8,128)S(1)} %get-tuple-element.565), channel_id=1, source_target_pairs={{0,8},{8,16},{16,24},{1,9},{9,17},{17,25},{2,10},{10,18},{18,26},{... | collective-permute-start | bytes 1572872 | tf_op jit(solution)/shard_map/ppermute | solution.py:14
  19.1 5.1 copy-start.15
  19.1 5.1 copy-start.16
  34.3 339.9 %collective-permute-start.1 = (f32[2,256,640]{2,1,0:T(8,128)}, f32[2,256,640]{2,1,0:T(8,128)}, u32[]{:S(2)}, u32[]{:S(2)}) collective-permute-start(f32[2,256,640]{2,1,0:T(8,128)} %get-tuple-element.994), channel_id=1, source_target_pairs={{0,8},{8,16},{16,24},{1,9},{9,17},{17,25},{2,10},{10,18},{18,26},{... | collective-permute-start | bytes 3932168 | tf_op jit(solution)/shard_map/ppermute | solution.py:14
  202.1 172.2 %collective-permute-start.2 = (f32[2,256,640]{2,1,0:T(8,128)}, f32[2,256,640]{2,1,0:T(8,128)}, u32[]{:S(2)}, u32[]{:S(2)}) collective-permute-start(f32[2,256,640]{2,1,0:T(8,128)} %get-tuple-element.994), channel_id=1, source_target_pairs={{8,0},{16,8},{24,16},{9,1},{17,9},{25,17},{10,2},{18,10},{26,18},{... | collective-permute-start | bytes 3932168 | tf_op jit(solution)/shard_map/ppermute | solution.py:14
  211.1 355.0 %collective-permute-start.10 = (f32[2,256,640]{2,1,0:T(8,128)}, f32[2,256,640]{2,1,0:T(8,128)}, u32[]{:S(2)}, u32[]{:S(2)}) collective-permute-start(f32[2,256,640]{2,1,0:T(8,128)} %get-tuple-element.1000), channel_id=1, source_target_pairs={{8,0},{16,8},{24,16},{9,1},{17,9},{25,17},{10,2},{18,10},{26,18},{... | collective-permute-start | bytes 3932168 | tf_op jit(solution)/shard_map/ppermute | solution.py:14
  212.4 353.7 %collective-permute-start.9 = (f32[2,256,640]{2,1,0:T(8,128)}, f32[2,256,640]{2,1,0:T(8,128)}, u32[]{:S(2)}, u32[]{:S(2)}) collective-permute-start(f32[2,256,640]{2,1,0:T(8,128)} %get-tuple-element.1000), channel_id=1, source_target_pairs={{0,8},{8,16},{16,24},{1,9},{9,17},{17,25},{2,10},{10,18},{18,26},{... | collective-permute-start | bytes 3932168 | tf_op jit(solution)/shard_map/ppermute | solution.py:14
  374.5 0.8 copy-start
  377.2 2.1 copy-start.1
  399.2 354.8 %collective-permute-start.3 = (f32[2,256,640]{2,1,0:T(8,128)}, f32[2,256,640]{2,1,0:T(8,128)}, u32[]{:S(2)}, u32[]{:S(2)}) collective-permute-start(f32[2,256,640]{2,1,0:T(8,128)} %get-tuple-element.995), channel_id=1, source_target_pairs={{0,16},{8,24},{1,17},{9,25},{2,18},{10,26},{3,19},{11,27},{4,20},{... | collective-permute-start | bytes 3932168 | tf_op jit(solution)/shard_map/ppermute | solution.py:14
  564.8 189.3 %collective-permute-start.4 = (f32[2,256,640]{2,1,0:T(8,128)}, f32[2,256,640]{2,1,0:T(8,128)}, u32[]{:S(2)}, u32[]{:S(2)}) collective-permute-start(f32[2,256,640]{2,1,0:T(8,128)} %get-tuple-element.995), channel_id=1, source_target_pairs={{16,0},{24,8},{17,1},{25,9},{18,2},{26,10},{19,3},{27,11},{20,4},{... | collective-permute-start | bytes 3932168 | tf_op jit(solution)/shard_map/ppermute | solution.py:14
  566.3 4.0 copy-start.2
  589.7 361.5 %collective-permute-start.11 = (f32[2,256,640]{2,1,0:T(8,128)}, f32[2,256,640]{2,1,0:T(8,128)}, u32[]{:S(2)}, u32[]{:S(2)}) collective-permute-start(f32[2,256,640]{2,1,0:T(8,128)} %get-tuple-element.1001), channel_id=1, source_target_pairs={{0,16},{8,24},{1,17},{9,25},{2,18},{10,26},{3,19},{11,27},{4,20},{... | collective-permute-start | bytes 3932168 | tf_op jit(solution)/shard_map/ppermute | solution.py:14
  752.6 198.6 %collective-permute-start.12 = (f32[2,256,640]{2,1,0:T(8,128)}, f32[2,256,640]{2,1,0:T(8,128)}, u32[]{:S(2)}, u32[]{:S(2)}) collective-permute-start(f32[2,256,640]{2,1,0:T(8,128)} %get-tuple-element.1001), channel_id=1, source_target_pairs={{16,0},{24,8},{17,1},{25,9},{18,2},{26,10},{19,3},{27,11},{20,4},{... | collective-permute-start | bytes 3932168 | tf_op jit(solution)/shard_map/ppermute | solution.py:14
  772.1 1.2 copy-start.20
  772.1 1.2 copy-start.21
  773.4 0.7 copy-start.24
  779.4 1.0 copy-start.13
  806.3 0.7 copy-start.36
  936.0 2.3 copy-start.3
  936.0 2.5 copy-start.29
  944.5 186.7 %collective-permute-start.5 = (f32[2,256,128]{2,1,0:T(8,128)}, f32[2,256,128]{2,1,0:T(8,128)}, u32[]{:S(2)}, u32[]{:S(2)}) collective-permute-start(f32[2,256,128]{2,1,0:T(8,128)} %get-tuple-element.997), channel_id=1, source_target_pairs={{16,0},{24,8},{17,1},{25,9},{18,2},{26,10},{19,3},{27,11},{20,4},{... | collective-permute-start | bytes 786440 | tf_op jit(solution)/shard_map/ppermute | solution.py:14
  945.8 185.4 %collective-permute-start.6 = (f32[2,256,128]{2,1,0:T(8,128)}, f32[2,256,128]{2,1,0:T(8,128)}, u32[]{:S(2)}, u32[]{:S(2)}) collective-permute-start(f32[2,256,128]{2,1,0:T(8,128)} %get-tuple-element.997), channel_id=1, source_target_pairs={{0,16},{8,24},{1,17},{9,25},{2,18},{10,26},{3,19},{11,27},{4,20},{... | collective-permute-start | bytes 786440 | tf_op jit(solution)/shard_map/ppermute | solution.py:14
  968.7 1.2 copy-start.22
  969.9 0.7 copy-start.25
  973.6 1.0 copy-start.14
  1077.4 41.7 %copy-start.4 = (f32[512,512]{1,0:T(8,128)S(1)}, f32[512,512]{1,0:T(8,128)}, u32[]{:S(2)}) copy-start(f32[512,512]{1,0:T(8,128)} %get-tuple-element.1024) | copy-start | bytes 3145732 | tf_op jit(solution)/shard_map/cond
  1125.0 11.5 collective-permute-start.13
  1126.3 10.2 collective-permute-start.14
  1131.2 20.7 %collective-permute-start.7 = (f32[2,256,128]{2,1,0:T(8,128)}, f32[2,256,128]{2,1,0:T(8,128)S(1)}, u32[]{:S(2)}, u32[]{:S(2)}) collective-permute-start(f32[2,256,128]{2,1,0:T(8,128)} %get-tuple-element.998), channel_id=1, source_target_pairs={{8,0},{16,8},{24,16},{9,1},{17,9},{25,17},{10,2},{18,10},{26,18},{... | collective-permute-start | bytes 786440 | tf_op jit(solution)/shard_map/ppermute | solution.py:14
  1132.5 19.4 %collective-permute-start.8 = (f32[2,256,128]{2,1,0:T(8,128)}, f32[2,256,128]{2,1,0:T(8,128)S(1)}, u32[]{:S(2)}, u32[]{:S(2)}) collective-permute-start(f32[2,256,128]{2,1,0:T(8,128)} %get-tuple-element.998), channel_id=1, source_target_pairs={{0,8},{8,16},{16,24},{1,9},{9,17},{17,25},{2,10},{10,18},{18,26},{... | collective-permute-start | bytes 786440 | tf_op jit(solution)/shard_map/ppermute | solution.py:14
  1136.5 18.6 %collective-permute-start.15 = (f32[2,256,128]{2,1,0:T(8,128)}, f32[2,256,128]{2,1,0:T(8,128)S(1)}, u32[]{:S(2)}, u32[]{:S(2)}) collective-permute-start(f32[2,256,128]{2,1,0:T(8,128)} %get-tuple-element.1004), channel_id=1, source_target_pairs={{8,0},{16,8},{24,16},{9,1},{17,9},{25,17},{10,2},{18,10},{26,18},{... | collective-permute-start | bytes 786440 | tf_op jit(solution)/shard_map/ppermute | solution.py:14
  1137.8 17.3 %collective-permute-start.16 = (f32[2,256,128]{2,1,0:T(8,128)}, f32[2,256,128]{2,1,0:T(8,128)}, u32[]{:S(2)}, u32[]{:S(2)}) collective-permute-start(f32[2,256,128]{2,1,0:T(8,128)} %get-tuple-element.1004), channel_id=1, source_target_pairs={{0,8},{8,16},{16,24},{1,9},{9,17},{17,25},{2,10},{10,18},{18,26},{... | collective-permute-start | bytes 786440 | tf_op jit(solution)/shard_map/ppermute | solution.py:14
  1155.3 2.1 copy-start.41
Sparse Core Ops, SparseCore 0:
  1161.0 72.3 reduce-scatter.1
where the time goes:
time: 1250 us; the launch traced here: 1240 us
  starting transfers between devices  700 us (56%)
  other arithmetic  264 us (21%)
  matrix products  97.4 us (8%)
  waiting for transfers between devices  79 us (6%)
  local copies, waits for them, and re-layouts  48.2 us (4%)
  loops' own time  33.3 us (3%)
  between operations  18.1 us (1%)
    ppermute x17, starting transfers between devices, from_behind(): lax.ppermute(value, axis, [(source, source + steps) for source in range(f...  700 us
    another operation x28, other arithmetic, normal_solve(): factor = jnp.linalg.cholesky(stacked)  163 us
    another operation x8, other arithmetic, normal_solve(): jax.scipy.linalg.cho_solve((factor, True), jnp.concatenate([proj_real, pr...  84.4 us
    reduce_scatter x1, waiting for transfers between devices, per_device(): lax.psum_scatter(term_all, ('point', 'win'), scatter_dimension=0, tiled=T...  72.6 us
    another operation x26, local copies, waits for them, and re-layouts, normal_solve(): jax.scipy.linalg.cho_solve((factor, True), jnp.concatenate([proj_real, pr...  28.1 us
    another operation x4, loops' own time, halving_solve(): lax.cond(eliminate, reduce_row, skip_row, (diagonal, upper_link, lower_li...  25.8 us
  transfers between devices with their start and end apart: 18, of which 3 were waited for; matrix products, arithmetic and copies ran while one was open for 32% of the time, Pallas kernels for 0%

commit v1 on v0

v1 whole, which is shorter than its diff:
```python
import math

import jax
import jax.numpy as jnp
from jax import lax
from jax.experimental import pallas as pl
from jax.experimental.pallas import tpu as pltpu
from jax.sharding import PartitionSpec as P

F32 = jnp.float32
BF16 = jnp.bfloat16
COARSE = 0.1


def dot(left, right):
    return lax.dot_general(left, right, (((1,), (0,)), ((), ())), preferred_element_type=F32)


def hi_lo(value):
    high = value.astype(BF16)
    return high, (value - high.astype(F32)).astype(BF16)


def packed_pair(value):
    high, low = hi_lo(value)
    return jnp.concatenate([high, low], 1)


def left_triple(pair):
    half = pair.shape[1] // 2
    return jnp.concatenate([pair, pair[:, :half]], 1)


def embed(re, im):
    return jnp.concatenate([jnp.concatenate([re, im], 1), jnp.concatenate([-im, re], 1)], 0)


def embed_triple(re, im):
    re_high, re_low = hi_lo(re)
    im_high, im_low = hi_lo(im)
    high = embed(re_high, im_high)
    return jnp.concatenate([high, high, embed(re_low, im_low)], 0)


def times_i(value):
    half = value.shape[1] // 2
    return jnp.concatenate([-value[:, half:], value[:, :half]], 1)


def column_triple(value):
    high, low = hi_lo(jnp.concatenate([value, times_i(value)], 0))
    return jnp.concatenate([high, high, low], 0)


def eye_of(order):
    row = lax.broadcasted_iota(jnp.int32, (order, order), 0)
    col = lax.broadcasted_iota(jnp.int32, (order, order), 1)
    return (row == col).astype(F32)


def invert(s_re, s_im, zeta_im, s_emb, x_ref, work):
    n = s_re.shape[0]
    eye = eye_of(n)
    s_emb[...] = embed_triple(s_re, s_im)
    adj_re, adj_im = s_re.T, -s_im.T
    gram = dot(jnp.concatenate([adj_re, adj_im], 1).astype(BF16), s_emb[0 : 2 * n, :])
    sums = jnp.sum(jnp.abs(gram), 0, keepdims=True)
    bound_sq = jnp.max(sums[:, :n] + sums[:, n:], axis=1, keepdims=True)
    bound = jnp.sqrt(bound_sq)
    ratio = jnp.abs(zeta_im) / bound
    shrink = 1.0 / (1.0 + ratio + ratio * ratio)
    alpha = shrink / bound_sq
    beta = shrink / bound * jnp.where(zeta_im > 0, 1.0, -1.0)
    x_re = alpha * adj_re
    x_im = alpha * adj_im - beta * eye
    x_ref[...] = jnp.concatenate([x_re, x_im], 1)
    work[:, 0 : 2 * n] = embed(
        eye - alpha * gram[:, :n] - beta * s_im, beta * s_re - alpha * gram[:, n:]
    ).astype(BF16)
    work[:, 2 * n :] = embed(x_re, x_im).astype(BF16)

    def double(size):
        both = dot(work[0:n, 0 : 2 * n], work[...])
        work[:, 0 : 2 * n] = embed(both[:, :n], both[:, n : 2 * n]).astype(BF16)
        x_now = x_ref[...] + both[:, 2 * n :]
        x_ref[...] = x_now
        work[:, 2 * n :] = embed(x_now[:, :n], x_now[:, n:]).astype(BF16)
        return size * size

    lax.while_loop(lambda size: size > COARSE, double, shrink[0, 0])
    wide_eye = jnp.concatenate([eye, jnp.zeros((n, n), F32)], 1)
    rest = wide_eye - dot(work[0:n, 2 * n :], s_emb[0 : 2 * n, :])
    x_ref[...] = x_ref[...] + dot(rest.astype(BF16), work[:, 2 * n :])
    x_now = x_ref[...]
    rest = wide_eye - dot(left_triple(packed_pair(x_now)), s_emb[...])
    return x_now + dot(rest.astype(BF16), embed(x_now[:, :n], x_now[:, n:]).astype(BF16))


def pick(flag, if_true, if_false):
    return jnp.where(flag, if_true, if_false)


def rows_of(direct, swapped, plane, point):
    mine, other = direct[plane], swapped[plane]
    return jnp.concatenate([pick(point == 0, mine, other), pick(point == 0, other, mine)], 0)


def unpack_diag(packed):
    n = packed.shape[0]
    row = lax.broadcasted_iota(jnp.int32, (n, n), 0)
    col = lax.broadcasted_iota(jnp.int32, (n, n), 1)
    turned = packed.T
    re = jnp.where(row >= col, packed, turned)
    im = jnp.where(row < col, packed, jnp.where(row > col, -turned, 0.0))
    return re, im


def oriented(flag, here, there):
    re = pick(flag, here[0], there[0].T)
    im = pick(flag, here[1], -there[1].T)
    adj_re = pick(flag, here[0].T, there[0])
    adj_im = pick(flag, -here[1].T, there[1])
    return re, im, adj_re, adj_im


def slot_of(scal, owner, slab, dims):
    win_count, local_count, parts = dims
    window = owner[scal[0] * local_count + slab // parts]
    shift = lax.rem(scal[0] - window // local_count + win_count, win_count)
    return shift, lax.rem(window, local_count)


def look_up(tables, row, shift, index):
    value = tables[0][row, index]
    for k in range(1, len(tables)):
        value = jnp.where(shift == k, tables[k][row, index], value)
    return value


def contour(scal, owner, tables, dims, point_count):
    shift, index = slot_of(scal, owner, scal[1], dims)
    center = look_up(tables, 0, shift, index)
    radius = look_up(tables, 1, shift, index)
    cosine = jnp.float32(0.0)
    sine = jnp.float32(0.0)
    for p in range(point_count):
        angle = 2.0 * math.pi * (p + 0.5) / point_count
        cosine = jnp.where(scal[2] == p, jnp.float32(math.cos(angle)), cosine)
        sine = jnp.where(scal[2] == p, jnp.float32(math.sin(angle)), sine)
    return center + radius * cosine, radius * sine, radius * cosine / point_count, radius * sine / point_count


def per_device(diag_blocks, couplings, subspace, widths, owner_order, centers, radii):
    slab = lax.axis_index("slab")
    slab_count = lax.axis_size("slab")
    point = lax.axis_index("point")
    point_count = lax.axis_size("point")
    win = lax.axis_index("win")
    win_count = lax.axis_size("win")
    n = diag_blocks.shape[2]
    columns = subspace.shape[4]
    local_count = subspace.shape[0]
    parts = slab_count // local_count
    width = columns // parts
    lanes = 2 * width
    half = n // point_count
    dims = (win_count, local_count, parts)
    assert slab_count == 4 and point_count == 2 and parts == 2

    smem = pl.BlockSpec(memory_space=pltpu.SMEM)
    vmem = pl.BlockSpec(memory_space=pltpu.VMEM)
    grant = pltpu.CompilerParams(vmem_limit_bytes=56 * 1024 * 1024)
    pair_shape = jax.ShapeDtypeStruct((n, 4 * n), BF16)
    scratch = [
        pltpu.VMEM((6 * n, 2 * n), BF16),
        pltpu.VMEM((n, 2 * n), F32),
        pltpu.VMEM((2 * n, 4 * n), BF16),
    ]

    def exchange(value, distance):
        return lax.ppermute(value, "slab", [(i, i ^ distance) for i in range(slab_count)])

    def swap(value):
        return lax.ppermute(value, "point", [(i, i ^ 1) for i in range(point_count)])

    def along_win(value, shift):
        return lax.ppermute(value, "win", [(i, (i + shift) % win_count) for i in range(win_count)])

    scal = jnp.stack([win, slab, point]).astype(jnp.int32)
    table = jnp.stack([centers, radii, widths.astype(F32)])
    row = lax.broadcasted_iota(jnp.int32, (n, n), 0)
    col = lax.broadcasted_iota(jnp.int32, (n, n), 1)
    packed = jnp.where(row >= col, diag_blocks[0, 0], diag_blocks[0, 1])
    shard = jnp.concatenate([packed[None], couplings[0]], 0)
    carried = lax.dynamic_slice_in_dim(shard, point * half, half, 1)
    from_x = exchange(carried, 1)
    from_y = exchange(carried, 2)
    tables = [table] + [along_win(table, k) for k in range(1, win_count)]
    block = lax.dynamic_slice_in_dim(subspace[:, 0], point * half, half, 2)
    blocks = [block] + [along_win(block, k) for k in range(1, win_count)]
    relay = jnp.where(point == 0, from_y, from_x)
    flat = [(2 * s, 2 * (s ^ 1)) for s in range(slab_count)]
    flat += [(2 * s + 1, 2 * (s ^ 2) + 1) for s in range(slab_count)]
    from_far = lax.ppermute(relay, ("slab", "point"), flat)
    from_x = (from_x, swap(from_x))
    from_y = (from_y, swap(from_y))
    from_far = (from_far, swap(from_far))

    def first_body(*refs):
        scal, owner = refs[:2]
        tables = refs[2 : 2 + win_count]
        diag, x_out, s_emb, x_ref, work = refs[2 + win_count :]
        z_re, z_im, _, _ = contour(scal, owner, tables, dims, point_count)
        eye = eye_of(n)
        x_out[...] = packed_pair(
            invert(z_re * eye - diag[0, 0], z_im * eye - diag[0, 1], z_im, s_emb, x_ref, work)
        )

    head = [scal, owner_order] + tables
    head_specs = [smem] * len(head)
    x_own = pl.pallas_call(
        first_body,
        out_shape=pair_shape,
        in_specs=head_specs + [vmem],
        out_specs=vmem,
        scratch_shapes=scratch,
        compiler_params=grant,
    )(*head, diag_blocks)

    def second_body(*refs):
        scal, owner = refs[:2]
        tables = refs[2 : 2 + win_count]
        (x_own, own_c, x_dir, x_swp, x_out, w_out, l_out, s_emb, x_ref, work) = refs[2 + win_count :]
        z_re, z_im, _, _ = contour(scal, owner, tables, dims, point_count)
        p = scal[2]
        near = [rows_of(x_dir, x_swp, k, p) for k in range(3)]
        even = lax.rem(scal[1], 2) == 0
        re, im, adj_re, adj_im = oriented(even, (own_c[0, 0], own_c[0, 1]), (near[1], near[2]))
        solved = dot(left_triple(x_own[...]), embed_triple(re, im))
        w_out[...] = packed_pair(solved)
        left = packed_pair(jnp.concatenate([adj_re, adj_im], 1))
        l_out[...] = left
        update = dot(left_triple(left), embed_triple(solved[:, :n], solved[:, n:]))
        d_re, d_im = unpack_diag(near[0])
        eye = eye_of(n)
        x_out[...] = packed_pair(
            invert(
                z_re * eye - d_re - update[:, :n],
                z_im * eye - d_im - update[:, n:],
                z_im,
                s_emb,
                x_ref,
                work,
            )
        )

    x_near, w_near, l_near = pl.pallas_call(
        second_body,
        out_shape=[pair_shape] * 3,
        in_specs=head_specs + [vmem] * 4,
        out_specs=[vmem] * 3,
        scratch_shapes=scratch,
        compiler_params=grant,
    )(*head, x_own, couplings, *from_x)

    def third_body(*refs):
        scal, owner = refs[:2]
        tables = refs[2 : 2 + win_count]
        (x_near, x_dir, x_swp, y_dir, y_swp, x_out, w_out, l_out, s_emb, x_ref, work, s_ref) = refs[
            2 + win_count :
        ]
        z_re, z_im, _, _ = contour(scal, owner, tables, dims, point_count)
        p = scal[2]
        even = lax.rem(scal[1], 2) == 0
        chain = lax.rem(scal[1], 2) == scal[1] // 2
        d_re, d_im = unpack_diag(rows_of(y_dir, y_swp, 0, p))
        eye = eye_of(n)
        s_ref[...] = jnp.concatenate([z_re * eye - d_re, z_im * eye - d_im], 1)

        @pl.when(chain)
        def _():
            re, im, adj_re, adj_im = oriented(
                even,
                [rows_of(x_dir, x_swp, k, p) for k in (1, 2)],
                [rows_of(y_dir, y_swp, k, p) for k in (1, 2)],
            )
            solved = dot(left_triple(x_near[...]), embed_triple(re, im))
            w_out[...] = packed_pair(solved)
            left = packed_pair(jnp.concatenate([adj_re, adj_im], 1))
            l_out[...] = left
            s_ref[...] = s_ref[...] - dot(
                left_triple(left), embed_triple(solved[:, :n], solved[:, n:])
            )

        x_out[...] = packed_pair(invert(s_ref[:, :n], s_ref[:, n:], z_im, s_emb, x_ref, work))

    x_side, w_mid, l_mid = pl.pallas_call(
        third_body,
        out_shape=[pair_shape] * 3,
        in_specs=head_specs + [vmem] * 5,
        out_specs=[vmem] * 3,
        scratch_shapes=scratch + [pltpu.VMEM((n, 2 * n), F32)],
        compiler_params=grant,
    )(*head, x_near, *from_x, *from_y)

    def route_body(*refs):
        scal, owner = refs[:2]
        tables = refs[2 : 2 + win_count]
        blocks = refs[2 + win_count : 2 + 2 * win_count]
        outs = refs[2 + 2 * win_count :]
        lane = lax.broadcasted_iota(jnp.int32, (half, lanes), 1)
        for k in range(slab_count):
            target = scal[1] ^ k
            part = lax.rem(target, parts)
            shift, index = slot_of(scal, owner, target, dims)
            live = look_up(tables, 2, shift, index).astype(jnp.int32)
            for k_win in range(win_count):

                @pl.when(shift == k_win)
                def _():
                    re = blocks[k_win][index, 0]
                    im = blocks[k_win][index, 1]
                    mine = jnp.where(
                        part == 0,
                        jnp.where(lane < width, re, pltpu.roll(im, width, 1)),
                        jnp.where(lane < width, pltpu.roll(re, width, 1), im),
                    )
                    number = part * width + lax.rem(lane, width)
                    outs[k][...] = jnp.where(number < live, mine, 0.0)

    piece = jax.ShapeDtypeStruct((half, lanes), F32)
    routed = pl.pallas_call(
        route_body,
        out_shape=[piece] * slab_count,
        in_specs=head_specs + [vmem] * win_count,
        out_specs=[vmem] * slab_count,
        compiler_params=grant,
    )(*head, *blocks)
    rhs = jnp.stack([routed[0]] + [exchange(routed[k], k) for k in range(1, slab_count)])
    rhs = (rhs, swap(rhs))

    def fourth_body(*refs):
        scal, owner = refs[:2]
        tables = refs[2 : 2 + win_count]
        (x_own, x_near, x_side, w_near, l_near, w_mid, l_mid, own_c, y_dir, y_swp, f_dir, f_swp) = refs[
            2 + win_count : 14 + win_count
        ]
        (x_out, w_far, l_far, w_cross, l_cross, w_last, l_last, s_emb, x_ref, work, s_ref) = refs[
            14 + win_count :
        ]
        z_re, z_im, _, _ = contour(scal, owner, tables, dims, point_count)
        p = scal[2]
        even = lax.rem(scal[1], 2) == 0
        chain = lax.rem(scal[1], 2) == scal[1] // 2
        far = [rows_of(f_dir, f_swp, k, p) for k in range(3)]
        side = [rows_of(y_dir, y_swp, k, p) for k in (1, 2)]
        d_re, d_im = unpack_diag(far[0])
        eye = eye_of(n)
        s_ref[...] = jnp.concatenate([z_re * eye - d_re, z_im * eye - d_im], 1)

        @pl.when(chain)
        def _():
            zero = jnp.zeros((n, 4 * n), BF16)
            w_cross[...] = zero
            l_cross[...] = zero
            w_far[...] = w_mid[...]
            l_far[...] = l_mid[...]

        @pl.when(jnp.logical_not(chain))
        def _():
            odd = jnp.logical_not(even)
            re, im, adj_re, adj_im = oriented(odd, (own_c[0, 0], own_c[0, 1]), (far[1], far[2]))
            cross = dot(left_triple(x_own[...]), embed_triple(re, im))
            w_cross[...] = packed_pair(cross)
            left = packed_pair(jnp.concatenate([adj_re, adj_im], 1))
            l_cross[...] = left
            cross_emb = embed_triple(cross[:, :n], cross[:, n:])
            fill = dot(left_triple(l_near[...]), cross_emb)
            w_pair = w_near[...]
            high, low = w_pair[:, : 2 * n], w_pair[:, 2 * n :]
            near_high = embed(high[:, :n], high[:, n:])
            near_emb = jnp.concatenate([near_high, near_high, embed(low[:, :n], low[:, n:])], 0)
            both = dot(left_triple(left), jnp.concatenate([near_emb, cross_emb], 1))
            back = packed_pair(both[:, : 2 * n])
            l_far[...] = back
            solved = dot(left_triple(x_near[...]), embed_triple(fill[:, :n], fill[:, n:]))
            w_far[...] = packed_pair(solved)
            s_ref[...] = (
                s_ref[...]
                - both[:, 2 * n :]
                - dot(left_triple(back), embed_triple(solved[:, :n], solved[:, n:]))
            )

        re, im, adj_re, adj_im = oriented(even, side, (far[1], far[2]))
        solved = dot(left_triple(x_side[...]), embed_triple(re, im))
        w_last[...] = packed_pair(solved)
        left = packed_pair(jnp.concatenate([adj_re, adj_im], 1))
        l_last[...] = left
        s_now = s_ref[...] - dot(left_triple(left), embed_triple(solved[:, :n], solved[:, n:]))
        x_out[...] = packed_pair(invert(s_now[:, :n], s_now[:, n:], z_im, s_emb, x_ref, work))

    x_far, w_far, l_far, w_cross, l_cross, w_last, l_last = pl.pallas_call(
        fourth_body,
        out_shape=[pair_shape] * 7,
        in_specs=head_specs + [vmem] * 12,
        out_specs=[vmem] * 7,
        scratch_shapes=scratch + [pltpu.VMEM((n, 2 * n), F32)],
        compiler_params=grant,
    )(*head, x_own, x_near, x_side, w_near, l_near, w_mid, l_mid, couplings, *from_y, *from_far)

    def solve_body(*refs):
        scal, owner = refs[:2]
        tables = refs[2 : 2 + win_count]
        (x_own, x_near, x_side, x_far, w_near, l_near, w_cross, l_cross, w_far, l_far, w_last, l_last) = refs[
            2 + win_count : 14 + win_count
        ]
        b_dir, b_swp, keep, send = refs[14 + win_count :]
        _, _, weight_re, weight_im = contour(scal, owner, tables, dims, point_count)
        p = scal[2]
        chain = lax.rem(scal[1], 2) == scal[1] // 2

        def apply(ref, value):
            return dot(left_triple(ref[...]), column_triple(value))

        b_own, b_near, b_side, b_far = [rows_of(b_dir, b_swp, k, p) for k in range(4)]
        u_own = apply(x_own, b_own)
        b_near = b_near + apply(l_near, u_own)
        b_far = b_far + apply(l_cross, u_own)
        u_near = apply(x_near, b_near)
        step = apply(l_far, u_near)
        b_side = b_side + pick(chain, step, 0.0)
        b_far = b_far + pick(chain, 0.0, step)
        u_side = apply(x_side, b_side)
        b_far = b_far + apply(l_last, u_side)
        far = apply(x_far, b_far)
        side = u_side + apply(w_last, far)
        near = u_near + apply(w_far, pick(chain, side, far))
        own = u_own + apply(w_near, near) + apply(w_cross, far)
        for k, value in enumerate((own, near, side, far)):
            value = weight_re * value + weight_im * times_i(value)
            keep[k] = pick(p == 0, value[:half], value[half:])
            send[k] = pick(p == 0, value[half:], value[:half])

    quad = jax.ShapeDtypeStruct((slab_count, half, lanes), F32)
    keep, send = pl.pallas_call(
        solve_body,
        out_shape=[quad] * 2,
        in_specs=head_specs + [vmem] * 14,
        out_specs=[vmem] * 2,
        compiler_params=grant,
    )(
        *head, x_own, x_near, x_side, x_far, w_near, l_near, w_cross, l_cross, w_far, l_far, w_last, l_last, *rhs
    )
    total = keep + swap(send)
    shares = [total[0]] + [exchange(total[k], k) for k in range(1, slab_count)]

    def place_body(*refs):
        scal = refs[0]
        shares = refs[1 : 1 + slab_count]
        out = refs[1 + slab_count]
        lane = lax.broadcasted_iota(jnp.int32, (half, lanes), 1)
        for slot in range(local_count):
            found = []
            for part in range(parts):
                distance = scal[1] ^ (slot * parts + part)
                value = shares[0][...]
                for k in range(1, slab_count):
                    value = jnp.where(distance == k, shares[k][...], value)
                found.append(value)
            low, high = found
            out[slot, 0, 0] = jnp.where(lane < width, low, pltpu.roll(high, width, 1))
            out[slot, 0, 1] = jnp.where(lane < width, pltpu.roll(low, width, 1), high)

    return pl.pallas_call(
        place_body,
        out_shape=jax.ShapeDtypeStruct((local_count, 1, 2, half, columns), F32),
        in_specs=[smem] + [vmem] * slab_count,
        out_specs=vmem,
        compiler_params=grant,
    )(scal, *shares)


def solution(mesh):
    placed = (
        P("slab", None, None, None),
        P("slab", None, None, None),
        P("win", "slab", None, None, None),
        P("win"),
        P(),
        P("win"),
        P("win"),
    )
    return jax.shard_map(
        per_device,
        mesh=mesh,
        in_specs=placed,
        out_specs=P("win", "slab", None, "point", None),
        check_vma=False,
    )
```

time: 1250 us -> 109 us (0.09)
  starting transfers between devices: 700 us -> 33.6 us
  other arithmetic: 264 us -> 3.77 us
  matrix products: 97.4 us -> 0 us
  waiting for transfers between devices: 79 us -> 20.5 us
  Pallas kernels: 0 us -> 41.9 us
  local copies, waits for them, and re-layouts: 48.2 us -> 6.56 us
  loops' own time: 33.3 us -> 0 us
  between operations: 18.1 us -> 0.19 us
    ppermute x17 -> x20, starting transfers between devices: 700 us -> 33.6 us  [the longest x6 13.8 us: along_win(): lax.ppermute(value, 'win', [(i, (i + shift) % win_count) for i in range(w...]
    another operation x47 -> x4, other arithmetic: 250 us -> 1.56 us  [the longest x1 0.93 us: per_device(): jnp.stack([routed[0]] + [exchange(routed[k], k) for k in range(1, slab_co...]
    dot_general x49 -> x0, matrix products: 73.8 us -> none  [the longest x8 15.8 us: complex_product(): jnp.dot(left[1], right[0], precision=HIGHEST_PRECISION, preferred_element...]
    reduce_scatter x1 -> x0, waiting for transfers between devices: 72.6 us -> none  [per_device(): lax.psum_scatter(term_all, ('point', 'win'), scatter_dimension=0, tiled=T...]
    pallas_call x0 -> x7, Pallas kernels: none -> 41.9 us  [the longest x1 8.98 us: per_device(): pl.pallas_call(fourth_body, out_shape=[pair_shape] * 7, in_specs=head_spe...]
    another operation x41 -> x0, local copies, waits for them, and re-layouts: 35.8 us -> none  [the longest x26 28.1 us: normal_solve(): jax.scipy.linalg.cho_solve((factor, True), jnp.concatenate([proj_real, pr...]
    another operation x16 -> x0, loops' own time: 33.3 us -> none  [the longest x4 25.8 us: halving_solve(): lax.cond(eliminate, reduce_row, skip_row, (diagonal, upper_link, lower_li...]
    another operation x40 -> x0, matrix products: 23.6 us -> none  [the longest x12 15 us: normal_solve(): factor = jnp.linalg.cholesky(stacked)]
  transfers between devices with their start and end apart: 18 -> 20, of which waited for: 3 -> 8; matrix products, arithmetic and copies ran while one was open for 32% -> 2% of each run, Pallas kernels for 0% -> 30%
where the time goes in v1:
time: 109 us; the launch traced here: 107 us
  Pallas kernels  41.9 us (38%)
  starting transfers between devices  33.6 us (31%)
  waiting for transfers between devices  20.5 us (19%)
  local copies, waits for them, and re-layouts  6.56 us (6%)
  other arithmetic  3.77 us (3%)
    ppermute x6, starting transfers between devices, along_win(): lax.ppermute(value, 'win', [(i, (i + shift) % win_count) for i in range(w...  13.8 us
    ppermute x8, starting transfers between devices, exchange(): lax.ppermute(value, 'slab', [(i, i ^ distance) for i in range(slab_count)])  12.2 us
    ppermute x6, waiting for transfers between devices, along_win(): lax.ppermute(value, 'win', [(i, (i + shift) % win_count) for i in range(w...  10.8 us
    pallas_call x1, Pallas kernels, per_device(): pl.pallas_call(fourth_body, out_shape=[pair_shape] * 7, in_specs=head_spe...  8.98 us
    pallas_call x1, Pallas kernels, per_device(): pl.pallas_call(solve_body, out_shape=[quad] * 2, in_specs=head_specs + [v...  8.04 us
    ppermute x8, waiting for transfers between devices, exchange(): lax.ppermute(value, 'slab', [(i, i ^ distance) for i in range(slab_count)])  7.99 us
    pallas_call x1, Pallas kernels, per_device(): pl.pallas_call(third_body, out_shape=[pair_shape] * 3, in_specs=head_spec...  7.57 us
    pallas_call x1, Pallas kernels, per_device(): pl.pallas_call(second_body, out_shape=[pair_shape] * 3, in_specs=head_spe...  7.34 us
  transfers between devices with their start and end apart: 20, of which 8 were waited for; matrix products, arithmetic and copies ran while one was open for 2% of the time, Pallas kernels for 30%

profile of v1, /device:TPU:1, one launch (start us, length us, event | category | flops | bytes accessed | tf_op | source)
XLA Modules:
  0.0 106.5 jit_solution(845067570204988654)
XLA Ops:
  0.0 1.1 %bitcast_select_fusion = f32[1,256,256]{2,1,0:T(8,128)S(1)} fusion(f32[1,2,256,256]{3,2,1,0:T(8,128)} %refs_6_.1), kind=kLoop, calls=%fused_computation.4 | loop fusion | flops 131072 | bytes 786432 | tf_op jit(solution)/shard_map/jit(_where)/select_n | solution.py:193
  1.1 0.1 copy-done.1
  1.3 2.1 %collective-permute-start.3 = (f32[3,128,256]{2,1,0:T(8,128)S(1)}, f32[3,128,256]{2,1,0:T(8,128)S(1)}, u32[]{:S(2)}, u32[]{:S(2)}) collective-permute-start(f32[3,128,256]{2,1,0:T(8,128)S(1)} %fusion), channel_id=1, source_target_pairs={{0,8},{8,0},{16,24},{24,16},{1,9},{9,1},{17,25},{25,17},{2,10},{10... | collective-permute-start | bytes 1179656 | tf_op jit(solution)/shard_map/ppermute | solution.py:181
  3.4 1.2 %collective-permute-start.5 = (f32[3,128,256]{2,1,0:T(8,128)S(1)}, f32[3,128,256]{2,1,0:T(8,128)S(1)}, u32[]{:S(2)}, u32[]{:S(2)}) collective-permute-start(f32[3,128,256]{2,1,0:T(8,128)S(1)} %fusion), channel_id=1, source_target_pairs={{0,16},{8,24},{16,0},{24,8},{1,17},{9,25},{17,1},{25,9},{2,18},{10... | collective-permute-start | bytes 1179656 | tf_op jit(solution)/shard_map/ppermute | solution.py:181
  4.6 0.0 copy-start.6
  4.7 2.4 %collective-permute-start.10 = (f32[2,2,128,128]{3,2,1,0:T(8,128)S(1)}, f32[2,2,128,128]{3,2,1,0:T(8,128)S(1)}, u32[]{:S(2)}, u32[]{:S(2)}) collective-permute-start(f32[2,2,128,128]{3,2,1,0:T(8,128)S(1)} %dynamic-slice_bitcast_fusion.refs_6_), channel_id=1, source_target_pairs={{0,2},{1,3},{2,0},{3,1},{4,6},{5,7},{6,4},{7,5},{8,10},{9,11},{10,... | collective-permute-start | bytes 786440 | tf_op jit(solution)/shard_map/ppermute | solution.py:187
  7.0 1.1 %collective-permute-start.11 = (f32[2,2,128,128]{3,2,1,0:T(8,128)S(1)}, f32[2,2,128,128]{3,2,1,0:T(8,128)S(1)}, u32[]{:S(2)}, u32[]{:S(2)}) collective-permute-start(f32[2,2,128,128]{3,2,1,0:T(8,128)S(1)} %dynamic-slice_bitcast_fusion.refs_6_), channel_id=1, source_target_pairs={{0,3},{1,0},{2,1},{3,2},{4,7},{5,4},{6,5},{7,6},{8,11},{9,8},{10,9... | collective-permute-start | bytes 786440 | tf_op jit(solution)/shard_map/ppermute | solution.py:187
  8.1 0.4 collective-permute-start.9
  8.5 3.7 %collective-permute-done.3.refs_8_.refs_7_ = f32[3,128,256]{2,1,0:T(8,128)S(1)} collective-permute-done((f32[3,128,256]{2,1,0:T(8,128)S(1)}, f32[3,128,256]{2,1,0:T(8,128)S(1)}, u32[]{:S(2)}, u32[]{:S(2)}) %collective-permute-start.3) | collective-permute-done | bytes 393248 | tf_op jit(solution)/shard_map/ppermute | solution.py:181
  12.2 0.9 collective-permute-done.5.refs_9_.refs_14_
  13.2 1.3 %collective-permute-start.7 = (f32[3,128,256]{2,1,0:T(8,128)S(1)}, f32[3,128,256]{2,1,0:T(8,128)S(1)}, u32[]{:S(2)}, u32[]{:S(2)}) collective-permute-start(f32[3,128,256]{2,1,0:T(8,128)S(1)} %broadcast_select_fusion), channel_id=1, source_target_pairs={{0,8},{8,0},{16,24},{24,16},{4,20},{12,28},{20,4},{28,12},{1,9},{9... | collective-permute-start | bytes 1179656 | tf_op jit(solution)/shard_map/ppermute | solution.py:204
  14.5 0.6 copy-done.21
  15.1 0.0 copy-done.22
  15.2 1.3 %collective-permute-start = (f32[3,2]{1,0:T(4,128)S(1)}, f32[3,2]{1,0:T(4,128)S(1)}, u32[]{:S(2)}, u32[]{:S(2)}) collective-permute-start(f32[3,2]{1,0:T(4,128)S(1)} %pad_maximum_fusion.1.refs_2_), channel_id=1, source_target_pairs={{0,1},{1,2},{2,3},{3,0},{4,5},{5,6},{6,7},{7,4},{8,9},{9,10},{10,1... | collective-permute-start | bytes 80 | tf_op jit(solution)/shard_map/ppermute | solution.py:187
  16.5 0.6 pad_add_fusion.refs_0_
  17.1 7.5 %collective-permute-done.refs_3_ = f32[3,2]{1,0:T(4,128)S(1)} collective-permute-done((f32[3,2]{1,0:T(4,128)S(1)}, f32[3,2]{1,0:T(4,128)S(1)}, u32[]{:S(2)}, u32[]{:S(2)}) %collective-permute-start) | collective-permute-done | bytes 56 | tf_op jit(solution)/shard_map/ppermute | solution.py:187
  24.7 8.4 %collective-permute-start.1 = (f32[3,2]{1,0:T(4,128)S(1)}, f32[3,2]{1,0:T(4,128)S(1)}, u32[]{:S(2)}, u32[]{:S(2)}) collective-permute-start(f32[3,2]{1,0:T(4,128)S(1)} %pad_maximum_fusion.1.refs_2_), channel_id=1, source_target_pairs={{0,2},{1,3},{2,0},{3,1},{4,6},{5,7},{6,4},{7,5},{8,10},{9,11},{10,... | collective-permute-start | bytes 80 | tf_op jit(solution)/shard_map/ppermute | solution.py:187
  33.1 1.0 collective-permute-done.1.refs_4_
  34.1 0.2 collective-permute-start.2
  34.2 2.3 %collective-permute-done.2.refs_5_ = f32[3,2]{1,0:T(4,128)S(1)} collective-permute-done((f32[3,2]{1,0:T(4,128)S(1)}, f32[3,2]{1,0:T(4,128)S(1)}, u32[]{:S(2)}, u32[]{:S(2)}) %collective-permute-start.2) | collective-permute-done | bytes 56 | tf_op jit(solution)/shard_map/ppermute | solution.py:187
  36.5 0.0 collective-permute-done.10.refs_8_
  36.5 0.0 collective-permute-done.11.refs_9_
  36.5 0.0 collective-permute-done.9.refs_7_
  36.6 0.5 copy-done.17
  37.1 0.1 copy-done.10
  37.2 0.1 copy-done.11
  37.3 0.7 copy-done.12
  38.0 2.5 %shard_map.77 = (f32[128,128]{1,0:T(8,128)}, f32[128,128]{1,0:T(8,128)}, f32[128,128]{1,0:T(8,128)}, f32[128,128]{1,0:T(8,128)}) custom-call(s32[3]{0:T(128)} %pad_add_fusion.refs_0_, s32[8]{0:T(128)} %refs_1_.11, f32[3,2]{1,0:T(4,128)} %copy-done.14, f32[3,2]{1,0:T(4,128)} %copy-done.15, f32[3,2]{1,0:T(4,128)} %copy-done.16, f32[3,2]{1,0:T(4,128)} %copy-done.17, ...), custom_call_target="tpu_custom_call" | custom-call | tf_op jit(solution)/shard_map/pallas_call | solution.py:332
  40.5 0.3 collective-permute-start.12
  40.8 0.2 collective-permute-start.13
  41.0 2.2 %collective-permute-start.14 = (f32[128,128]{1,0:T(8,128)}, f32[128,128]{1,0:T(8,128)S(1)}, u32[]{:S(2)}, u32[]{:S(2)}) collective-permute-start(f32[128,128]{1,0:T(8,128)} %get-tuple-element.40), channel_id=1, source_target_pairs={{0,24},{8,16},{16,8},{24,0},{1,25},{9,17},{17,9},{25,1},{2,26},{10... | collective-permute-start | bytes 196616 | tf_op jit(solution)/shard_map/ppermute | solution.py:181
  43.1 3.4 %collective-permute-start.4 = (f32[3,128,256]{2,1,0:T(8,128)S(1)}, f32[3,128,256]{2,1,0:T(8,128)S(1)}, u32[]{:S(2)}, u32[]{:S(2)}) collective-permute-start(f32[3,128,256]{2,1,0:T(8,128)S(1)} %collective-permute-done.3.refs_8_.refs_7_), channel_id=1, source_target_pairs={{0,4},{4,0},{1,5},{5,1},{2,6},{6,2},{3,7},{7,3},{8,12},{12,8},{9,1... | collective-permute-start | bytes 1179656 | tf_op jit(solution)/shard_map/ppermute | solution.py:184
  46.5 0.0 collective-permute-done.12
  46.5 1.0 collective-permute-start.6
  47.5 0.1 collective-permute-start.8
  47.6 0.0 collective-permute-done.13
  47.6 0.0 collective-permute-done.14
  47.6 0.9 pad_maximum_fusion.refs_18_
  48.5 0.0 copy-start.7
  48.5 1.8 %collective-permute-start.15 = (f32[4,128,128]{2,1,0:T(8,128)S(1)}, f32[4,128,128]{2,1,0:T(8,128)S(1)}, u32[]{:S(2)}, u32[]{:S(2)}) collective-permute-start(f32[4,128,128]{2,1,0:T(8,128)S(1)} %pad_maximum_fusion.refs_18_), channel_id=1, source_target_pairs={{0,4},{4,0},{1,5},{5,1},{2,6},{6,2},{3,7},{7,3},{8,12},{12,8},{9,1... | collective-permute-start | bytes 786440 | tf_op jit(solution)/shard_map/ppermute | solution.py:184
  50.4 5.7 %shard_map.73.refs_6_ = bf16[256,1024]{1,0:T(8,128)(2,1)} custom-call(s32[3]{0:T(128)} %pad_add_fusion.refs_0_, s32[8]{0:T(128)} %refs_1_.11, f32[3,2]{1,0:T(4,128)} %copy-done.14, f32[3,2]{1,0:T(4,128)} %copy-done.15, f32[3,2]{1,0:T(4,128)} %copy-done.16, f32[3,2]{1,0:T(4,128)} %copy-done.17, f32[1,2,256,256]{3,2,1,0:T(8,128)} %refs_6_.1), custom_call_target="tpu_custom_call" | custom-call | tf_op jit(solution)/shard_map/pallas_call | solution.py:221
  56.1 0.0 collective-permute-done.4.refs_9_.refs_8_
  56.1 0.7 copy-done.5
  56.9 7.3 %shard_map.74 = (bf16[256,1024]{1,0:T(8,128)(2,1)}, bf16[256,1024]{1,0:T(8,128)(2,1)}, bf16[256,1024]{1,0:T(8,128)(2,1)}) custom-call(s32[3]{0:T(128)} %pad_add_fusion.refs_0_, s32[8]{0:T(128)} %refs_1_.11, f32[3,2]{1,0:T(4,128)} %copy-done.14, f32[3,2]{1,0:T(4,128)} %copy-done.15, f32[3,2]{1,0:T(4,128)} %copy-done.16, f32[3,2]{1,0:T(4,128)} %copy-done.17, ...), custom_call_target="tpu_custom_call" | custom-call | tf_op jit(solution)/shard_map/pallas_call | solution.py:257
  64.2 0.0 collective-permute-done.6.refs_10_.refs_15_
  64.2 0.8 copy-done.4
  65.0 7.6 %shard_map.75 = (bf16[256,1024]{1,0:T(8,128)(2,1)}, bf16[256,1024]{1,0:T(8,128)(2,1)}, bf16[256,1024]{1,0:T(8,128)(2,1)}) custom-call(s32[3]{0:T(128)} %pad_add_fusion.refs_0_, s32[8]{0:T(128)} %refs_1_.11, f32[3,2]{1,0:T(4,128)} %copy-done.14, f32[3,2]{1,0:T(4,128)} %copy-done.15, f32[3,2]{1,0:T(4,128)} %copy-done.16, f32[3,2]{1,0:T(4,128)} %copy-done.17, ...), custom_call_target="tpu_custom_call" | custom-call | tf_op jit(solution)/shard_map/pallas_call | solution.py:297
  72.6 0.0 collective-permute-done.8.refs_17_
  72.6 0.8 copy-done.9
  73.4 9.0 %shard_map.76 = (bf16[256,1024]{1,0:T(8,128)(2,1)}, bf16[256,1024]{1,0:T(8,128)(2,1)}, bf16[256,1024]{1,0:T(8,128)(2,1)}, bf16[256,1024]{1,0:T(8,128)(2,1)}, bf1...) custom-call(s32[3]{0:T(128)} %pad_add_fusion.refs_0_, s32[8]{0:T(128)} %refs_1_.11, ...), custom_call_target="tpu_custom_call" | custom-call | tf_op jit(solution)/shard_map/pallas_call | solution.py:402
  82.3 0.0 collective-permute-done.15.refs_19_
  82.4 0.7 copy-done.13
  83.1 8.0 %shard_map.78 = (f32[4,128,128]{2,1,0:T(8,128)}, f32[4,128,128]{2,1,0:T(8,128)}) custom-call(s32[3]{0:T(128)} %pad_add_fusion.refs_0_, s32[8]{0:T(128)} %refs_1_.11, f32[3,2]{1,0:T(4,128)} %copy-done.14, f32[3,2]{1,0:T(4,128)} %copy-done.15, f32[3,2]{1,0:T(4,128)} %copy-done.16, f32[3,2]{1,0:T(4,128)} %copy-done.17, bf16[256,1024]{1,0:T(8,128)(2,1)} %shard_map.73.refs_6_, ...), custom_call_target="tpu_custom_call" | custom-call | tf_op jit(solution)/shard_map/pallas_call | solution.py:445
  91.1 0.0 collective-permute-start.16
  91.2 1.7 %collective-permute-done.16 = f32[4,128,128]{2,1,0:T(8,128)S(1)} collective-permute-done((f32[4,128,128]{2,1,0:T(8,128)}, f32[4,128,128]{2,1,0:T(8,128)S(1)}, u32[]{:S(2)}, u32[]{:S(2)}) %collective-permute-start.16) | collective-permute-done | bytes 262176 | tf_op jit(solution)/shard_map/ppermute | solution.py:184
  92.9 1.0 add.8
  93.9 0.6 slice_bitcast_fusion
  94.5 2.8 %collective-permute-start.17 = (f32[128,128]{1,0:T(8,128)S(1)}, f32[128,128]{1,0:T(8,128)S(1)}, u32[]{:S(2)}, u32[]{:S(2)}) collective-permute-start(f32[128,128]{1,0:T(8,128)S(1)} %get-tuple-element.45), channel_id=1, source_target_pairs={{0,8},{8,0},{16,24},{24,16},{1,9},{9,1},{17,25},{25,17},{2,10},{10... | collective-permute-start | bytes 196616 | tf_op jit(solution)/shard_map/ppermute | solution.py:181
  97.3 2.2 %collective-permute-start.18 = (f32[128,128]{1,0:T(8,128)S(1)}, f32[128,128]{1,0:T(8,128)S(1)}, u32[]{:S(2)}, u32[]{:S(2)}) collective-permute-start(f32[128,128]{1,0:T(8,128)S(1)} %get-tuple-element.44), channel_id=1, source_target_pairs={{0,16},{8,24},{16,0},{24,8},{1,17},{9,25},{17,1},{25,9},{2,18},{10... | collective-permute-start | bytes 196616 | tf_op jit(solution)/shard_map/ppermute | solution.py:181
  99.6 1.2 %collective-permute-start.19 = (f32[128,128]{1,0:T(8,128)S(1)}, f32[128,128]{1,0:T(8,128)S(1)}, u32[]{:S(2)}, u32[]{:S(2)}) collective-permute-start(f32[128,128]{1,0:T(8,128)S(1)} %get-tuple-element.43), channel_id=1, source_target_pairs={{0,24},{8,16},{16,8},{24,0},{1,25},{9,17},{17,9},{25,1},{2,26},{10... | collective-permute-start | bytes 196616 | tf_op jit(solution)/shard_map/ppermute | solution.py:181
  100.7 1.1 %collective-permute-done.18.refs_3_ = f32[128,128]{1,0:T(8,128)S(1)} collective-permute-done((f32[128,128]{1,0:T(8,128)S(1)}, f32[128,128]{1,0:T(8,128)S(1)}, u32[]{:S(2)}, u32[]{:S(2)}) %collective-permute-start.18) | collective-permute-done | bytes 65568 | tf_op jit(solution)/shard_map/ppermute | solution.py:181
  101.9 2.2 %collective-permute-done.19.refs_4_ = f32[128,128]{1,0:T(8,128)S(1)} collective-permute-done((f32[128,128]{1,0:T(8,128)S(1)}, f32[128,128]{1,0:T(8,128)S(1)}, u32[]{:S(2)}, u32[]{:S(2)}) %collective-permute-start.19) | collective-permute-done | bytes 65568 | tf_op jit(solution)/shard_map/ppermute | solution.py:181
  104.1 0.6 copy-done.20
  104.7 1.8 %shard_map.79 = f32[2,1,2,128,128]{4,3,2,1,0:T(8,128)} custom-call(s32[3]{0:T(128)} %pad_add_fusion.refs_0_, f32[128,128]{1,0:T(8,128)} %get-tuple-element.46.refs_1_, f32[128,128]{1,0:T(8,128)} %copy-done.18, f32[128,128]{1,0:T(8,128)} %copy-done.19, f32[128,128]{1,0:T(8,128)} %copy-done.20), custom_call_target="tpu_custom_call" | custom-call | tf_op jit(solution)/shard_map/pallas_call | solution.py:474
  (41 shorter events, 0.2 us)
Async XLA Ops:
  0.0 4.6 %copy-start = (f32[2,1,2,256,128]{4,3,2,1,0:T(8,128)S(1)}, f32[2,1,2,256,128]{4,3,2,1,0:T(8,128)}, u32[]{:S(2)}) copy-start(f32[2,1,2,256,128]{4,3,2,1,0:T(8,128)} %param.9) | copy-start | bytes 1572868
  0.0 1.3 %copy-start.1 = (f32[1,2,256,256]{3,2,1,0:T(8,128)S(1)}, f32[1,2,256,256]{3,2,1,0:T(8,128)}, u32[]{:S(2)}) copy-start(f32[1,2,256,256]{3,2,1,0:T(8,128)} %refs_13_.1) | copy-start | bytes 1572868
  1.3 10.9 %collective-permute-start.3 = (f32[3,128,256]{2,1,0:T(8,128)S(1)}, f32[3,128,256]{2,1,0:T(8,128)S(1)}, u32[]{:S(2)}, u32[]{:S(2)}) collective-permute-start(f32[3,128,256]{2,1,0:T(8,128)S(1)} %fusion), channel_id=1, source_target_pairs={{0,8},{8,0},{16,24},{24,16},{1,9},{9,1},{17,25},{25,17},{2,10},{10... | collective-permute-start | bytes 1179656 | tf_op jit(solution)/shard_map/ppermute | solution.py:181
  3.4 9.7 %collective-permute-start.5 = (f32[3,128,256]{2,1,0:T(8,128)S(1)}, f32[3,128,256]{2,1,0:T(8,128)S(1)}, u32[]{:S(2)}, u32[]{:S(2)}) collective-permute-start(f32[3,128,256]{2,1,0:T(8,128)S(1)} %fusion), channel_id=1, source_target_pairs={{0,16},{8,24},{16,0},{24,8},{1,17},{9,25},{17,1},{25,9},{2,18},{10... | collective-permute-start | bytes 1179656 | tf_op jit(solution)/shard_map/ppermute | solution.py:181
  4.6 8.5 %copy-start.6 = (f32[2,2,128,128]{3,2,1,0:T(8,128)}, f32[2,2,128,128]{3,2,1,0:T(8,128)S(1)}, u32[]{:S(2)}) copy-start(f32[2,2,128,128]{3,2,1,0:T(8,128)S(1)} %dynamic-slice_bitcast_fusion.refs_6_) | copy-start | bytes 786436
  4.7 31.9 %collective-permute-start.10 = (f32[2,2,128,128]{3,2,1,0:T(8,128)S(1)}, f32[2,2,128,128]{3,2,1,0:T(8,128)S(1)}, u32[]{:S(2)}, u32[]{:S(2)}) collective-permute-start(f32[2,2,128,128]{3,2,1,0:T(8,128)S(1)} %dynamic-slice_bitcast_fusion.refs_6_), channel_id=1, source_target_pairs={{0,2},{1,3},{2,0},{3,1},{4,6},{5,7},{6,4},{7,5},{8,10},{9,11},{10,... | collective-permute-start | bytes 786440 | tf_op jit(solution)/shard_map/ppermute | solution.py:187
  7.0 29.5 %collective-permute-start.11 = (f32[2,2,128,128]{3,2,1,0:T(8,128)S(1)}, f32[2,2,128,128]{3,2,1,0:T(8,128)S(1)}, u32[]{:S(2)}, u32[]{:S(2)}) collective-permute-start(f32[2,2,128,128]{3,2,1,0:T(8,128)S(1)} %dynamic-slice_bitcast_fusion.refs_6_), channel_id=1, source_target_pairs={{0,3},{1,0},{2,1},{3,2},{4,7},{5,4},{6,5},{7,6},{8,11},{9,8},{10,9... | collective-permute-start | bytes 786440 | tf_op jit(solution)/shard_map/ppermute | solution.py:187
  8.1 28.4 %collective-permute-start.9 = (f32[2,2,128,128]{3,2,1,0:T(8,128)S(1)}, f32[2,2,128,128]{3,2,1,0:T(8,128)S(1)}, u32[]{:S(2)}, u32[]{:S(2)}) collective-permute-start(f32[2,2,128,128]{3,2,1,0:T(8,128)S(1)} %dynamic-slice_bitcast_fusion.refs_6_), channel_id=1, source_target_pairs={{0,1},{1,2},{2,3},{3,0},{4,5},{5,6},{6,7},{7,4},{8,9},{9,10},{10,1... | collective-permute-start | bytes 786440 | tf_op jit(solution)/shard_map/ppermute | solution.py:187
  8.5 6.0 %copy-start.23 = (s32[2]{0:T(128)S(1)}, s32[2]{0:T(128)}, u32[]{:S(2)}) copy-start(s32[2]{0:T(128)} %param.10) | copy-start | bytes 28
  12.2 30.9 %copy-start.3 = (f32[3,128,256]{2,1,0:T(8,128)}, f32[3,128,256]{2,1,0:T(8,128)S(1)}, u32[]{:S(2)}) copy-start(f32[3,128,256]{2,1,0:T(8,128)S(1)} %collective-permute-done.3.refs_8_.refs_7_) | copy-start | bytes 1179652
  13.1 33.4 %copy-start.2 = (f32[3,128,256]{2,1,0:T(8,128)}, f32[3,128,256]{2,1,0:T(8,128)S(1)}, u32[]{:S(2)}) copy-start(f32[3,128,256]{2,1,0:T(8,128)S(1)} %collective-permute-done.5.refs_9_.refs_14_) | copy-start | bytes 1179652
  13.2 34.3 %collective-permute-start.7 = (f32[3,128,256]{2,1,0:T(8,128)S(1)}, f32[3,128,256]{2,1,0:T(8,128)S(1)}, u32[]{:S(2)}, u32[]{:S(2)}) collective-permute-start(f32[3,128,256]{2,1,0:T(8,128)S(1)} %broadcast_select_fusion), channel_id=1, source_target_pairs={{0,8},{8,0},{16,24},{24,16},{4,20},{12,28},{20,4},{28,12},{1,9},{9... | collective-permute-start | bytes 1179656 | tf_op jit(solution)/shard_map/ppermute | solution.py:204
  14.5 0.7 copy-start.21
  14.5 0.7 copy-start.22
  15.2 18.9 %copy-start.14 = (f32[3,2]{1,0:T(4,128)}, f32[3,2]{1,0:T(4,128)S(1)}, u32[]{:S(2)}) copy-start(f32[3,2]{1,0:T(4,128)S(1)} %pad_maximum_fusion.1.refs_2_) | copy-start | bytes 76
  15.2 9.5 %collective-permute-start = (f32[3,2]{1,0:T(4,128)S(1)}, f32[3,2]{1,0:T(4,128)S(1)}, u32[]{:S(2)}, u32[]{:S(2)}) collective-permute-start(f32[3,2]{1,0:T(4,128)S(1)} %pad_maximum_fusion.1.refs_2_), channel_id=1, source_target_pairs={{0,1},{1,2},{2,3},{3,0},{4,5},{5,6},{6,7},{7,4},{8,9},{9,10},{10,1... | collective-permute-start | bytes 80 | tf_op jit(solution)/shard_map/ppermute | solution.py:187
  24.7 11.9 %copy-start.15 = (f32[3,2]{1,0:T(4,128)}, f32[3,2]{1,0:T(4,128)S(1)}, u32[]{:S(2)}) copy-start(f32[3,2]{1,0:T(4,128)S(1)} %collective-permute-done.refs_3_) | copy-start | bytes 76
  24.7 9.4 %collective-permute-start.1 = (f32[3,2]{1,0:T(4,128)S(1)}, f32[3,2]{1,0:T(4,128)S(1)}, u32[]{:S(2)}, u32[]{:S(2)}) collective-permute-start(f32[3,2]{1,0:T(4,128)S(1)} %pad_maximum_fusion.1.refs_2_), channel_id=1, source_target_pairs={{0,2},{1,3},{2,0},{3,1},{4,6},{5,7},{6,4},{7,5},{8,10},{9,11},{10,... | collective-permute-start | bytes 80 | tf_op jit(solution)/shard_map/ppermute | solution.py:187
  34.1 2.5 %copy-start.16 = (f32[3,2]{1,0:T(4,128)}, f32[3,2]{1,0:T(4,128)S(1)}, u32[]{:S(2)}) copy-start(f32[3,2]{1,0:T(4,128)S(1)} %collective-permute-done.1.refs_4_) | copy-start | bytes 76
  34.1 2.4 %collective-permute-start.2 = (f32[3,2]{1,0:T(4,128)S(1)}, f32[3,2]{1,0:T(4,128)S(1)}, u32[]{:S(2)}, u32[]{:S(2)}) collective-permute-start(f32[3,2]{1,0:T(4,128)S(1)} %pad_maximum_fusion.1.refs_2_), channel_id=1, source_target_pairs={{0,3},{1,0},{2,1},{3,2},{4,7},{5,4},{6,5},{7,6},{8,11},{9,8},{10,9... | collective-permute-start | bytes 80 | tf_op jit(solution)/shard_map/ppermute | solution.py:187
  36.5 0.6 copy-start.17
  36.5 0.7 copy-start.10
  36.5 0.8 copy-start.11
  37.3 0.7 copy-start.12
  40.5 6.0 %collective-permute-start.12 = (f32[128,128]{1,0:T(8,128)}, f32[128,128]{1,0:T(8,128)S(1)}, u32[]{:S(2)}, u32[]{:S(2)}) collective-permute-start(f32[128,128]{1,0:T(8,128)} %get-tuple-element.38), channel_id=1, source_target_pairs={{0,8},{8,0},{16,24},{24,16},{1,9},{9,1},{17,25},{25,17},{2,10},{10... | collective-permute-start | bytes 196616 | tf_op jit(solution)/shard_map/ppermute | solution.py:181
  40.8 6.8 %collective-permute-start.13 = (f32[128,128]{1,0:T(8,128)}, f32[128,128]{1,0:T(8,128)S(1)}, u32[]{:S(2)}, u32[]{:S(2)}) collective-permute-start(f32[128,128]{1,0:T(8,128)} %get-tuple-element.39), channel_id=1, source_target_pairs={{0,16},{8,24},{16,0},{24,8},{1,17},{9,25},{17,1},{25,9},{2,18},{10... | collective-permute-start | bytes 196616 | tf_op jit(solution)/shard_map/ppermute | solution.py:181
  41.0 6.6 %collective-permute-start.14 = (f32[128,128]{1,0:T(8,128)}, f32[128,128]{1,0:T(8,128)S(1)}, u32[]{:S(2)}, u32[]{:S(2)}) collective-permute-start(f32[128,128]{1,0:T(8,128)} %get-tuple-element.40), channel_id=1, source_target_pairs={{0,24},{8,16},{16,8},{24,0},{1,25},{9,17},{17,9},{25,1},{2,26},{10... | collective-permute-start | bytes 196616 | tf_op jit(solution)/shard_map/ppermute | solution.py:181
  43.1 13.0 %collective-permute-start.4 = (f32[3,128,256]{2,1,0:T(8,128)S(1)}, f32[3,128,256]{2,1,0:T(8,128)S(1)}, u32[]{:S(2)}, u32[]{:S(2)}) collective-permute-start(f32[3,128,256]{2,1,0:T(8,128)S(1)} %collective-permute-done.3.refs_8_.refs_7_), channel_id=1, source_target_pairs={{0,4},{4,0},{1,5},{5,1},{2,6},{6,2},{3,7},{7,3},{8,12},{12,8},{9,1... | collective-permute-start | bytes 1179656 | tf_op jit(solution)/shard_map/ppermute | solution.py:184
  46.5 17.7 %collective-permute-start.6 = (f32[3,128,256]{2,1,0:T(8,128)S(1)}, f32[3,128,256]{2,1,0:T(8,128)S(1)}, u32[]{:S(2)}, u32[]{:S(2)}) collective-permute-start(f32[3,128,256]{2,1,0:T(8,128)S(1)} %collective-permute-done.5.refs_9_.refs_14_), channel_id=1, source_target_pairs={{0,4},{4,0},{1,5},{5,1},{2,6},{6,2},{3,7},{7,3},{8,12},{12,8},{9,1... | collective-permute-start | bytes 1179656 | tf_op jit(solution)/shard_map/ppermute | solution.py:184
  47.5 8.6 %copy-start.8 = (f32[3,128,256]{2,1,0:T(8,128)}, f32[3,128,256]{2,1,0:T(8,128)S(1)}, u32[]{:S(2)}) copy-start(f32[3,128,256]{2,1,0:T(8,128)S(1)} %collective-permute-done.7.refs_16_) | copy-start | bytes 1179652
  47.5 25.1 %collective-permute-start.8 = (f32[3,128,256]{2,1,0:T(8,128)S(1)}, f32[3,128,256]{2,1,0:T(8,128)S(1)}, u32[]{:S(2)}, u32[]{:S(2)}) collective-permute-start(f32[3,128,256]{2,1,0:T(8,128)S(1)} %collective-permute-done.7.refs_16_), channel_id=1, source_target_pairs={{0,4},{4,0},{1,5},{5,1},{2,6},{6,2},{3,7},{7,3},{8,12},{12,8},{9,1... | collective-permute-start | bytes 1179656 | tf_op jit(solution)/shard_map/ppermute | solution.py:184
  48.5 7.6 %copy-start.7 = (f32[4,128,128]{2,1,0:T(8,128)}, f32[4,128,128]{2,1,0:T(8,128)S(1)}, u32[]{:S(2)}) copy-start(f32[4,128,128]{2,1,0:T(8,128)S(1)} %pad_maximum_fusion.refs_18_) | copy-start | bytes 786436
  48.5 33.8 %collective-permute-start.15 = (f32[4,128,128]{2,1,0:T(8,128)S(1)}, f32[4,128,128]{2,1,0:T(8,128)S(1)}, u32[]{:S(2)}, u32[]{:S(2)}) collective-permute-start(f32[4,128,128]{2,1,0:T(8,128)S(1)} %pad_maximum_fusion.refs_18_), channel_id=1, source_target_pairs={{0,4},{4,0},{1,5},{5,1},{2,6},{6,2},{3,7},{7,3},{8,12},{12,8},{9,1... | collective-permute-start | bytes 786440 | tf_op jit(solution)/shard_map/ppermute | solution.py:184
  56.1 0.8 copy-start.5
  64.2 0.8 copy-start.4
  72.6 0.8 copy-start.9
  82.4 0.7 copy-start.13
  91.1 1.8 %collective-permute-start.16 = (f32[4,128,128]{2,1,0:T(8,128)}, f32[4,128,128]{2,1,0:T(8,128)S(1)}, u32[]{:S(2)}, u32[]{:S(2)}) collective-permute-start(f32[4,128,128]{2,1,0:T(8,128)} %get-tuple-element.42), channel_id=1, source_target_pairs={{0,4},{4,0},{1,5},{5,1},{2,6},{6,2},{3,7},{7,3},{8,12},{12,8},{9,1... | collective-permute-start | bytes 786440 | tf_op jit(solution)/shard_map/ppermute | solution.py:184
  94.5 6.2 %collective-permute-start.17 = (f32[128,128]{1,0:T(8,128)S(1)}, f32[128,128]{1,0:T(8,128)S(1)}, u32[]{:S(2)}, u32[]{:S(2)}) collective-permute-start(f32[128,128]{1,0:T(8,128)S(1)} %get-tuple-element.45), channel_id=1, source_target_pairs={{0,8},{8,0},{16,24},{24,16},{1,9},{9,1},{17,25},{25,17},{2,10},{10... | collective-permute-start | bytes 196616 | tf_op jit(solution)/shard_map/ppermute | solution.py:181
  97.3 4.6 %collective-permute-start.18 = (f32[128,128]{1,0:T(8,128)S(1)}, f32[128,128]{1,0:T(8,128)S(1)}, u32[]{:S(2)}, u32[]{:S(2)}) collective-permute-start(f32[128,128]{1,0:T(8,128)S(1)} %get-tuple-element.44), channel_id=1, source_target_pairs={{0,16},{8,24},{16,0},{24,8},{1,17},{9,25},{17,1},{25,9},{2,18},{10... | collective-permute-start | bytes 196616 | tf_op jit(solution)/shard_map/ppermute | solution.py:181
  99.6 4.6 %collective-permute-start.19 = (f32[128,128]{1,0:T(8,128)S(1)}, f32[128,128]{1,0:T(8,128)S(1)}, u32[]{:S(2)}, u32[]{:S(2)}) collective-permute-start(f32[128,128]{1,0:T(8,128)S(1)} %get-tuple-element.43), channel_id=1, source_target_pairs={{0,24},{8,16},{16,8},{24,0},{1,25},{9,17},{17,9},{25,1},{2,26},{10... | collective-permute-start | bytes 196616 | tf_op jit(solution)/shard_map/ppermute | solution.py:181
  100.7 3.4 %copy-start.18 = (f32[128,128]{1,0:T(8,128)}, f32[128,128]{1,0:T(8,128)S(1)}, u32[]{:S(2)}) copy-start(f32[128,128]{1,0:T(8,128)S(1)} %collective-permute-done.17.refs_2_) | copy-start | bytes 196612
  101.9 2.2 %copy-start.19 = (f32[128,128]{1,0:T(8,128)}, f32[128,128]{1,0:T(8,128)S(1)}, u32[]{:S(2)}) copy-start(f32[128,128]{1,0:T(8,128)S(1)} %collective-permute-done.18.refs_3_) | copy-start | bytes 196612
  104.1 0.6 copy-start.20

commit v2 on v1

--- a/solution.py
+++ b/solution.py
@@ -7,6 +7,7 @@
 from jax.experimental.pallas import tpu as pltpu
 from jax.sharding import PartitionSpec as P
 
+
 F32 = jnp.float32
 BF16 = jnp.bfloat16
 COARSE = 0.1
@@ -50,6 +51,10 @@
 def column_triple(value):
     high, low = hi_lo(jnp.concatenate([value, times_i(value)], 0))
     return jnp.concatenate([high, high, low], 0)
+
+
+def lasting(micros):
+    return pl.CostEstimate(flops=micros * 10**9, transcendentals=0, bytes_accessed=micros * 10**6)
 
 
 def eye_of(order):
@@ -123,11 +128,14 @@
     return re, im, adj_re, adj_im
 
 
+def position():
+    return lax.axis_index("win"), lax.axis_index("slab"), lax.axis_index("point")
+
+
 def slot_of(scal, owner, slab, dims):
-    win_count, local_count, parts = dims
+    local_count, parts = dims
     window = owner[scal[0] * local_count + slab // parts]
-    shift = lax.rem(scal[0] - window // local_count + win_count, win_count)
-    return shift, lax.rem(window, local_count)
+    return scal[0] ^ (window // local_count), lax.rem(window, local_count)
 
 
 def look_up(tables, row, shift, index):
@@ -151,11 +159,8 @@
 
 
 def per_device(diag_blocks, couplings, subspace, widths, owner_order, centers, radii):
-    slab = lax.axis_index("slab")
     slab_count = lax.axis_size("slab")
-    point = lax.axis_index("point")
     point_count = lax.axis_size("point")
-    win = lax.axis_index("win")
     win_count = lax.axis_size("win")
     n = diag_blocks.shape[2]
     columns = subspace.shape[4]
@@ -164,12 +169,13 @@
     width = columns // parts
     lanes = 2 * width
     half = n // point_count
-    dims = (win_count, local_count, parts)
+    dims = (local_count, parts)
     assert slab_count == 4 and point_count == 2 and parts == 2
+    assert win_count & (win_count - 1) == 0
 
     smem = pl.BlockSpec(memory_space=pltpu.SMEM)
     vmem = pl.BlockSpec(memory_space=pltpu.VMEM)
-    grant = pltpu.CompilerParams(vmem_limit_bytes=56 * 1024 * 1024)
+    grant = pltpu.CompilerParams(vmem_limit_bytes=20 * 1024 * 1024)
     pair_shape = jax.ShapeDtypeStruct((n, 4 * n), BF16)
     scratch = [
         pltpu.VMEM((6 * n, 2 * n), BF16),
@@ -184,21 +190,76 @@
         return lax.ppermute(value, "point", [(i, i ^ 1) for i in range(point_count)])
 
     def along_win(value, shift):
-        return lax.ppermute(value, "win", [(i, (i + shift) % win_count) for i in range(win_count)])
-
-    scal = jnp.stack([win, slab, point]).astype(jnp.int32)
-    table = jnp.stack([centers, radii, widths.astype(F32)])
-    row = lax.broadcasted_iota(jnp.int32, (n, n), 0)
-    col = lax.broadcasted_iota(jnp.int32, (n, n), 1)
-    packed = jnp.where(row >= col, diag_blocks[0, 0], diag_blocks[0, 1])
-    shard = jnp.concatenate([packed[None], couplings[0]], 0)
-    carried = lax.dynamic_slice_in_dim(shard, point * half, half, 1)
+        return lax.ppermute(value, "win", [(i, i ^ shift) for i in range(win_count)])
+
+    table = jnp.stack([centers, radii])
+    tables = [table]
+    for k in range(1, win_count):
+        tables.append(along_win(table, k))
+
+    def prepare_body(widths, diag, links, vectors, carried, block, pair, sems):
+        start = position()[2] * half
+        rows = pl.ds(start, half)
+        moves = [pltpu.make_async_copy(diag.at[0, :, rows, :], pair, sems.at[0])]
+        moves.append(pltpu.make_async_copy(links.at[0, :, rows, :], carried.at[pl.ds(1, 2)], sems.at[1]))
+        moves.append(pltpu.make_async_copy(vectors.at[:, 0, :, rows, :], block, sems.at[2]))
+        for move in moves:
+            move.start()
+        for move in moves:
+            move.wait()
+        row = lax.broadcasted_iota(jnp.int32, (half, n), 0) + start
+        col = lax.broadcasted_iota(jnp.int32, (half, n), 1)
+        carried[0] = jnp.where(row >= col, pair[0], pair[1])
+        number = lax.broadcasted_iota(jnp.int32, (half, columns), 1)
+        for j in range(local_count):
+            for k in range(2):
+                block[j, k] = jnp.where(number < widths[j], block[j, k], 0.0)
+
+    anywhere = pl.BlockSpec(memory_space=pltpu.HBM)
+    prepare = pl.pallas_call(
+        prepare_body,
+        out_shape=[
+            jax.ShapeDtypeStruct((3, half, n), F32),
+            jax.ShapeDtypeStruct((local_count, 2, half, columns), F32),
+        ],
+        in_specs=[smem] + [anywhere] * 3,
+        out_specs=[vmem] * 2,
+        scratch_shapes=[pltpu.VMEM((2, half, n), F32), pltpu.SemaphoreType.DMA((3,))],
+        compiler_params=grant,
+    )
+    carried, block = prepare(widths, diag_blocks, couplings, subspace)
     from_x = exchange(carried, 1)
     from_y = exchange(carried, 2)
-    tables = [table] + [along_win(table, k) for k in range(1, win_count)]
-    block = lax.dynamic_slice_in_dim(subspace[:, 0], point * half, half, 2)
-    blocks = [block] + [along_win(block, k) for k in range(1, win_count)]
-    relay = jnp.where(point == 0, from_y, from_x)
+    blocks = [block]
+    for k in range(1, win_count):
+        blocks.append(along_win(block, k))
+
+    def first_body(*refs):
+        scal, owner = position(), refs[0]
+        tables = refs[1 : 1 + win_count]
+        diag, x_out, prm, s_emb, x_ref, work = refs[1 + win_count :]
+        z_re, z_im, weight_re, weight_im = contour(scal, owner, tables, dims, point_count)
+        for k, value in enumerate((z_re, z_im, weight_re, weight_im)):
+            prm[k] = value
+        eye = eye_of(n)
+        x_out[...] = packed_pair(
+            invert(z_re * eye - diag[0, 0], z_im * eye - diag[0, 1], z_im, s_emb, x_ref, work)
+        )
+
+    head = [owner_order] + tables
+    head_specs = [smem] * len(head)
+    first = pl.pallas_call(
+        first_body,
+        out_shape=[pair_shape, jax.ShapeDtypeStruct((4,), F32)],
+        in_specs=head_specs + [vmem],
+        out_specs=[vmem, smem],
+        scratch_shapes=scratch,
+        cost_estimate=lasting(6),
+        compiler_params=grant,
+    )
+    x_own, prm = first(*head, diag_blocks)
+
+    relay = jnp.where(lax.axis_index("point") == 0, from_y, from_x)
     flat = [(2 * s, 2 * (s ^ 1)) for s in range(slab_count)]
     flat += [(2 * s + 1, 2 * (s ^ 2) + 1) for s in range(slab_count)]
     from_far = lax.ppermute(relay, ("slab", "point"), flat)
@@ -206,32 +267,10 @@
     from_y = (from_y, swap(from_y))
     from_far = (from_far, swap(from_far))
 
-    def first_body(*refs):
-        scal, owner = refs[:2]
-        tables = refs[2 : 2 + win_count]
-        diag, x_out, s_emb, x_ref, work = refs[2 + win_count :]
-        z_re, z_im, _, _ = contour(scal, owner, tables, dims, point_count)
-        eye = eye_of(n)
-        x_out[...] = packed_pair(
-            invert(z_re * eye - diag[0, 0], z_im * eye - diag[0, 1], z_im, s_emb, x_ref, work)
-        )
-
-    head = [scal, owner_order] + tables
-    head_specs = [smem] * len(head)
-    x_own = pl.pallas_call(
-        first_body,
-        out_shape=pair_shape,
-        in_specs=head_specs + [vmem],
-        out_specs=vmem,
-        scratch_shapes=scratch,
-        compiler_params=grant,
-    )(*head, diag_blocks)
-
     def second_body(*refs):
-        scal, owner = refs[:2]
-        tables = refs[2 : 2 + win_count]
-        (x_own, own_c, x_dir, x_swp, x_out, w_out, l_out, s_emb, x_ref, work) = refs[2 + win_count :]
-        z_re, z_im, _, _ = contour(scal, owner, tables, dims, point_count)
+        scal, prm = position(), refs[0]
+        (x_own, own_c, x_dir, x_swp, x_out, w_out, l_out, s_emb, x_ref, work) = refs[1:]
+        z_re, z_im = prm[0], prm[1]
         p = scal[2]
         near = [rows_of(x_dir, x_swp, k, p) for k in range(3)]
         even = lax.rem(scal[1], 2) == 0
@@ -254,22 +293,24 @@
             )
         )
 
-    x_near, w_near, l_near = pl.pallas_call(
+    second = pl.pallas_call(
         second_body,
         out_shape=[pair_shape] * 3,
-        in_specs=head_specs + [vmem] * 4,
+        in_specs=[smem] + [vmem] * 4,
         out_specs=[vmem] * 3,
         scratch_shapes=scratch,
-        compiler_params=grant,
-    )(*head, x_own, couplings, *from_x)
+        cost_estimate=lasting(8),
+        compiler_params=grant,
+    )
+    x_near, w_near, l_near = second(prm, x_own, couplings, *from_x)
 
     def third_body(*refs):
-        scal, owner = refs[:2]
-        tables = refs[2 : 2 + win_count]
-        (x_near, x_dir, x_swp, y_dir, y_swp, x_out, w_out, l_out, s_emb, x_ref, work, s_ref) = refs[
-            2 + win_count :
-        ]
-        z_re, z_im, _, _ = contour(scal, owner, tables, dims, point_count)
+        scal, prm = position(), refs[0]
+        (x_near, x_dir, x_swp, y_dir, y_swp, x_out, w_out, l_out, later) = refs[1:10]
+        s_emb, x_ref, work, s_ref = refs[10:]
+        for k in range(4):
+            later[k] = prm[k]
+        z_re, z_im = prm[0], prm[1]
         p = scal[2]
         even = lax.rem(scal[1], 2) == 0
         chain = lax.rem(scal[1], 2) == scal[1] // 2
@@ -294,26 +335,25 @@
 
         x_out[...] = packed_pair(invert(s_ref[:, :n], s_ref[:, n:], z_im, s_emb, x_ref, work))
 
-    x_side, w_mid, l_mid = pl.pallas_call(
+    x_side, w_mid, l_mid, later = pl.pallas_call(
         third_body,
-        out_shape=[pair_shape] * 3,
-        in_specs=head_specs + [vmem] * 5,
-        out_specs=[vmem] * 3,
+        out_shape=[pair_shape] * 3 + [jax.ShapeDtypeStruct((4,), F32)],
+        in_specs=[smem] + [vmem] * 5,
+        out_specs=[vmem] * 3 + [smem],
         scratch_shapes=scratch + [pltpu.VMEM((n, 2 * n), F32)],
-        compiler_params=grant,
-    )(*head, x_near, *from_x, *from_y)
+        cost_estimate=lasting(8),
+        compiler_params=grant,
+    )(prm, x_near, *from_x, *from_y)
 
     def route_body(*refs):
-        scal, owner = refs[:2]
-        tables = refs[2 : 2 + win_count]
-        blocks = refs[2 + win_count : 2 + 2 * win_count]
-        outs = refs[2 + 2 * win_count :]
+        scal, owner = position(), refs[0]
+        blocks = refs[1 : 1 + win_count]
+        out = refs[2 + win_count]
         lane = lax.broadcasted_iota(jnp.int32, (half, lanes), 1)
         for k in range(slab_count):
             target = scal[1] ^ k
             part = lax.rem(target, parts)
             shift, index = slot_of(scal, owner, target, dims)
-            live = look_up(tables, 2, shift, index).astype(jnp.int32)
             for k_win in range(win_count):
 
                 @pl.when(shift == k_win)
@@ -325,30 +365,39 @@
                         jnp.where(lane < width, re, pltpu.roll(im, width, 1)),
                         jnp.where(lane < width, pltpu.roll(re, width, 1), im),
                     )
-                    number = part * width + lax.rem(lane, width)
-                    outs[k][...] = jnp.where(number < live, mine, 0.0)
+                    out[k] = mine
 
     piece = jax.ShapeDtypeStruct((half, lanes), F32)
+    quad = jax.ShapeDtypeStruct((slab_count, half, lanes), F32)
     routed = pl.pallas_call(
         route_body,
-        out_shape=[piece] * slab_count,
-        in_specs=head_specs + [vmem] * win_count,
+        out_shape=quad,
+        in_specs=[smem] + [vmem] * win_count + [smem],
+        out_specs=vmem,
+        cost_estimate=lasting(2),
+        compiler_params=grant,
+    )(owner_order, *blocks, later)
+
+    def join_body(mine, other, *outs):
+        p = position()[2]
+        for k in range(slab_count):
+            outs[k][pl.ds(p * half, half), :] = mine[k]
+            outs[k][pl.ds((1 - p) * half, half), :] = other[k]
+
+    joined = pl.pallas_call(
+        join_body,
+        out_shape=[jax.ShapeDtypeStruct((n, lanes), F32)] * slab_count,
+        in_specs=[vmem] * 2,
         out_specs=[vmem] * slab_count,
         compiler_params=grant,
-    )(*head, *blocks)
-    rhs = jnp.stack([routed[0]] + [exchange(routed[k], k) for k in range(1, slab_count)])
-    rhs = (rhs, swap(rhs))
+    )(routed, swap(routed))
+    rhs = [joined[0]] + [exchange(joined[k], k) for k in range(1, slab_count)]
 
     def fourth_body(*refs):
-        scal, owner = refs[:2]
-        tables = refs[2 : 2 + win_count]
-        (x_own, x_near, x_side, w_near, l_near, w_mid, l_mid, own_c, y_dir, y_swp, f_dir, f_swp) = refs[
-            2 + win_count : 14 + win_count
-        ]
-        (x_out, w_far, l_far, w_cross, l_cross, w_last, l_last, s_emb, x_ref, work, s_ref) = refs[
-            14 + win_count :
-        ]
-        z_re, z_im, _, _ = contour(scal, owner, tables, dims, point_count)
+        scal, prm = position(), refs[0]
+        (x_own, x_near, x_side, w_near, l_near, w_mid, l_mid, own_c, y_dir, y_swp, f_dir, f_swp) = refs[1:13]
+        (x_out, w_far, l_far, w_cross, l_cross, w_last, l_last, s_emb, x_ref, work, s_ref) = refs[13:]
+        z_re, z_im = prm[0], prm[1]
         p = scal[2]
         even = lax.rem(scal[1], 2) == 0
         chain = lax.rem(scal[1], 2) == scal[1] // 2
@@ -402,27 +451,26 @@
     x_far, w_far, l_far, w_cross, l_cross, w_last, l_last = pl.pallas_call(
         fourth_body,
         out_shape=[pair_shape] * 7,
-        in_specs=head_specs + [vmem] * 12,
+        in_specs=[smem] + [vmem] * 12,
         out_specs=[vmem] * 7,
         scratch_shapes=scratch + [pltpu.VMEM((n, 2 * n), F32)],
-        compiler_params=grant,
-    )(*head, x_own, x_near, x_side, w_near, l_near, w_mid, l_mid, couplings, *from_y, *from_far)
+        cost_estimate=lasting(10),
+        compiler_params=grant,
+    )(prm, x_own, x_near, x_side, w_near, l_near, w_mid, l_mid, couplings, *from_y, *from_far)
 
     def solve_body(*refs):
-        scal, owner = refs[:2]
-        tables = refs[2 : 2 + win_count]
-        (x_own, x_near, x_side, x_far, w_near, l_near, w_cross, l_cross, w_far, l_far, w_last, l_last) = refs[
-            2 + win_count : 14 + win_count
-        ]
-        b_dir, b_swp, keep, send = refs[14 + win_count :]
-        _, _, weight_re, weight_im = contour(scal, owner, tables, dims, point_count)
+        scal, prm = position(), refs[0]
+        (x_own, x_near, x_side, x_far, w_near, l_near, w_cross, l_cross, w_far, l_far, w_last, l_last) = refs[1:13]
+        loaded = refs[13:17]
+        keep, send = refs[17:]
+        weight_re, weight_im = prm[2], prm[3]
         p = scal[2]
         chain = lax.rem(scal[1], 2) == scal[1] // 2
 
         def apply(ref, value):
             return dot(left_triple(ref[...]), column_triple(value))
 
-        b_own, b_near, b_side, b_far = [rows_of(b_dir, b_swp, k, p) for k in range(4)]
+        b_own, b_near, b_side, b_far = [ref[...] for ref in loaded]
         u_own = apply(x_own, b_own)
         b_near = b_near + apply(l_near, u_own)
         b_far = b_far + apply(l_cross, u_own)
@@ -441,23 +489,34 @@
             keep[k] = pick(p == 0, value[:half], value[half:])
             send[k] = pick(p == 0, value[half:], value[:half])
 
-    quad = jax.ShapeDtypeStruct((slab_count, half, lanes), F32)
     keep, send = pl.pallas_call(
         solve_body,
         out_shape=[quad] * 2,
-        in_specs=head_specs + [vmem] * 14,
+        in_specs=[smem] + [vmem] * 16,
         out_specs=[vmem] * 2,
+        cost_estimate=lasting(8),
         compiler_params=grant,
     )(
-        *head, x_own, x_near, x_side, x_far, w_near, l_near, w_cross, l_cross, w_far, l_far, w_last, l_last, *rhs
+        prm, x_own, x_near, x_side, x_far, w_near, l_near, w_cross, l_cross, w_far, l_far, w_last, l_last, *rhs
     )
-    total = keep + swap(send)
+
+    def add_body(keep, send, *outs):
+        for k in range(slab_count):
+            outs[k][...] = keep[k] + send[k]
+
+    total = pl.pallas_call(
+        add_body,
+        out_shape=[piece] * slab_count,
+        in_specs=[vmem] * 2,
+        out_specs=[vmem] * slab_count,
+        compiler_params=grant,
+    )(keep, swap(send))
     shares = [total[0]] + [exchange(total[k], k) for k in range(1, slab_count)]
 
     def place_body(*refs):
-        scal = refs[0]
-        shares = refs[1 : 1 + slab_count]
-        out = refs[1 + slab_count]
+        scal = position()
+        shares = refs[:slab_count]
+        out = refs[slab_count]
         lane = lax.broadcasted_iota(jnp.int32, (half, lanes), 1)
         for slot in range(local_count):
             found = []
@@ -474,10 +533,10 @@
     return pl.pallas_call(
         place_body,
         out_shape=jax.ShapeDtypeStruct((local_count, 1, 2, half, columns), F32),
-        in_specs=[smem] + [vmem] * slab_count,
+        in_specs=[vmem] * slab_count,
         out_specs=vmem,
         compiler_params=grant,
-    )(scal, *shares)
+    )(*shares)
 
 
 def solution(mesh):
@@ -490,6 +549,7 @@
         P("win"),
         P("win"),
     )
+
     return jax.shard_map(
         per_device,
         mesh=mesh,

time: 109 us -> 71.9 us (0.66)
  the two profiles are of different devices: /device:TPU:1 before, /device:TPU:10 now
where the time goes in v2:
time: 71.9 us; the launch traced here: 71.6 us
  Pallas kernels  31.3 us (44%)
  starting transfers between devices  18 us (25%)
  waiting for transfers between devices  17.7 us (25%)
  local copies, waits for them, and re-layouts  4.46 us (6%)
    ppermute x8, starting transfers between devices, exchange(): lax.ppermute(value, 'slab', [(i, i ^ distance) for i in range(slab_count)])  9.22 us
    ppermute x8, waiting for transfers between devices, exchange(): lax.ppermute(value, 'slab', [(i, i ^ distance) for i in range(slab_count)])  9.21 us
    pallas_call x1, Pallas kernels, per_device(): pl.pallas_call(fourth_body, out_shape=[pair_shape] * 7, in_specs=[smem] +...  9.03 us
    ppermute x6, starting transfers between devices, along_win(): lax.ppermute(value, 'win', [(i, i ^ shift) for i in range(win_count)])  7.1 us
    pallas_call x1, Pallas kernels, per_device(): x_near, w_near, l_near = second(prm, x_own, couplings, *from_x)  5.65 us
    pallas_call x1, Pallas kernels, per_device(): pl.pallas_call(solve_body, out_shape=[quad] * 2, in_specs=[smem] + [vmem]...  4.92 us
    pallas_call x1, Pallas kernels, per_device(): pl.pallas_call(third_body, out_shape=[pair_shape] * 3 + [jax.ShapeDtypeSt...  4.5 us
    pallas_call x1, Pallas kernels, per_device(): x_own, prm = first(*head, diag_blocks)  4.49 us
  transfers between devices with their start and end apart: 20, of which 8 were waited for; matrix products, arithmetic and copies ran while one was open for 0% of the time, Pallas kernels for 35%

profile of v2, /device:TPU:10, one launch (start us, length us, event | category | flops | bytes accessed | tf_op | source)
XLA Modules:
  0.0 71.6 jit_solution(7716302683248377732)
XLA Ops:
  0.0 0.0 copy-start
  0.0 1.0 %copy-done = f32[2,1,2,256,128]{4,3,2,1,0:T(8,128)S(1)} copy-done((f32[2,1,2,256,128]{4,3,2,1,0:T(8,128)S(1)}, f32[2,1,2,256,128]{4,3,2,1,0:T(8,128)}, u32[]{:S(2)}) %copy-start) | copy-done | bytes 524312
  1.0 0.0 copy-start.1
  1.0 1.0 %copy-done.1 = f32[1,2,256,256]{3,2,1,0:T(8,128)S(1)} copy-done((f32[1,2,256,256]{3,2,1,0:T(8,128)S(1)}, f32[1,2,256,256]{3,2,1,0:T(8,128)}, u32[]{:S(2)}) %copy-start.1) | copy-done | bytes 524312
  2.1 0.0 copy-start.3
  2.1 1.0 %copy-done.3 = f32[1,2,256,256]{3,2,1,0:T(8,128)S(1)} copy-done((f32[1,2,256,256]{3,2,1,0:T(8,128)S(1)}, f32[1,2,256,256]{3,2,1,0:T(8,128)}, u32[]{:S(2)}) %copy-start.3) | copy-done | bytes 524312
  3.1 0.0 copy-start.5
  3.1 0.7 copy-done.5
  3.8 0.7 shard_map.74
  4.5 0.6 collective-permute-start.3
  5.1 1.5 %collective-permute-start.5 = (f32[3,128,256]{2,1,0:T(8,128)S(1)}, f32[3,128,256]{2,1,0:T(8,128)S(1)}, u32[]{:S(2)}, u32[]{:S(2)}) collective-permute-start(f32[3,128,256]{2,1,0:T(8,128)S(1)} %get-tuple-element.35), channel_id=1, source_target_pairs={{0,16},{8,24},{16,0},{24,8},{1,17},{9,25},{17,1},{25,9},{2,18},{10... | collective-permute-start | bytes 1179656 | tf_op jit(solution)/shard_map/ppermute | solution.py:187
  6.6 0.0 copy-start.7
  6.6 0.0 copy-start.8
  6.6 0.7 copy-done.7
  7.2 0.0 copy-done.8
  7.3 0.5 collective-permute-start
  7.8 2.6 %collective-permute-start.1 = (f32[2,2]{1,0:T(2,128)S(1)}, f32[2,2]{1,0:T(2,128)S(1)}, u32[]{:S(2)}, u32[]{:S(2)}) collective-permute-start(f32[2,2]{1,0:T(2,128)S(1)} %pad_maximum_fusion.refs_1_), channel_id=1, source_target_pairs={{0,2},{1,3},{2,0},{3,1},{4,6},{5,7},{6,4},{7,5},{8,10},{9,11},{10,... | collective-permute-start | bytes 56 | tf_op jit(solution)/shard_map/ppermute | solution.py:193
  10.4 0.5 collective-permute-start.2
  10.8 4.6 %collective-permute-done.3.refs_3_.refs_2_ = f32[3,128,256]{2,1,0:T(8,128)S(1)} collective-permute-done((f32[3,128,256]{2,1,0:T(8,128)S(1)}, f32[3,128,256]{2,1,0:T(8,128)S(1)}, u32[]{:S(2)}, u32[]{:S(2)}) %collective-permute-start.3) | collective-permute-done | bytes 393248 | tf_op jit(solution)/shard_map/ppermute | solution.py:187
  15.4 0.4 collective-permute-start.9
  15.8 0.0 collective-permute-done.5.refs_4_.refs_9_
  15.8 2.6 %collective-permute-start.10 = (f32[2,2,128,128]{3,2,1,0:T(8,128)S(1)}, f32[2,2,128,128]{3,2,1,0:T(8,128)S(1)}, u32[]{:S(2)}, u32[]{:S(2)}) collective-permute-start(f32[2,2,128,128]{3,2,1,0:T(8,128)S(1)} %get-tuple-element.49.refs_1_), channel_id=1, source_target_pairs={{0,2},{1,3},{2,0},{3,1},{4,6},{5,7},{6,4},{7,5},{8,10},{9,11},{10,... | collective-permute-start | bytes 786440 | tf_op jit(solution)/shard_map/ppermute | solution.py:193
  18.5 0.0 copy-start.4
  18.5 0.0 collective-permute-done.refs_2_
  18.5 0.5 collective-permute-start.11
  19.0 0.0 collective-permute-done.1.refs_3_
  19.0 0.9 %collective-permute-start.7 = (f32[3,128,256]{2,1,0:T(8,128)S(1)}, f32[3,128,256]{2,1,0:T(8,128)S(1)}, u32[]{:S(2)}, u32[]{:S(2)}) collective-permute-start(f32[3,128,256]{2,1,0:T(8,128)S(1)} %broadcast_select_fusion), channel_id=1, source_target_pairs={{0,8},{8,0},{16,24},{24,16},{4,20},{12,28},{20,4},{28,12},{1,9},{9... | collective-permute-start | bytes 1179656 | tf_op jit(solution)/shard_map/ppermute | solution.py:265
  19.9 0.0 collective-permute-done.2.refs_4_
  20.0 0.0 collective-permute-start.4
  20.0 0.0 copy-done.2
  20.0 0.0 copy-done.6
  20.0 4.5 %shard_map.73 = (bf16[256,1024]{1,0:T(8,128)(2,1)S(1)}, f32[4]{0:T(128)S(1)}) custom-call(s32[8]{0:T(128)S(1)} %copy-done.6, f32[2,2]{1,0:T(2,128)S(1)} %pad_maximum_fusion.refs_1_, f32[2,2]{1,0:T(2,128)S(1)} %collective-permute-done.refs_2_, f32[2,2]{1,0:T(2,128)S(1)} %collective-permute-done.1.refs_3_, f32[2,2]{1,0:T(2,128)S(1)} %collective-permute-done.2.refs_4_, ...), custom_call_target="tpu_custom_call" | custom-call | flops 6000000000 | bytes 6000000 | tf_op jit(solution)/shard_map/pallas_call | solution.py:260
  24.5 0.0 collective-permute-done.4.refs_4_.refs_3_
  24.5 0.6 collective-permute-start.6
  25.0 1.8 %collective-permute-done.7.refs_11_ = f32[3,128,256]{2,1,0:T(8,128)S(1)} collective-permute-done((f32[3,128,256]{2,1,0:T(8,128)S(1)}, f32[3,128,256]{2,1,0:T(8,128)S(1)}, u32[]{:S(2)}, u32[]{:S(2)}) %collective-permute-start.7) | collective-permute-done | bytes 393248 | tf_op jit(solution)/shard_map/ppermute | solution.py:265
  26.8 0.0 collective-permute-start.8
  26.8 0.0 copy-done.4
  26.8 5.6 %shard_map.75 = (bf16[256,1024]{1,0:T(8,128)(2,1)S(1)}, bf16[256,1024]{1,0:T(8,128)(2,1)S(1)}, bf16[256,1024]{1,0:T(8,128)(2,1)S(1)}) custom-call(f32[4]{0:T(128)S(1)} %get-tuple-element.33.refs_0_, bf16[256,1024]{1,0:T(8,128)(2,1)S(1)} %get-tuple-element.34.refs_1_, f32[1,2,256,256]{3,2,1,0:T(8,128)S(1)} %copy-done.4, ...), custom_call_target="tpu_custom_call" | custom-call | flops 8000000000 | bytes 8000000 | tf_op jit(solution)/shard_map/pallas_call | solution.py:305
  32.5 0.0 collective-permute-done.6.refs_5_.refs_10_
  32.5 4.5 %shard_map.76 = (bf16[256,1024]{1,0:T(8,128)(2,1)S(1)}, bf16[256,1024]{1,0:T(8,128)(2,1)S(1)}, bf16[256,1024]{1,0:T(8,128)(2,1)S(1)}, f32[4]{0:T(128)S(1)}) custom-call(f32[4]{0:T(128)S(1)} %get-tuple-element.33.refs_0_, bf16[256,1024]{1,0:T(8,128)(2,1)S(1)} %get-tuple-element.36.refs_1_.refs_2_, f32[3,128,256]{2,1,0:T(8,128)S(1)} %collective-permute-done.3.refs_3_.refs_2_, ...), custom_call_target="tpu_custom_call" | custom-call | flops 8000000000 | bytes 8000000 | tf_op jit(solution)/shard_map/pallas_call | solution.py:338
  37.0 0.0 collective-permute-done.9.refs_2_
  37.0 0.0 collective-permute-done.10.refs_3_
  37.0 3.7 %collective-permute-done.11.refs_4_ = f32[2,2,128,128]{3,2,1,0:T(8,128)S(1)} collective-permute-done((f32[2,2,128,128]{3,2,1,0:T(8,128)S(1)}, f32[2,2,128,128]{3,2,1,0:T(8,128)S(1)}, u32[]{:S(2)}, u32[]{:S(2)}) %collective-permute-start.11) | collective-permute-done | bytes 262176 | tf_op jit(solution)/shard_map/ppermute | solution.py:193
  40.7 1.1 %shard_map.78.mine = f32[4,128,128]{2,1,0:T(8,128)S(1)} custom-call(s32[8]{0:T(128)S(1)} %copy-done.6, f32[2,2,128,128]{3,2,1,0:T(8,128)S(1)} %get-tuple-element.49.refs_1_, f32[2,2,128,128]{3,2,1,0:T(8,128)S(1)} %collective-permute-done.9.refs_2_, f32[2,2,128,128]{3,2,1,0:T(8,128)S(1)} %collective-permute-done.10.refs_3_, ...), custom_call_target="tpu_custom_call" | custom-call | flops 2000000000 | bytes 2000000 | tf_op jit(solution)/shard_map/pallas_call | solution.py:372
  41.7 0.1 collective-permute-start.12
  41.8 1.5 %collective-permute-done.12.other = f32[4,128,128]{2,1,0:T(8,128)S(1)} collective-permute-done((f32[4,128,128]{2,1,0:T(8,128)S(1)}, f32[4,128,128]{2,1,0:T(8,128)S(1)}, u32[]{:S(2)}, u32[]{:S(2)}) %collective-permute-start.12) | collective-permute-done | bytes 262176 | tf_op jit(solution)/shard_map/ppermute | solution.py:190
  43.4 0.6 collective-permute-start.13
  44.0 1.5 %collective-permute-start.14 = (f32[256,128]{1,0:T(8,128)S(1)}, f32[256,128]{1,0:T(8,128)S(1)}, u32[]{:S(2)}, u32[]{:S(2)}) collective-permute-start(f32[256,128]{1,0:T(8,128)S(1)} %get-tuple-element.53), channel_id=1, source_target_pairs={{0,16},{8,24},{16,0},{24,8},{1,17},{9,25},{17,1},{25,9},{2,18},{10... | collective-permute-start | bytes 393224 | tf_op jit(solution)/shard_map/ppermute | solution.py:187
  45.5 1.4 %collective-permute-start.15 = (f32[256,128]{1,0:T(8,128)S(1)}, f32[256,128]{1,0:T(8,128)S(1)}, u32[]{:S(2)}, u32[]{:S(2)}) collective-permute-start(f32[256,128]{1,0:T(8,128)S(1)} %get-tuple-element.54), channel_id=1, source_target_pairs={{0,24},{8,16},{16,8},{24,0},{1,25},{9,17},{17,9},{25,1},{2,26},{10... | collective-permute-start | bytes 393224 | tf_op jit(solution)/shard_map/ppermute | solution.py:187
  47.0 0.0 collective-permute-done.8.refs_12_
  47.0 9.0 %shard_map.77 = (bf16[256,1024]{1,0:T(8,128)(2,1)S(1)}, bf16[256,1024]{1,0:T(8,128)(2,1)S(1)}, bf16[256,1024]{1,0:T(8,128)(2,1)S(1)}, bf16[256,1024]{1,0:T(8,128...) custom-call(f32[4]{0:T(128)S(1)} %get-tuple-element.33.refs_0_, ...), custom_call_target="tpu_custom_call" | custom-call | flops 10000000000 | bytes 10000000 | tf_op jit(solution)/shard_map/pallas_call | solution.py:451
  56.0 0.0 collective-permute-done.13.refs_14_
  56.0 0.0 collective-permute-done.14.refs_15_
  56.0 0.0 collective-permute-done.15.refs_16_
  56.0 4.9 %shard_map.80 = (f32[4,128,128]{2,1,0:T(8,128)S(1)}, f32[4,128,128]{2,1,0:T(8,128)S(1)}) custom-call(f32[4]{0:T(128)S(1)} %get-tuple-element.33.refs_0_, bf16[256,1024]{1,0:T(8,128)(2,1)S(1)} %get-tuple-element.34.refs_1_, bf16[256,1024]{1,0:T(8,128)(2,1)S(1)} %get-tuple-element.36.refs_1_.refs_2_, bf16[256,1024]{1,0:T(8,128)(2,1)S(1)} %get-tuple-element.37.refs_3_, ...), custom_call_target="tpu_custom_call" | custom-call | flops 8000000000 | bytes 8000000 | tf_op jit(solution)/shard_map/pallas_call | solution.py:492
  61.0 0.1 collective-permute-start.16
  61.0 1.5 %collective-permute-done.16.send = f32[4,128,128]{2,1,0:T(8,128)S(1)} collective-permute-done((f32[4,128,128]{2,1,0:T(8,128)S(1)}, f32[4,128,128]{2,1,0:T(8,128)S(1)}, u32[]{:S(2)}, u32[]{:S(2)}) %collective-permute-start.16) | collective-permute-done | bytes 262176 | tf_op jit(solution)/shard_map/ppermute | solution.py:190
  62.6 0.1 collective-permute-start.17
  62.7 2.9 %collective-permute-start.18 = (f32[128,128]{1,0:T(8,128)S(1)}, f32[128,128]{1,0:T(8,128)S(1)}, u32[]{:S(2)}, u32[]{:S(2)}) collective-permute-start(f32[128,128]{1,0:T(8,128)S(1)} %get-tuple-element.59), channel_id=1, source_target_pairs={{0,16},{8,24},{16,0},{24,8},{1,17},{9,25},{17,1},{25,9},{2,18},{10... | collective-permute-start | bytes 196616 | tf_op jit(solution)/shard_map/ppermute | solution.py:187
  65.6 0.5 collective-permute-start.19
  66.1 0.8 %collective-permute-done.17.refs_1_ = f32[128,128]{1,0:T(8,128)S(1)} collective-permute-done((f32[128,128]{1,0:T(8,128)S(1)}, f32[128,128]{1,0:T(8,128)S(1)}, u32[]{:S(2)}, u32[]{:S(2)}) %collective-permute-start.17) | collective-permute-done | bytes 65568 | tf_op jit(solution)/shard_map/ppermute | solution.py:187
  66.9 1.7 %collective-permute-done.18.refs_2_ = f32[128,128]{1,0:T(8,128)S(1)} collective-permute-done((f32[128,128]{1,0:T(8,128)S(1)}, f32[128,128]{1,0:T(8,128)S(1)}, u32[]{:S(2)}, u32[]{:S(2)}) %collective-permute-start.18) | collective-permute-done | bytes 65568 | tf_op jit(solution)/shard_map/ppermute | solution.py:187
  68.6 2.2 %collective-permute-done.19.refs_3_ = f32[128,128]{1,0:T(8,128)S(1)} collective-permute-done((f32[128,128]{1,0:T(8,128)S(1)}, f32[128,128]{1,0:T(8,128)S(1)}, u32[]{:S(2)}, u32[]{:S(2)}) %collective-permute-start.19) | collective-permute-done | bytes 65568 | tf_op jit(solution)/shard_map/ppermute | solution.py:187
  70.8 0.8 %shard_map.82 = f32[2,1,2,128,128]{4,3,2,1,0:T(8,128)} custom-call(f32[128,128]{1,0:T(8,128)S(1)} %get-tuple-element.57.refs_0_, f32[128,128]{1,0:T(8,128)S(1)} %collective-permute-done.17.refs_1_, f32[128,128]{1,0:T(8,128)S(1)} %collective-permute-done.18.refs_2_, f32[128,128]{1,0:T(8,128)S(1)} %collective-permute-done.19.refs_3_), custom_call_target="tpu_custom_call" | custom-call | tf_op jit(solution)/shard_map/pallas_call | solution.py:533
  (6 shorter events, 0.1 us)
Async XLA Ops:
  0.0 1.0 %copy-start = (f32[2,1,2,256,128]{4,3,2,1,0:T(8,128)S(1)}, f32[2,1,2,256,128]{4,3,2,1,0:T(8,128)}, u32[]{:S(2)}) copy-start(f32[2,1,2,256,128]{4,3,2,1,0:T(8,128)} %vectors.1) | copy-start | bytes 1572868
  1.0 1.0 %copy-start.1 = (f32[1,2,256,256]{3,2,1,0:T(8,128)S(1)}, f32[1,2,256,256]{3,2,1,0:T(8,128)}, u32[]{:S(2)}) copy-start(f32[1,2,256,256]{3,2,1,0:T(8,128)} %diag.1) | copy-start | bytes 1572868
  2.1 1.0 %copy-start.3 = (f32[1,2,256,256]{3,2,1,0:T(8,128)S(1)}, f32[1,2,256,256]{3,2,1,0:T(8,128)}, u32[]{:S(2)}) copy-start(f32[1,2,256,256]{3,2,1,0:T(8,128)} %refs_8_.1) | copy-start | bytes 1572868
  3.1 0.7 copy-start.5
  4.5 10.9 %collective-permute-start.3 = (f32[3,128,256]{2,1,0:T(8,128)S(1)}, f32[3,128,256]{2,1,0:T(8,128)S(1)}, u32[]{:S(2)}, u32[]{:S(2)}) collective-permute-start(f32[3,128,256]{2,1,0:T(8,128)S(1)} %get-tuple-element.35), channel_id=1, source_target_pairs={{0,8},{8,0},{16,24},{24,16},{1,9},{9,1},{17,25},{25,17},{2,10},{10... | collective-permute-start | bytes 1179656 | tf_op jit(solution)/shard_map/ppermute | solution.py:187
  5.1 10.8 %collective-permute-start.5 = (f32[3,128,256]{2,1,0:T(8,128)S(1)}, f32[3,128,256]{2,1,0:T(8,128)S(1)}, u32[]{:S(2)}, u32[]{:S(2)}) collective-permute-start(f32[3,128,256]{2,1,0:T(8,128)S(1)} %get-tuple-element.35), channel_id=1, source_target_pairs={{0,16},{8,24},{16,0},{24,8},{1,17},{9,25},{17,1},{25,9},{2,18},{10... | collective-permute-start | bytes 1179656 | tf_op jit(solution)/shard_map/ppermute | solution.py:187
  6.6 0.7 copy-start.7
  6.6 0.7 copy-start.8
  7.3 11.2 %collective-permute-start = (f32[2,2]{1,0:T(2,128)S(1)}, f32[2,2]{1,0:T(2,128)S(1)}, u32[]{:S(2)}, u32[]{:S(2)}) collective-permute-start(f32[2,2]{1,0:T(2,128)S(1)} %pad_maximum_fusion.refs_1_), channel_id=1, source_target_pairs={{0,1},{1,0},{2,3},{3,2},{4,5},{5,4},{6,7},{7,6},{8,9},{9,8},{10,11... | collective-permute-start | bytes 56 | tf_op jit(solution)/shard_map/ppermute | solution.py:193
  7.8 11.3 %collective-permute-start.1 = (f32[2,2]{1,0:T(2,128)S(1)}, f32[2,2]{1,0:T(2,128)S(1)}, u32[]{:S(2)}, u32[]{:S(2)}) collective-permute-start(f32[2,2]{1,0:T(2,128)S(1)} %pad_maximum_fusion.refs_1_), channel_id=1, source_target_pairs={{0,2},{1,3},{2,0},{3,1},{4,6},{5,7},{6,4},{7,5},{8,10},{9,11},{10,... | collective-permute-start | bytes 56 | tf_op jit(solution)/shard_map/ppermute | solution.py:193
  10.4 9.6 %collective-permute-start.2 = (f32[2,2]{1,0:T(2,128)S(1)}, f32[2,2]{1,0:T(2,128)S(1)}, u32[]{:S(2)}, u32[]{:S(2)}) collective-permute-start(f32[2,2]{1,0:T(2,128)S(1)} %pad_maximum_fusion.refs_1_), channel_id=1, source_target_pairs={{0,3},{1,2},{2,1},{3,0},{4,7},{5,6},{6,5},{7,4},{8,11},{9,10},{10,... | collective-permute-start | bytes 56 | tf_op jit(solution)/shard_map/ppermute | solution.py:193
  15.4 4.6 %copy-start.2 = (f32[1,2,256,256]{3,2,1,0:T(8,128)S(1)}, f32[1,2,256,256]{3,2,1,0:T(8,128)}, u32[]{:S(2)}) copy-start(f32[1,2,256,256]{3,2,1,0:T(8,128)} %diag.1) | copy-start | bytes 1572868
  15.4 4.6 %copy-start.6 = (s32[8]{0:T(128)S(1)}, s32[8]{0:T(128)}, u32[]{:S(2)}) copy-start(s32[8]{0:T(128)} %refs_0_.3) | copy-start | bytes 100
  15.4 21.6 %collective-permute-start.9 = (f32[2,2,128,128]{3,2,1,0:T(8,128)S(1)}, f32[2,2,128,128]{3,2,1,0:T(8,128)S(1)}, u32[]{:S(2)}, u32[]{:S(2)}) collective-permute-start(f32[2,2,128,128]{3,2,1,0:T(8,128)S(1)} %get-tuple-element.49.refs_1_), channel_id=1, source_target_pairs={{0,1},{1,0},{2,3},{3,2},{4,5},{5,4},{6,7},{7,6},{8,9},{9,8},{10,11... | collective-permute-start | bytes 786440 | tf_op jit(solution)/shard_map/ppermute | solution.py:193
  15.8 21.1 %collective-permute-start.10 = (f32[2,2,128,128]{3,2,1,0:T(8,128)S(1)}, f32[2,2,128,128]{3,2,1,0:T(8,128)S(1)}, u32[]{:S(2)}, u32[]{:S(2)}) collective-permute-start(f32[2,2,128,128]{3,2,1,0:T(8,128)S(1)} %get-tuple-element.49.refs_1_), channel_id=1, source_target_pairs={{0,2},{1,3},{2,0},{3,1},{4,6},{5,7},{6,4},{7,5},{8,10},{9,11},{10,... | collective-permute-start | bytes 786440 | tf_op jit(solution)/shard_map/ppermute | solution.py:193
  18.5 8.3 %copy-start.4 = (f32[1,2,256,256]{3,2,1,0:T(8,128)S(1)}, f32[1,2,256,256]{3,2,1,0:T(8,128)}, u32[]{:S(2)}) copy-start(f32[1,2,256,256]{3,2,1,0:T(8,128)} %refs_8_.1) | copy-start | bytes 1572868
  18.5 22.2 %collective-permute-start.11 = (f32[2,2,128,128]{3,2,1,0:T(8,128)S(1)}, f32[2,2,128,128]{3,2,1,0:T(8,128)S(1)}, u32[]{:S(2)}, u32[]{:S(2)}) collective-permute-start(f32[2,2,128,128]{3,2,1,0:T(8,128)S(1)} %get-tuple-element.49.refs_1_), channel_id=1, source_target_pairs={{0,3},{1,2},{2,1},{3,0},{4,7},{5,6},{6,5},{7,4},{8,11},{9,10},{10,... | collective-permute-start | bytes 786440 | tf_op jit(solution)/shard_map/ppermute | solution.py:193
  19.0 7.8 %collective-permute-start.7 = (f32[3,128,256]{2,1,0:T(8,128)S(1)}, f32[3,128,256]{2,1,0:T(8,128)S(1)}, u32[]{:S(2)}, u32[]{:S(2)}) collective-permute-start(f32[3,128,256]{2,1,0:T(8,128)S(1)} %broadcast_select_fusion), channel_id=1, source_target_pairs={{0,8},{8,0},{16,24},{24,16},{4,20},{12,28},{20,4},{28,12},{1,9},{9... | collective-permute-start | bytes 1179656 | tf_op jit(solution)/shard_map/ppermute | solution.py:265
  20.0 4.5 %collective-permute-start.4 = (f32[3,128,256]{2,1,0:T(8,128)S(1)}, f32[3,128,256]{2,1,0:T(8,128)S(1)}, u32[]{:S(2)}, u32[]{:S(2)}) collective-permute-start(f32[3,128,256]{2,1,0:T(8,128)S(1)} %collective-permute-done.3.refs_3_.refs_2_), channel_id=1, source_target_pairs={{0,4},{4,0},{1,5},{5,1},{2,6},{6,2},{3,7},{7,3},{8,12},{12,8},{9,1... | collective-permute-start | bytes 1179656 | tf_op jit(solution)/shard_map/ppermute | solution.py:190
  24.5 8.0 %collective-permute-start.6 = (f32[3,128,256]{2,1,0:T(8,128)S(1)}, f32[3,128,256]{2,1,0:T(8,128)S(1)}, u32[]{:S(2)}, u32[]{:S(2)}) collective-permute-start(f32[3,128,256]{2,1,0:T(8,128)S(1)} %collective-permute-done.5.refs_4_.refs_9_), channel_id=1, source_target_pairs={{0,4},{4,0},{1,5},{5,1},{2,6},{6,2},{3,7},{7,3},{8,12},{12,8},{9,1... | collective-permute-start | bytes 1179656 | tf_op jit(solution)/shard_map/ppermute | solution.py:190
  26.8 20.2 %collective-permute-start.8 = (f32[3,128,256]{2,1,0:T(8,128)S(1)}, f32[3,128,256]{2,1,0:T(8,128)S(1)}, u32[]{:S(2)}, u32[]{:S(2)}) collective-permute-start(f32[3,128,256]{2,1,0:T(8,128)S(1)} %collective-permute-done.7.refs_11_), channel_id=1, source_target_pairs={{0,4},{4,0},{1,5},{5,1},{2,6},{6,2},{3,7},{7,3},{8,12},{12,8},{9,1... | collective-permute-start | bytes 1179656 | tf_op jit(solution)/shard_map/ppermute | solution.py:190
  41.7 1.6 %collective-permute-start.12 = (f32[4,128,128]{2,1,0:T(8,128)S(1)}, f32[4,128,128]{2,1,0:T(8,128)S(1)}, u32[]{:S(2)}, u32[]{:S(2)}) collective-permute-start(f32[4,128,128]{2,1,0:T(8,128)S(1)} %shard_map.78.mine), channel_id=1, source_target_pairs={{0,4},{4,0},{1,5},{5,1},{2,6},{6,2},{3,7},{7,3},{8,12},{12,8},{9,1... | collective-permute-start | bytes 786440 | tf_op jit(solution)/shard_map/ppermute | solution.py:190
  43.4 12.6 %collective-permute-start.13 = (f32[256,128]{1,0:T(8,128)S(1)}, f32[256,128]{1,0:T(8,128)S(1)}, u32[]{:S(2)}, u32[]{:S(2)}) collective-permute-start(f32[256,128]{1,0:T(8,128)S(1)} %get-tuple-element.52), channel_id=1, source_target_pairs={{0,8},{8,0},{16,24},{24,16},{1,9},{9,1},{17,25},{25,17},{2,10},{10... | collective-permute-start | bytes 393224 | tf_op jit(solution)/shard_map/ppermute | solution.py:187
  44.0 12.0 %collective-permute-start.14 = (f32[256,128]{1,0:T(8,128)S(1)}, f32[256,128]{1,0:T(8,128)S(1)}, u32[]{:S(2)}, u32[]{:S(2)}) collective-permute-start(f32[256,128]{1,0:T(8,128)S(1)} %get-tuple-element.53), channel_id=1, source_target_pairs={{0,16},{8,24},{16,0},{24,8},{1,17},{9,25},{17,1},{25,9},{2,18},{10... | collective-permute-start | bytes 393224 | tf_op jit(solution)/shard_map/ppermute | solution.py:187
  45.5 10.5 %collective-permute-start.15 = (f32[256,128]{1,0:T(8,128)S(1)}, f32[256,128]{1,0:T(8,128)S(1)}, u32[]{:S(2)}, u32[]{:S(2)}) collective-permute-start(f32[256,128]{1,0:T(8,128)S(1)} %get-tuple-element.54), channel_id=1, source_target_pairs={{0,24},{8,16},{16,8},{24,0},{1,25},{9,17},{17,9},{25,1},{2,26},{10... | collective-permute-start | bytes 393224 | tf_op jit(solution)/shard_map/ppermute | solution.py:187
  61.0 1.6 %collective-permute-start.16 = (f32[4,128,128]{2,1,0:T(8,128)S(1)}, f32[4,128,128]{2,1,0:T(8,128)S(1)}, u32[]{:S(2)}, u32[]{:S(2)}) collective-permute-start(f32[4,128,128]{2,1,0:T(8,128)S(1)} %get-tuple-element.56), channel_id=1, source_target_pairs={{0,4},{4,0},{1,5},{5,1},{2,6},{6,2},{3,7},{7,3},{8,12},{12,8},{9,1... | collective-permute-start | bytes 786440 | tf_op jit(solution)/shard_map/ppermute | solution.py:190
  62.6 4.3 %collective-permute-start.17 = (f32[128,128]{1,0:T(8,128)S(1)}, f32[128,128]{1,0:T(8,128)S(1)}, u32[]{:S(2)}, u32[]{:S(2)}) collective-permute-start(f32[128,128]{1,0:T(8,128)S(1)} %get-tuple-element.58), channel_id=1, source_target_pairs={{0,8},{8,0},{16,24},{24,16},{1,9},{9,1},{17,25},{25,17},{2,10},{10... | collective-permute-start | bytes 196616 | tf_op jit(solution)/shard_map/ppermute | solution.py:187
  62.7 5.9 %collective-permute-start.18 = (f32[128,128]{1,0:T(8,128)S(1)}, f32[128,128]{1,0:T(8,128)S(1)}, u32[]{:S(2)}, u32[]{:S(2)}) collective-permute-start(f32[128,128]{1,0:T(8,128)S(1)} %get-tuple-element.59), channel_id=1, source_target_pairs={{0,16},{8,24},{16,0},{24,8},{1,17},{9,25},{17,1},{25,9},{2,18},{10... | collective-permute-start | bytes 196616 | tf_op jit(solution)/shard_map/ppermute | solution.py:187
  65.6 5.2 %collective-permute-start.19 = (f32[128,128]{1,0:T(8,128)S(1)}, f32[128,128]{1,0:T(8,128)S(1)}, u32[]{:S(2)}, u32[]{:S(2)}) collective-permute-start(f32[128,128]{1,0:T(8,128)S(1)} %get-tuple-element.60), channel_id=1, source_target_pairs={{0,24},{8,16},{16,8},{24,0},{1,25},{9,17},{17,9},{25,1},{2,26},{10... | collective-permute-start | bytes 196616 | tf_op jit(solution)/shard_map/ppermute | solution.py:187

commit v3 on v2

--- a/solution.py
+++ b/solution.py
@@ -11,6 +11,8 @@
 F32 = jnp.float32
 BF16 = jnp.bfloat16
 COARSE = 0.1
+FINE = 0.016
+ROOM = 3.2
 
 
 def dot(left, right):
@@ -46,11 +48,6 @@
 def times_i(value):
     half = value.shape[1] // 2
     return jnp.concatenate([-value[:, half:], value[:, :half]], 1)
-
-
-def column_triple(value):
-    high, low = hi_lo(jnp.concatenate([value, times_i(value)], 0))
-    return jnp.concatenate([high, high, low], 0)
 
 
 def lasting(micros):
@@ -69,8 +66,9 @@
     s_emb[...] = embed_triple(s_re, s_im)
     adj_re, adj_im = s_re.T, -s_im.T
     gram = dot(jnp.concatenate([adj_re, adj_im], 1).astype(BF16), s_emb[0 : 2 * n, :])
-    sums = jnp.sum(jnp.abs(gram), 0, keepdims=True)
-    bound_sq = jnp.max(sums[:, :n] + sums[:, n:], axis=1, keepdims=True)
+    total_sq = jnp.sum(jnp.sum(s_re * s_re + s_im * s_im, 0, keepdims=True), 1, keepdims=True)
+    total_4th = jnp.sum(jnp.sum(gram * gram, 0, keepdims=True), 1, keepdims=True)
+    bound_sq = ROOM * total_4th / total_sq
     bound = jnp.sqrt(bound_sq)
     ratio = jnp.abs(zeta_im) / bound
     shrink = 1.0 / (1.0 + ratio + ratio * ratio)
@@ -92,13 +90,45 @@
         work[:, 2 * n :] = embed(x_now[:, :n], x_now[:, n:]).astype(BF16)
         return size * size
 
-    lax.while_loop(lambda size: size > COARSE, double, shrink[0, 0])
+    lax.while_loop(lambda size: size * size > COARSE, double, shrink[0, 0])
+    x_now = x_ref[...] + dot(work[0:n, 0 : 2 * n], work[:, 2 * n :])
     wide_eye = jnp.concatenate([eye, jnp.zeros((n, n), F32)], 1)
-    rest = wide_eye - dot(work[0:n, 2 * n :], s_emb[0 : 2 * n, :])
-    x_ref[...] = x_ref[...] + dot(rest.astype(BF16), work[:, 2 * n :])
-    x_now = x_ref[...]
-    rest = wide_eye - dot(left_triple(packed_pair(x_now)), s_emb[...])
-    return x_now + dot(rest.astype(BF16), embed(x_now[:, :n], x_now[:, n:]).astype(BF16))
+    x_emb = embed(x_now[:, :n], x_now[:, n:]).astype(BF16)
+    work[:, 2 * n :] = x_emb
+    rest = wide_eye - dot(x_emb[0:n, :], s_emb[0 : 2 * n, :])
+    x_now = x_now + dot(rest.astype(BF16), work[:, 2 * n :])
+
+    def correct(value):
+        rounded = embed(value[:, :n], value[:, n:]).astype(BF16)
+        work[:, 2 * n :] = rounded
+        left = rounded[0:n, :]
+        rest = wide_eye - dot(jnp.concatenate([left, left], 1), s_emb[2 * n :, :])
+        x_ref[...] = left.astype(F32) + dot(rest.astype(BF16), work[:, 2 * n :])
+        return jnp.sum(jnp.sum(rest * rest, 0, keepdims=True), 1, keepdims=True)[0, 0]
+
+    size = correct(x_now)
+
+    def again(state):
+        before, safe, steps = state
+        size = correct(x_ref[...])
+        restart = jnp.logical_and(jnp.logical_not(size < before), safe == 0)
+
+        @pl.when(restart)
+        def _():
+            x_ref[...] = jnp.concatenate([s_re.T, -s_im.T], 1) / total_sq
+
+        return (
+            jnp.where(restart, jnp.float32(4 * n), size),
+            jnp.where(restart, 1, safe),
+            steps + 1,
+        )
+
+    lax.while_loop(
+        lambda state: jnp.logical_and(jnp.logical_not(state[0] <= FINE), state[2] < 96),
+        again,
+        (size, jnp.int32(0), jnp.int32(0)),
+    )
+    return x_ref[...]
 
 
 def pick(flag, if_true, if_false):
@@ -197,37 +227,16 @@
     for k in range(1, win_count):
         tables.append(along_win(table, k))
 
-    def prepare_body(widths, diag, links, vectors, carried, block, pair, sems):
-        start = position()[2] * half
-        rows = pl.ds(start, half)
-        moves = [pltpu.make_async_copy(diag.at[0, :, rows, :], pair, sems.at[0])]
-        moves.append(pltpu.make_async_copy(links.at[0, :, rows, :], carried.at[pl.ds(1, 2)], sems.at[1]))
-        moves.append(pltpu.make_async_copy(vectors.at[:, 0, :, rows, :], block, sems.at[2]))
-        for move in moves:
-            move.start()
-        for move in moves:
-            move.wait()
-        row = lax.broadcasted_iota(jnp.int32, (half, n), 0) + start
-        col = lax.broadcasted_iota(jnp.int32, (half, n), 1)
-        carried[0] = jnp.where(row >= col, pair[0], pair[1])
-        number = lax.broadcasted_iota(jnp.int32, (half, columns), 1)
-        for j in range(local_count):
-            for k in range(2):
-                block[j, k] = jnp.where(number < widths[j], block[j, k], 0.0)
-
-    anywhere = pl.BlockSpec(memory_space=pltpu.HBM)
-    prepare = pl.pallas_call(
-        prepare_body,
-        out_shape=[
-            jax.ShapeDtypeStruct((3, half, n), F32),
-            jax.ShapeDtypeStruct((local_count, 2, half, columns), F32),
-        ],
-        in_specs=[smem] + [anywhere] * 3,
-        out_specs=[vmem] * 2,
-        scratch_shapes=[pltpu.VMEM((2, half, n), F32), pltpu.SemaphoreType.DMA((3,))],
-        compiler_params=grant,
-    )
-    carried, block = prepare(widths, diag_blocks, couplings, subspace)
+    start = lax.axis_index("point") * half
+    row = lax.broadcasted_iota(jnp.int32, (half, n), 0) + start
+    col = lax.broadcasted_iota(jnp.int32, (half, n), 1)
+    diag_part = lax.dynamic_slice_in_dim(diag_blocks[0], start, half, 1)
+    link_part = lax.dynamic_slice_in_dim(couplings[0], start, half, 1)
+    packed = jnp.where(row >= col, diag_part[0], diag_part[1])
+    carried = jnp.concatenate([packed[None], link_part], 0)
+    live = jnp.arange(columns, dtype=jnp.int32)[None, :] < widths[:, None]
+    block = lax.dynamic_slice_in_dim(subspace[:, 0], start, half, 2)
+    block = jnp.where(live[:, None, None, :], block, 0.0)
     from_x = exchange(carried, 1)
     from_y = exchange(carried, 2)
     blocks = [block]
@@ -468,7 +477,10 @@
         chain = lax.rem(scal[1], 2) == scal[1] // 2
 
         def apply(ref, value):
-            return dot(left_triple(ref[...]), column_triple(value))
+            pair = ref[...]
+            high, low = hi_lo(jnp.concatenate([value, times_i(value)], 0))
+            wide = dot(pair[:, : 2 * n], jnp.concatenate([high, low], 1))
+            return wide[:, :lanes] + wide[:, lanes:] + dot(pair[:, 2 * n :], high)
 
         b_own, b_near, b_side, b_far = [ref[...] for ref in loaded]
         u_own = apply(x_own, b_own)

time: 71.9 us -> 69.9 us (0.972)
  the two profiles are of different devices: /device:TPU:10 before, /device:TPU:0 now
where the time goes in v3:
time: 69.9 us; the launch traced here: 69.7 us
  Pallas kernels  27.6 us (39%)
  starting transfers between devices  24.2 us (35%)
  waiting for transfers between devices  15.7 us (22%)
  local copies, waits for them, and re-layouts  1 us (1%)
  other arithmetic  1 us (1%)
    ppermute x8, starting transfers between devices, exchange(): lax.ppermute(value, 'slab', [(i, i ^ distance) for i in range(slab_count)])  12 us
    ppermute x8, waiting for transfers between devices, exchange(): lax.ppermute(value, 'slab', [(i, i ^ distance) for i in range(slab_count)])  11.6 us
    ppermute x6, starting transfers between devices, along_win(): lax.ppermute(value, 'win', [(i, i ^ shift) for i in range(win_count)])  9.87 us
    pallas_call x1, Pallas kernels, per_device(): pl.pallas_call(third_body, out_shape=[pair_shape] * 3 + [jax.ShapeDtypeSt...  6.07 us
    pallas_call x1, Pallas kernels, per_device(): pl.pallas_call(fourth_body, out_shape=[pair_shape] * 7, in_specs=[smem] +...  5.79 us
    pallas_call x1, Pallas kernels, per_device(): x_near, w_near, l_near = second(prm, x_own, couplings, *from_x)  5.33 us
    pallas_call x1, Pallas kernels, per_device(): x_own, prm = first(*head, diag_blocks)  4.67 us
    pallas_call x1, Pallas kernels, per_device(): pl.pallas_call(solve_body, out_shape=[quad] * 2, in_specs=[smem] + [vmem]...  3.69 us
  transfers between devices with their start and end apart: 20, of which 7 were waited for; matrix products, arithmetic and copies ran while one was open for 2% of the time, Pallas kernels for 33%

profile of v3, /device:TPU:0, one launch (start us, length us, event | category | flops | bytes accessed | tf_op | source)
XLA Modules:
  0.0 69.7 jit_solution(6353156779510857522)
XLA Ops:
  0.0 0.0 copy-start.1
  0.0 0.7 %pad_maximum_fusion.1.refs_1_ = f32[2,2]{1,0:T(2,128)S(1)} fusion(f32[1,2]{1,0:T(1,128)} %bitcast.14, f32[1,2]{1,0:T(1,128)} %bitcast.15), kind=kLoop, calls=%fused_computation.8 | loop fusion | flops 4 | bytes 32 | tf_op jit(solution)/shard_map/stack | solution.py:225
  0.7 3.1 %collective-permute-start = (f32[2,2]{1,0:T(2,128)S(1)}, f32[2,2]{1,0:T(2,128)S(1)}, u32[]{:S(2)}, u32[]{:S(2)}) collective-permute-start(f32[2,2]{1,0:T(2,128)S(1)} %pad_maximum_fusion.1.refs_1_), channel_id=1, source_target_pairs={{0,1},{1,0},{2,3},{3,2},{4,5},{5,4},{6,7},{7,6},{8,9},{9,8},{10,11... | collective-permute-start | bytes 56 | tf_op jit(solution)/shard_map/ppermute | solution.py:223
  3.8 2.6 %collective-permute-start.1 = (f32[2,2]{1,0:T(2,128)S(1)}, f32[2,2]{1,0:T(2,128)S(1)}, u32[]{:S(2)}, u32[]{:S(2)}) collective-permute-start(f32[2,2]{1,0:T(2,128)S(1)} %pad_maximum_fusion.1.refs_1_), channel_id=1, source_target_pairs={{0,2},{1,3},{2,0},{3,1},{4,6},{5,7},{6,4},{7,5},{8,10},{9,11},{10,... | collective-permute-start | bytes 56 | tf_op jit(solution)/shard_map/ppermute | solution.py:223
  6.4 0.0 collective-permute-start.2
  6.4 1.0 %dynamic-slice_bitcast_fusion = f32[2,128,256]{2,1,0:T(8,128)S(1)} fusion(f32[1,2,256,256]{3,2,1,0:T(8,128)} %refs_8_.1, s32[]{:T(128)S(6)} %select_n.28), kind=kLoop, calls=%fused_computation.2 | loop fusion | bytes 524292 | tf_op jit(solution)/shard_map/dynamic_slice | solution.py:234
  7.4 0.0 copy-done.1
  7.4 0.0 copy-start.3
  7.4 0.1 fusion
  7.5 0.0 copy-start.4
  7.5 1.8 %collective-permute-start.3 = (f32[3,128,256]{2,1,0:T(8,128)S(1)}, f32[3,128,256]{2,1,0:T(8,128)S(1)}, u32[]{:S(2)}, u32[]{:S(2)}) collective-permute-start(f32[3,128,256]{2,1,0:T(8,128)S(1)} %pad_maximum_fusion), channel_id=1, source_target_pairs={{0,8},{8,0},{16,24},{24,16},{1,9},{9,1},{17,25},{25,17},{2,10},{10... | collective-permute-start | bytes 1179656 | tf_op jit(solution)/shard_map/ppermute | solution.py:217
  9.3 1.5 %collective-permute-start.5 = (f32[3,128,256]{2,1,0:T(8,128)S(1)}, f32[3,128,256]{2,1,0:T(8,128)S(1)}, u32[]{:S(2)}, u32[]{:S(2)}) collective-permute-start(f32[3,128,256]{2,1,0:T(8,128)S(1)} %pad_maximum_fusion), channel_id=1, source_target_pairs={{0,16},{8,24},{16,0},{24,8},{1,17},{9,25},{17,1},{25,9},{2,18},{10... | collective-permute-start | bytes 1179656 | tf_op jit(solution)/shard_map/ppermute | solution.py:217
  10.8 0.0 copy-done.4
  10.8 0.1 iota_compare_fusion.1
  10.9 0.0 copy-done.3
  10.9 0.0 copy-start.2
  10.9 6.9 %collective-permute-done.3.refs_3_.refs_2_ = f32[3,128,256]{2,1,0:T(8,128)S(1)} collective-permute-done((f32[3,128,256]{2,1,0:T(8,128)S(1)}, f32[3,128,256]{2,1,0:T(8,128)S(1)}, u32[]{:S(2)}, u32[]{:S(2)}) %collective-permute-start.3) | collective-permute-done | bytes 393248 | tf_op jit(solution)/shard_map/ppermute | solution.py:217
  17.9 0.6 collective-permute-start.9
  18.5 0.6 collective-permute-done.5.refs_4_.refs_9_
  19.1 2.9 %collective-permute-start.10 = (f32[2,2,128,128]{3,2,1,0:T(8,128)S(1)}, f32[2,2,128,128]{3,2,1,0:T(8,128)S(1)}, u32[]{:S(2)}, u32[]{:S(2)}) collective-permute-start(f32[2,2,128,128]{3,2,1,0:T(8,128)S(1)} %bitcast_select_fusion.refs_1_), channel_id=1, source_target_pairs={{0,2},{1,3},{2,0},{3,1},{4,6},{5,7},{6,4},{7,5},{8,10},{9,11},{10,... | collective-permute-start | bytes 786440 | tf_op jit(solution)/shard_map/ppermute | solution.py:223
  22.0 0.0 copy-start
  22.1 0.0 collective-permute-done.refs_2_
  22.1 0.7 %collective-permute-start.11 = (f32[2,2,128,128]{3,2,1,0:T(8,128)S(1)}, f32[2,2,128,128]{3,2,1,0:T(8,128)S(1)}, u32[]{:S(2)}, u32[]{:S(2)}) collective-permute-start(f32[2,2,128,128]{3,2,1,0:T(8,128)S(1)} %bitcast_select_fusion.refs_1_), channel_id=1, source_target_pairs={{0,3},{1,2},{2,1},{3,0},{4,7},{5,6},{6,5},{7,4},{8,11},{9,10},{10,... | collective-permute-start | bytes 786440 | tf_op jit(solution)/shard_map/ppermute | solution.py:223
  22.8 0.0 collective-permute-done.1.refs_3_
  22.8 1.1 %collective-permute-start.7 = (f32[3,128,256]{2,1,0:T(8,128)S(1)}, f32[3,128,256]{2,1,0:T(8,128)S(1)}, u32[]{:S(2)}, u32[]{:S(2)}) collective-permute-start(f32[3,128,256]{2,1,0:T(8,128)S(1)} %broadcast_select_fusion), channel_id=1, source_target_pairs={{0,8},{8,0},{16,24},{24,16},{4,20},{12,28},{20,4},{28,12},{1,9},{9... | collective-permute-start | bytes 1179656 | tf_op jit(solution)/shard_map/ppermute | solution.py:274
  23.9 0.0 collective-permute-done.2.refs_4_
  23.9 0.0 collective-permute-start.4
  23.9 0.0 copy-done.2
  23.9 4.7 %shard_map.73 = (bf16[256,1024]{1,0:T(8,128)(2,1)S(1)}, f32[4]{0:T(128)S(1)}) custom-call(s32[8]{0:T(128)S(1)} %copy-done.2, f32[2,2]{1,0:T(2,128)S(1)} %pad_maximum_fusion.1.refs_1_, f32[2,2]{1,0:T(2,128)S(1)} %collective-permute-done.refs_2_, f32[2,2]{1,0:T(2,128)S(1)} %collective-permute-done.1.refs_3_, f32[2,2]{1,0:T(2,128)S(1)} %collective-permute-done.2.refs_4_, ...), custom_call_target="tpu_custom_call" | custom-call | flops 6000000000 | bytes 6000000 | tf_op jit(solution)/shard_map/pallas_call | solution.py:269
  28.6 0.0 collective-permute-done.4.refs_4_.refs_3_
  28.6 0.6 collective-permute-start.6
  29.2 1.4 %collective-permute-done.7.refs_11_ = f32[3,128,256]{2,1,0:T(8,128)S(1)} collective-permute-done((f32[3,128,256]{2,1,0:T(8,128)S(1)}, f32[3,128,256]{2,1,0:T(8,128)S(1)}, u32[]{:S(2)}, u32[]{:S(2)}) %collective-permute-start.7) | collective-permute-done | bytes 393248 | tf_op jit(solution)/shard_map/ppermute | solution.py:274
  30.6 0.0 collective-permute-start.8
  30.6 0.0 copy-done
  30.6 5.3 %shard_map.74 = (bf16[256,1024]{1,0:T(8,128)(2,1)S(1)}, bf16[256,1024]{1,0:T(8,128)(2,1)S(1)}, bf16[256,1024]{1,0:T(8,128)(2,1)S(1)}) custom-call(f32[4]{0:T(128)S(1)} %get-tuple-element.31.refs_0_, bf16[256,1024]{1,0:T(8,128)(2,1)S(1)} %get-tuple-element.32.refs_1_, f32[1,2,256,256]{3,2,1,0:T(8,128)S(1)} %copy-done, ...), custom_call_target="tpu_custom_call" | custom-call | flops 8000000000 | bytes 8000000 | tf_op jit(solution)/shard_map/pallas_call | solution.py:314
  35.9 0.0 collective-permute-done.6.refs_5_.refs_10_
  35.9 6.1 %shard_map.75 = (bf16[256,1024]{1,0:T(8,128)(2,1)S(1)}, bf16[256,1024]{1,0:T(8,128)(2,1)S(1)}, bf16[256,1024]{1,0:T(8,128)(2,1)S(1)}, f32[4]{0:T(128)S(1)}) custom-call(f32[4]{0:T(128)S(1)} %get-tuple-element.31.refs_0_, bf16[256,1024]{1,0:T(8,128)(2,1)S(1)} %get-tuple-element.33.refs_1_.refs_2_, f32[3,128,256]{2,1,0:T(8,128)S(1)} %collective-permute-done.3.refs_3_.refs_2_, ...), custom_call_target="tpu_custom_call" | custom-call | flops 8000000000 | bytes 8000000 | tf_op jit(solution)/shard_map/pallas_call | solution.py:347
  42.0 0.0 collective-permute-done.9.refs_2_
  42.0 0.0 collective-permute-done.10.refs_3_
  42.0 0.0 collective-permute-done.11.refs_4_
  42.0 1.1 %shard_map.77.mine = f32[4,128,128]{2,1,0:T(8,128)S(1)} custom-call(s32[8]{0:T(128)S(1)} %copy-done.2, f32[2,2,128,128]{3,2,1,0:T(8,128)S(1)} %bitcast_select_fusion.refs_1_, f32[2,2,128,128]{3,2,1,0:T(8,128)S(1)} %collective-permute-done.9.refs_2_, f32[2,2,128,128]{3,2,1,0:T(8,128)S(1)} %collective-permute-done.10.refs_3_, ...), custom_call_target="tpu_custom_call" | custom-call | flops 2000000000 | bytes 2000000 | tf_op jit(solution)/shard_map/pallas_call | solution.py:381
  43.1 0.6 collective-permute-start.12
  43.7 1.2 %collective-permute-done.12.other = f32[4,128,128]{2,1,0:T(8,128)S(1)} collective-permute-done((f32[4,128,128]{2,1,0:T(8,128)S(1)}, f32[4,128,128]{2,1,0:T(8,128)S(1)}, u32[]{:S(2)}, u32[]{:S(2)}) %collective-permute-start.12) | collective-permute-done | bytes 262176 | tf_op jit(solution)/shard_map/ppermute | solution.py:220
  44.9 0.1 collective-permute-start.13
  45.0 2.6 %collective-permute-start.14 = (f32[256,128]{1,0:T(8,128)S(1)}, f32[256,128]{1,0:T(8,128)S(1)}, u32[]{:S(2)}, u32[]{:S(2)}) collective-permute-start(f32[256,128]{1,0:T(8,128)S(1)} %get-tuple-element.49), channel_id=1, source_target_pairs={{0,16},{8,24},{16,0},{24,8},{1,17},{9,25},{17,1},{25,9},{2,18},{10... | collective-permute-start | bytes 393224 | tf_op jit(solution)/shard_map/ppermute | solution.py:217
  47.6 0.8 %collective-permute-start.15 = (f32[256,128]{1,0:T(8,128)S(1)}, f32[256,128]{1,0:T(8,128)S(1)}, u32[]{:S(2)}, u32[]{:S(2)}) collective-permute-start(f32[256,128]{1,0:T(8,128)S(1)} %get-tuple-element.50), channel_id=1, source_target_pairs={{0,24},{8,16},{16,8},{24,0},{1,25},{9,17},{17,9},{25,1},{2,26},{10... | collective-permute-start | bytes 393224 | tf_op jit(solution)/shard_map/ppermute | solution.py:217
  48.4 0.0 collective-permute-done.8.refs_12_
  48.5 5.8 %shard_map.76 = (bf16[256,1024]{1,0:T(8,128)(2,1)S(1)}, bf16[256,1024]{1,0:T(8,128)(2,1)S(1)}, bf16[256,1024]{1,0:T(8,128)(2,1)S(1)}, bf16[256,1024]{1,0:T(8,128...) custom-call(f32[4]{0:T(128)S(1)} %get-tuple-element.31.refs_0_, ...), custom_call_target="tpu_custom_call" | custom-call | flops 10000000000 | bytes 10000000 | tf_op jit(solution)/shard_map/pallas_call | solution.py:460
  54.3 0.0 collective-permute-done.13.refs_14_
  54.3 0.0 collective-permute-done.14.refs_15_
  54.3 0.0 collective-permute-done.15.refs_16_
  54.3 3.7 %shard_map.79 = (f32[4,128,128]{2,1,0:T(8,128)S(1)}, f32[4,128,128]{2,1,0:T(8,128)S(1)}) custom-call(f32[4]{0:T(128)S(1)} %get-tuple-element.31.refs_0_, bf16[256,1024]{1,0:T(8,128)(2,1)S(1)} %get-tuple-element.32.refs_1_, bf16[256,1024]{1,0:T(8,128)(2,1)S(1)} %get-tuple-element.33.refs_1_.refs_2_, bf16[256,1024]{1,0:T(8,128)(2,1)S(1)} %get-tuple-element.34.refs_3_, ...), custom_call_target="tpu_custom_call" | custom-call | flops 8000000000 | bytes 8000000 | tf_op jit(solution)/shard_map/pallas_call | solution.py:504
  58.0 0.1 collective-permute-start.16
  58.1 1.5 %collective-permute-done.16.send = f32[4,128,128]{2,1,0:T(8,128)S(1)} collective-permute-done((f32[4,128,128]{2,1,0:T(8,128)S(1)}, f32[4,128,128]{2,1,0:T(8,128)S(1)}, u32[]{:S(2)}, u32[]{:S(2)}) %collective-permute-start.16) | collective-permute-done | bytes 262176 | tf_op jit(solution)/shard_map/ppermute | solution.py:220
  59.6 3.6 %collective-permute-start.17 = (f32[128,128]{1,0:T(8,128)S(1)}, f32[128,128]{1,0:T(8,128)S(1)}, u32[]{:S(2)}, u32[]{:S(2)}) collective-permute-start(f32[128,128]{1,0:T(8,128)S(1)} %get-tuple-element.54), channel_id=1, source_target_pairs={{0,8},{8,0},{16,24},{24,16},{1,9},{9,1},{17,25},{25,17},{2,10},{10... | collective-permute-start | bytes 196616 | tf_op jit(solution)/shard_map/ppermute | solution.py:217
  63.2 0.2 collective-permute-start.18
  63.4 1.4 %collective-permute-start.19 = (f32[128,128]{1,0:T(8,128)S(1)}, f32[128,128]{1,0:T(8,128)S(1)}, u32[]{:S(2)}, u32[]{:S(2)}) collective-permute-start(f32[128,128]{1,0:T(8,128)S(1)} %get-tuple-element.56), channel_id=1, source_target_pairs={{0,24},{8,16},{16,8},{24,0},{1,25},{9,17},{17,9},{25,1},{2,26},{10... | collective-permute-start | bytes 196616 | tf_op jit(solution)/shard_map/ppermute | solution.py:217
  64.8 0.8 %collective-permute-done.17.refs_1_ = f32[128,128]{1,0:T(8,128)S(1)} collective-permute-done((f32[128,128]{1,0:T(8,128)S(1)}, f32[128,128]{1,0:T(8,128)S(1)}, u32[]{:S(2)}, u32[]{:S(2)}) %collective-permute-start.17) | collective-permute-done | bytes 65568 | tf_op jit(solution)/shard_map/ppermute | solution.py:217
  65.6 3.2 %collective-permute-done.18.refs_2_ = f32[128,128]{1,0:T(8,128)S(1)} collective-permute-done((f32[128,128]{1,0:T(8,128)S(1)}, f32[128,128]{1,0:T(8,128)S(1)}, u32[]{:S(2)}, u32[]{:S(2)}) %collective-permute-start.18) | collective-permute-done | bytes 65568 | tf_op jit(solution)/shard_map/ppermute | solution.py:217
  68.9 0.0 collective-permute-done.19.refs_3_
  68.9 0.8 %shard_map.81 = f32[2,1,2,128,128]{4,3,2,1,0:T(8,128)} custom-call(f32[128,128]{1,0:T(8,128)S(1)} %get-tuple-element.53.refs_0_, f32[128,128]{1,0:T(8,128)S(1)} %collective-permute-done.17.refs_1_, f32[128,128]{1,0:T(8,128)S(1)} %collective-permute-done.18.refs_2_, f32[128,128]{1,0:T(8,128)S(1)} %collective-permute-done.19.refs_3_), custom_call_target="tpu_custom_call" | custom-call | tf_op jit(solution)/shard_map/pallas_call | solution.py:545
  (6 shorter events, 0.2 us)
Async XLA Ops:
  0.0 7.4 %copy-start.1 = (f32[1,2,256,256]{3,2,1,0:T(8,128)S(1)}, f32[1,2,256,256]{3,2,1,0:T(8,128)}, u32[]{:S(2)}) copy-start(f32[1,2,256,256]{3,2,1,0:T(8,128)} %refs_5_.1) | copy-start | bytes 1572868
  0.7 21.3 %collective-permute-start = (f32[2,2]{1,0:T(2,128)S(1)}, f32[2,2]{1,0:T(2,128)S(1)}, u32[]{:S(2)}, u32[]{:S(2)}) collective-permute-start(f32[2,2]{1,0:T(2,128)S(1)} %pad_maximum_fusion.1.refs_1_), channel_id=1, source_target_pairs={{0,1},{1,0},{2,3},{3,2},{4,5},{5,4},{6,7},{7,6},{8,9},{9,8},{10,11... | collective-permute-start | bytes 56 | tf_op jit(solution)/shard_map/ppermute | solution.py:223
  3.8 19.0 %collective-permute-start.1 = (f32[2,2]{1,0:T(2,128)S(1)}, f32[2,2]{1,0:T(2,128)S(1)}, u32[]{:S(2)}, u32[]{:S(2)}) collective-permute-start(f32[2,2]{1,0:T(2,128)S(1)} %pad_maximum_fusion.1.refs_1_), channel_id=1, source_target_pairs={{0,2},{1,3},{2,0},{3,1},{4,6},{5,7},{6,4},{7,5},{8,10},{9,11},{10,... | collective-permute-start | bytes 56 | tf_op jit(solution)/shard_map/ppermute | solution.py:223
  6.4 17.5 %collective-permute-start.2 = (f32[2,2]{1,0:T(2,128)S(1)}, f32[2,2]{1,0:T(2,128)S(1)}, u32[]{:S(2)}, u32[]{:S(2)}) collective-permute-start(f32[2,2]{1,0:T(2,128)S(1)} %pad_maximum_fusion.1.refs_1_), channel_id=1, source_target_pairs={{0,3},{1,2},{2,1},{3,0},{4,7},{5,6},{6,5},{7,4},{8,11},{9,10},{10,... | collective-permute-start | bytes 56 | tf_op jit(solution)/shard_map/ppermute | solution.py:223
  7.4 3.5 %copy-start.3 = (f32[2,1,2,256,128]{4,3,2,1,0:T(8,128)S(1)}, f32[2,1,2,256,128]{4,3,2,1,0:T(8,128)}, u32[]{:S(2)}) copy-start(f32[2,1,2,256,128]{4,3,2,1,0:T(8,128)} %param.9) | copy-start | bytes 1572868
  7.5 3.3 %copy-start.4 = (s32[2]{0:T(128)S(1)}, s32[2]{0:T(128)}, u32[]{:S(2)}) copy-start(s32[2]{0:T(128)} %param.10) | copy-start | bytes 28
  7.5 10.4 %collective-permute-start.3 = (f32[3,128,256]{2,1,0:T(8,128)S(1)}, f32[3,128,256]{2,1,0:T(8,128)S(1)}, u32[]{:S(2)}, u32[]{:S(2)}) collective-permute-start(f32[3,128,256]{2,1,0:T(8,128)S(1)} %pad_maximum_fusion), channel_id=1, source_target_pairs={{0,8},{8,0},{16,24},{24,16},{1,9},{9,1},{17,25},{25,17},{2,10},{10... | collective-permute-start | bytes 1179656 | tf_op jit(solution)/shard_map/ppermute | solution.py:217
  9.3 9.8 %collective-permute-start.5 = (f32[3,128,256]{2,1,0:T(8,128)S(1)}, f32[3,128,256]{2,1,0:T(8,128)S(1)}, u32[]{:S(2)}, u32[]{:S(2)}) collective-permute-start(f32[3,128,256]{2,1,0:T(8,128)S(1)} %pad_maximum_fusion), channel_id=1, source_target_pairs={{0,16},{8,24},{16,0},{24,8},{1,17},{9,25},{17,1},{25,9},{2,18},{10... | collective-permute-start | bytes 1179656 | tf_op jit(solution)/shard_map/ppermute | solution.py:217
  10.9 13.0 %copy-start.2 = (s32[8]{0:T(128)S(1)}, s32[8]{0:T(128)}, u32[]{:S(2)}) copy-start(s32[8]{0:T(128)} %refs_0_.3) | copy-start | bytes 100
  17.9 24.1 %collective-permute-start.9 = (f32[2,2,128,128]{3,2,1,0:T(8,128)S(1)}, f32[2,2,128,128]{3,2,1,0:T(8,128)S(1)}, u32[]{:S(2)}, u32[]{:S(2)}) collective-permute-start(f32[2,2,128,128]{3,2,1,0:T(8,128)S(1)} %bitcast_select_fusion.refs_1_), channel_id=1, source_target_pairs={{0,1},{1,0},{2,3},{3,2},{4,5},{5,4},{6,7},{7,6},{8,9},{9,8},{10,11... | collective-permute-start | bytes 786440 | tf_op jit(solution)/shard_map/ppermute | solution.py:223
  19.1 22.9 %collective-permute-start.10 = (f32[2,2,128,128]{3,2,1,0:T(8,128)S(1)}, f32[2,2,128,128]{3,2,1,0:T(8,128)S(1)}, u32[]{:S(2)}, u32[]{:S(2)}) collective-permute-start(f32[2,2,128,128]{3,2,1,0:T(8,128)S(1)} %bitcast_select_fusion.refs_1_), channel_id=1, source_target_pairs={{0,2},{1,3},{2,0},{3,1},{4,6},{5,7},{6,4},{7,5},{8,10},{9,11},{10,... | collective-permute-start | bytes 786440 | tf_op jit(solution)/shard_map/ppermute | solution.py:223
  22.0 8.5 %copy-start = (f32[1,2,256,256]{3,2,1,0:T(8,128)S(1)}, f32[1,2,256,256]{3,2,1,0:T(8,128)}, u32[]{:S(2)}) copy-start(f32[1,2,256,256]{3,2,1,0:T(8,128)} %refs_8_.1) | copy-start | bytes 1572868
  22.1 20.0 %collective-permute-start.11 = (f32[2,2,128,128]{3,2,1,0:T(8,128)S(1)}, f32[2,2,128,128]{3,2,1,0:T(8,128)S(1)}, u32[]{:S(2)}, u32[]{:S(2)}) collective-permute-start(f32[2,2,128,128]{3,2,1,0:T(8,128)S(1)} %bitcast_select_fusion.refs_1_), channel_id=1, source_target_pairs={{0,3},{1,2},{2,1},{3,0},{4,7},{5,6},{6,5},{7,4},{8,11},{9,10},{10,... | collective-permute-start | bytes 786440 | tf_op jit(solution)/shard_map/ppermute | solution.py:223
  22.8 7.8 %collective-permute-start.7 = (f32[3,128,256]{2,1,0:T(8,128)S(1)}, f32[3,128,256]{2,1,0:T(8,128)S(1)}, u32[]{:S(2)}, u32[]{:S(2)}) collective-permute-start(f32[3,128,256]{2,1,0:T(8,128)S(1)} %broadcast_select_fusion), channel_id=1, source_target_pairs={{0,8},{8,0},{16,24},{24,16},{4,20},{12,28},{20,4},{28,12},{1,9},{9... | collective-permute-start | bytes 1179656 | tf_op jit(solution)/shard_map/ppermute | solution.py:274
  23.9 4.7 %collective-permute-start.4 = (f32[3,128,256]{2,1,0:T(8,128)S(1)}, f32[3,128,256]{2,1,0:T(8,128)S(1)}, u32[]{:S(2)}, u32[]{:S(2)}) collective-permute-start(f32[3,128,256]{2,1,0:T(8,128)S(1)} %collective-permute-done.3.refs_3_.refs_2_), channel_id=1, source_target_pairs={{0,4},{4,0},{1,5},{5,1},{2,6},{6,2},{3,7},{7,3},{8,12},{12,8},{9,1... | collective-permute-start | bytes 1179656 | tf_op jit(solution)/shard_map/ppermute | solution.py:220
  28.6 7.3 %collective-permute-start.6 = (f32[3,128,256]{2,1,0:T(8,128)S(1)}, f32[3,128,256]{2,1,0:T(8,128)S(1)}, u32[]{:S(2)}, u32[]{:S(2)}) collective-permute-start(f32[3,128,256]{2,1,0:T(8,128)S(1)} %collective-permute-done.5.refs_4_.refs_9_), channel_id=1, source_target_pairs={{0,4},{4,0},{1,5},{5,1},{2,6},{6,2},{3,7},{7,3},{8,12},{12,8},{9,1... | collective-permute-start | bytes 1179656 | tf_op jit(solution)/shard_map/ppermute | solution.py:220
  30.6 17.9 %collective-permute-start.8 = (f32[3,128,256]{2,1,0:T(8,128)S(1)}, f32[3,128,256]{2,1,0:T(8,128)S(1)}, u32[]{:S(2)}, u32[]{:S(2)}) collective-permute-start(f32[3,128,256]{2,1,0:T(8,128)S(1)} %collective-permute-done.7.refs_11_), channel_id=1, source_target_pairs={{0,4},{4,0},{1,5},{5,1},{2,6},{6,2},{3,7},{7,3},{8,12},{12,8},{9,1... | collective-permute-start | bytes 1179656 | tf_op jit(solution)/shard_map/ppermute | solution.py:220
  43.1 1.7 %collective-permute-start.12 = (f32[4,128,128]{2,1,0:T(8,128)S(1)}, f32[4,128,128]{2,1,0:T(8,128)S(1)}, u32[]{:S(2)}, u32[]{:S(2)}) collective-permute-start(f32[4,128,128]{2,1,0:T(8,128)S(1)} %shard_map.77.mine), channel_id=1, source_target_pairs={{0,4},{4,0},{1,5},{5,1},{2,6},{6,2},{3,7},{7,3},{8,12},{12,8},{9,1... | collective-permute-start | bytes 786440 | tf_op jit(solution)/shard_map/ppermute | solution.py:220
  44.9 9.4 %collective-permute-start.13 = (f32[256,128]{1,0:T(8,128)S(1)}, f32[256,128]{1,0:T(8,128)S(1)}, u32[]{:S(2)}, u32[]{:S(2)}) collective-permute-start(f32[256,128]{1,0:T(8,128)S(1)} %get-tuple-element.48), channel_id=1, source_target_pairs={{0,8},{8,0},{16,24},{24,16},{1,9},{9,1},{17,25},{25,17},{2,10},{10... | collective-permute-start | bytes 393224 | tf_op jit(solution)/shard_map/ppermute | solution.py:217
  45.0 9.3 %collective-permute-start.14 = (f32[256,128]{1,0:T(8,128)S(1)}, f32[256,128]{1,0:T(8,128)S(1)}, u32[]{:S(2)}, u32[]{:S(2)}) collective-permute-start(f32[256,128]{1,0:T(8,128)S(1)} %get-tuple-element.49), channel_id=1, source_target_pairs={{0,16},{8,24},{16,0},{24,8},{1,17},{9,25},{17,1},{25,9},{2,18},{10... | collective-permute-start | bytes 393224 | tf_op jit(solution)/shard_map/ppermute | solution.py:217
  47.6 6.7 %collective-permute-start.15 = (f32[256,128]{1,0:T(8,128)S(1)}, f32[256,128]{1,0:T(8,128)S(1)}, u32[]{:S(2)}, u32[]{:S(2)}) collective-permute-start(f32[256,128]{1,0:T(8,128)S(1)} %get-tuple-element.50), channel_id=1, source_target_pairs={{0,24},{8,16},{16,8},{24,0},{1,25},{9,17},{17,9},{25,1},{2,26},{10... | collective-permute-start | bytes 393224 | tf_op jit(solution)/shard_map/ppermute | solution.py:217
  58.0 1.6 %collective-permute-start.16 = (f32[4,128,128]{2,1,0:T(8,128)S(1)}, f32[4,128,128]{2,1,0:T(8,128)S(1)}, u32[]{:S(2)}, u32[]{:S(2)}) collective-permute-start(f32[4,128,128]{2,1,0:T(8,128)S(1)} %get-tuple-element.52), channel_id=1, source_target_pairs={{0,4},{4,0},{1,5},{5,1},{2,6},{6,2},{3,7},{7,3},{8,12},{12,8},{9,1... | collective-permute-start | bytes 786440 | tf_op jit(solution)/shard_map/ppermute | solution.py:220
  59.6 6.0 %collective-permute-start.17 = (f32[128,128]{1,0:T(8,128)S(1)}, f32[128,128]{1,0:T(8,128)S(1)}, u32[]{:S(2)}, u32[]{:S(2)}) collective-permute-start(f32[128,128]{1,0:T(8,128)S(1)} %get-tuple-element.54), channel_id=1, source_target_pairs={{0,8},{8,0},{16,24},{24,16},{1,9},{9,1},{17,25},{25,17},{2,10},{10... | collective-permute-start | bytes 196616 | tf_op jit(solution)/shard_map/ppermute | solution.py:217
  63.2 5.6 %collective-permute-start.18 = (f32[128,128]{1,0:T(8,128)S(1)}, f32[128,128]{1,0:T(8,128)S(1)}, u32[]{:S(2)}, u32[]{:S(2)}) collective-permute-start(f32[128,128]{1,0:T(8,128)S(1)} %get-tuple-element.55), channel_id=1, source_target_pairs={{0,16},{8,24},{16,0},{24,8},{1,17},{9,25},{17,1},{25,9},{2,18},{10... | collective-permute-start | bytes 196616 | tf_op jit(solution)/shard_map/ppermute | solution.py:217
  63.4 5.5 %collective-permute-start.19 = (f32[128,128]{1,0:T(8,128)S(1)}, f32[128,128]{1,0:T(8,128)S(1)}, u32[]{:S(2)}, u32[]{:S(2)}) collective-permute-start(f32[128,128]{1,0:T(8,128)S(1)} %get-tuple-element.56), channel_id=1, source_target_pairs={{0,24},{8,16},{16,8},{24,0},{1,25},{9,17},{17,9},{25,1},{2,26},{10... | collective-permute-start | bytes 196616 | tf_op jit(solution)/shard_map/ppermute | solution.py:217

commit v4 on v3

--- a/solution.py
+++ b/solution.py
@@ -29,11 +29,6 @@
     return jnp.concatenate([high, low], 1)
 
 
-def left_triple(pair):
-    half = pair.shape[1] // 2
-    return jnp.concatenate([pair, pair[:, :half]], 1)
-
-
 def embed(re, im):
     return jnp.concatenate([jnp.concatenate([re, im], 1), jnp.concatenate([-im, re], 1)], 0)
 
@@ -43,6 +38,25 @@
     im_high, im_low = hi_lo(im)
     high = embed(re_high, im_high)
     return jnp.concatenate([high, high, embed(re_low, im_low)], 0)
+
+
+def whole(pair):
+    half = pair.shape[1] // 2
+    return pair[:, :half].astype(F32) + pair[:, half:].astype(F32)
+
+
+def product(pair, right):
+    n = right.shape[0]
+    left = whole(pair)
+
+    def real(left_high, left_low, value):
+        high, low = hi_lo(value)
+        return dot(left_high, high) + dot(left_low, high) + dot(left_high, low)
+
+    first = real(pair[:, :n], pair[:, 2 * n : 3 * n], right[:, :n])
+    second = real(pair[:, n : 2 * n], pair[:, 3 * n :], right[:, n:])
+    third = real(*hi_lo(left[:, :n] + left[:, n:]), right[:, :n] + right[:, n:])
+    return jnp.concatenate([first - second, third - first - second], 1)
 
 
 def times_i(value):
@@ -284,11 +298,11 @@
         near = [rows_of(x_dir, x_swp, k, p) for k in range(3)]
         even = lax.rem(scal[1], 2) == 0
         re, im, adj_re, adj_im = oriented(even, (own_c[0, 0], own_c[0, 1]), (near[1], near[2]))
-        solved = dot(left_triple(x_own[...]), embed_triple(re, im))
+        solved = product(x_own[...], jnp.concatenate([re, im], 1))
         w_out[...] = packed_pair(solved)
         left = packed_pair(jnp.concatenate([adj_re, adj_im], 1))
         l_out[...] = left
-        update = dot(left_triple(left), embed_triple(solved[:, :n], solved[:, n:]))
+        update = product(left, solved)
         d_re, d_im = unpack_diag(near[0])
         eye = eye_of(n)
         x_out[...] = packed_pair(
@@ -315,14 +329,16 @@
 
     def third_body(*refs):
         scal, prm = position(), refs[0]
-        (x_near, x_dir, x_swp, y_dir, y_swp, x_out, w_out, l_out, later) = refs[1:10]
-        s_emb, x_ref, work, s_ref = refs[10:]
+        (x_own, x_near, l_near, own_c, x_dir, x_swp, y_dir, y_swp) = refs[1:9]
+        (x_out, w_out, l_out, ahead, later, s_emb, x_ref, work, s_ref) = refs[9:]
         for k in range(4):
             later[k] = prm[k]
         z_re, z_im = prm[0], prm[1]
         p = scal[2]
         even = lax.rem(scal[1], 2) == 0
         chain = lax.rem(scal[1], 2) == scal[1] // 2
+        odd_fork = jnp.logical_not(jnp.logical_or(chain, even))
+        even_fork = jnp.logical_and(jnp.logical_not(chain), even)
         d_re, d_im = unpack_diag(rows_of(y_dir, y_swp, 0, p))
         eye = eye_of(n)
         s_ref[...] = jnp.concatenate([z_re * eye - d_re, z_im * eye - d_im], 1)
@@ -334,25 +350,41 @@
                 [rows_of(x_dir, x_swp, k, p) for k in (1, 2)],
                 [rows_of(y_dir, y_swp, k, p) for k in (1, 2)],
             )
-            solved = dot(left_triple(x_near[...]), embed_triple(re, im))
+            solved = product(x_near[...], jnp.concatenate([re, im], 1))
             w_out[...] = packed_pair(solved)
             left = packed_pair(jnp.concatenate([adj_re, adj_im], 1))
             l_out[...] = left
-            s_ref[...] = s_ref[...] - dot(
-                left_triple(left), embed_triple(solved[:, :n], solved[:, n:])
-            )
-
-        x_out[...] = packed_pair(invert(s_ref[:, :n], s_ref[:, n:], z_im, s_emb, x_ref, work))
-
-    x_side, w_mid, l_mid, later = pl.pallas_call(
+            s_ref[...] = s_ref[...] - product(left, solved)
+
+        @pl.when(odd_fork)
+        def _():
+            cross = product(x_own[...], jnp.concatenate([own_c[0, 0], own_c[0, 1]], 1))
+            w_out[...] = packed_pair(cross)
+            l_out[...] = packed_pair(jnp.concatenate([own_c[0, 0].T, -own_c[0, 1].T], 1))
+            ahead[...] = product(l_near[...], cross)
+
+        x_pair = packed_pair(invert(s_ref[:, :n], s_ref[:, n:], z_im, s_emb, x_ref, work))
+        x_out[...] = x_pair
+
+        @pl.when(even_fork)
+        def _():
+            re, im = [rows_of(y_dir, y_swp, k, p) for k in (1, 2)]
+            solved = product(x_pair, jnp.concatenate([re, im], 1))
+            w_out[...] = packed_pair(solved)
+            left = packed_pair(jnp.concatenate([re.T, -im.T], 1))
+            l_out[...] = left
+            ahead[...] = product(left, solved)
+
+    wide_shape = jax.ShapeDtypeStruct((n, 2 * n), F32)
+    x_side, w_mid, l_mid, ahead, later = pl.pallas_call(
         third_body,
-        out_shape=[pair_shape] * 3 + [jax.ShapeDtypeStruct((4,), F32)],
-        in_specs=[smem] + [vmem] * 5,
-        out_specs=[vmem] * 3 + [smem],
+        out_shape=[pair_shape] * 3 + [wide_shape, jax.ShapeDtypeStruct((4,), F32)],
+        in_specs=[smem] + [vmem] * 8,
+        out_specs=[vmem] * 4 + [smem],
         scratch_shapes=scratch + [pltpu.VMEM((n, 2 * n), F32)],
         cost_estimate=lasting(8),
         compiler_params=grant,
-    )(prm, x_near, *from_x, *from_y)
+    )(prm, x_own, x_near, l_near, couplings, *from_x, *from_y)
 
     def route_body(*refs):
         scal, owner = position(), refs[0]
@@ -404,8 +436,8 @@
 
     def fourth_body(*refs):
         scal, prm = position(), refs[0]
-        (x_own, x_near, x_side, w_near, l_near, w_mid, l_mid, own_c, y_dir, y_swp, f_dir, f_swp) = refs[1:13]
-        (x_out, w_far, l_far, w_cross, l_cross, w_last, l_last, s_emb, x_ref, work, s_ref) = refs[13:]
+        (x_own, x_near, x_side, w_near, l_near, w_mid, l_mid, ahead, y_dir, y_swp, f_dir, f_swp) = refs[1:13]
+        (x_out, w_far, l_far, w_cross, l_cross, w_last, l_last, s_emb, x_ref, work, s_ref, fill) = refs[13:]
         z_re, z_im = prm[0], prm[1]
         p = scal[2]
         even = lax.rem(scal[1], 2) == 0
@@ -424,37 +456,48 @@
             w_far[...] = w_mid[...]
             l_far[...] = l_mid[...]
 
+        odd_fork = jnp.logical_not(jnp.logical_or(chain, even))
+        even_fork = jnp.logical_and(jnp.logical_not(chain), even)
+
+        @pl.when(odd_fork)
+        def _():
+            w_cross[...] = w_mid[...]
+            l_cross[...] = l_mid[...]
+            fill[...] = ahead[...]
+
+        @pl.when(even_fork)
+        def _():
+            cross = product(x_own[...], jnp.concatenate([far[1].T, -far[2].T], 1))
+            w_cross[...] = packed_pair(cross)
+            l_cross[...] = packed_pair(jnp.concatenate([far[1], far[2]], 1))
+            fill[...] = product(l_near[...], cross)
+
         @pl.when(jnp.logical_not(chain))
         def _():
-            odd = jnp.logical_not(even)
-            re, im, adj_re, adj_im = oriented(odd, (own_c[0, 0], own_c[0, 1]), (far[1], far[2]))
-            cross = dot(left_triple(x_own[...]), embed_triple(re, im))
-            w_cross[...] = packed_pair(cross)
-            left = packed_pair(jnp.concatenate([adj_re, adj_im], 1))
-            l_cross[...] = left
-            cross_emb = embed_triple(cross[:, :n], cross[:, n:])
-            fill = dot(left_triple(l_near[...]), cross_emb)
-            w_pair = w_near[...]
-            high, low = w_pair[:, : 2 * n], w_pair[:, 2 * n :]
-            near_high = embed(high[:, :n], high[:, n:])
-            near_emb = jnp.concatenate([near_high, near_high, embed(low[:, :n], low[:, n:])], 0)
-            both = dot(left_triple(left), jnp.concatenate([near_emb, cross_emb], 1))
-            back = packed_pair(both[:, : 2 * n])
+            back = packed_pair(product(l_cross[...], whole(w_near[...])))
             l_far[...] = back
-            solved = dot(left_triple(x_near[...]), embed_triple(fill[:, :n], fill[:, n:]))
+            solved = product(x_near[...], fill[...])
             w_far[...] = packed_pair(solved)
             s_ref[...] = (
-                s_ref[...]
-                - both[:, 2 * n :]
-                - dot(left_triple(back), embed_triple(solved[:, :n], solved[:, n:]))
+                s_ref[...] - product(l_cross[...], whole(w_cross[...])) - product(back, solved)
             )
 
-        re, im, adj_re, adj_im = oriented(even, side, (far[1], far[2]))
-        solved = dot(left_triple(x_side[...]), embed_triple(re, im))
-        w_last[...] = packed_pair(solved)
-        left = packed_pair(jnp.concatenate([adj_re, adj_im], 1))
-        l_last[...] = left
-        s_now = s_ref[...] - dot(left_triple(left), embed_triple(solved[:, :n], solved[:, n:]))
+        @pl.when(even_fork)
+        def _():
+            w_last[...] = w_mid[...]
+            l_last[...] = l_mid[...]
+            s_ref[...] = s_ref[...] - ahead[...]
+
+        @pl.when(jnp.logical_not(even_fork))
+        def _():
+            re, im, adj_re, adj_im = oriented(even, side, (far[1], far[2]))
+            solved = product(x_side[...], jnp.concatenate([re, im], 1))
+            w_last[...] = packed_pair(solved)
+            left = packed_pair(jnp.concatenate([adj_re, adj_im], 1))
+            l_last[...] = left
+            s_ref[...] = s_ref[...] - product(left, solved)
+
+        s_now = s_ref[...]
         x_out[...] = packed_pair(invert(s_now[:, :n], s_now[:, n:], z_im, s_emb, x_ref, work))
 
     x_far, w_far, l_far, w_cross, l_cross, w_last, l_last = pl.pallas_call(
@@ -462,10 +505,10 @@
         out_shape=[pair_shape] * 7,
         in_specs=[smem] + [vmem] * 12,
         out_specs=[vmem] * 7,
-        scratch_shapes=scratch + [pltpu.VMEM((n, 2 * n), F32)],
+        scratch_shapes=scratch + [pltpu.VMEM((n, 2 * n), F32)] * 2,
         cost_estimate=lasting(10),
         compiler_params=grant,
-    )(prm, x_own, x_near, x_side, w_near, l_near, w_mid, l_mid, couplings, *from_y, *from_far)
+    )(prm, x_own, x_near, x_side, w_near, l_near, w_mid, l_mid, ahead, *from_y, *from_far)
 
     def solve_body(*refs):
         scal, prm = position(), refs[0]

time: 69.9 us -> 68.6 us (0.981)
  starting transfers between devices: 24.2 us -> 23.1 us
    ppermute x8, starting transfers between devices: 12 us -> 10.9 us  [exchange(): lax.ppermute(value, 'slab', [(i, i ^ distance) for i in range(slab_count)])]
  transfers between devices with their start and end apart: 20 -> 20, of which waited for: 7 -> 8; matrix products, arithmetic and copies ran while one was open for 2% -> 2% of each run, Pallas kernels for 33% -> 33%
where the time goes in v4:
time: 68.6 us; the launch traced here: 68.5 us
  Pallas kernels  27.3 us (40%)
  starting transfers between devices  23.1 us (34%)
  waiting for transfers between devices  15.8 us (23%)
  local copies, waits for them, and re-layouts  1 us (1%)
  other arithmetic  1 us (1%)
    ppermute x8, waiting for transfers between devices, exchange(): lax.ppermute(value, 'slab', [(i, i ^ distance) for i in range(slab_count)])  11.7 us
    ppermute x8, starting transfers between devices, exchange(): lax.ppermute(value, 'slab', [(i, i ^ distance) for i in range(slab_count)])  10.9 us
    ppermute x6, starting transfers between devices, along_win(): lax.ppermute(value, 'win', [(i, i ^ shift) for i in range(win_count)])  9.87 us
    pallas_call x1, Pallas kernels, per_device(): pl.pallas_call(third_body, out_shape=[pair_shape] * 3 + [wide_shape, jax....  6.17 us
    pallas_call x1, Pallas kernels, per_device(): pl.pallas_call(fourth_body, out_shape=[pair_shape] * 7, in_specs=[smem] +...  5.58 us
    pallas_call x1, Pallas kernels, per_device(): x_near, w_near, l_near = second(prm, x_own, couplings, *from_x)  5.22 us
    pallas_call x1, Pallas kernels, per_device(): x_own, prm = first(*head, diag_blocks)  4.67 us
    pallas_call x1, Pallas kernels, per_device(): pl.pallas_call(solve_body, out_shape=[quad] * 2, in_specs=[smem] + [vmem]...  3.68 us
  transfers between devices with their start and end apart: 20, of which 8 were waited for; matrix products, arithmetic and copies ran while one was open for 2% of the time, Pallas kernels for 33%

profile of v4, /device:TPU:0, one launch (start us, length us, event | category | flops | bytes accessed | tf_op | source)
XLA Modules:
  0.0 68.5 jit_solution(6267394879478598941)
XLA Ops:
  0.0 0.0 copy-start.1
  0.0 0.7 %pad_maximum_fusion.1.refs_1_ = f32[2,2]{1,0:T(2,128)S(1)} fusion(f32[1,2]{1,0:T(1,128)} %bitcast.14, f32[1,2]{1,0:T(1,128)} %bitcast.15), kind=kLoop, calls=%fused_computation.8 | loop fusion | flops 4 | bytes 32 | tf_op jit(solution)/shard_map/stack | solution.py:239
  0.7 3.1 %collective-permute-start = (f32[2,2]{1,0:T(2,128)S(1)}, f32[2,2]{1,0:T(2,128)S(1)}, u32[]{:S(2)}, u32[]{:S(2)}) collective-permute-start(f32[2,2]{1,0:T(2,128)S(1)} %pad_maximum_fusion.1.refs_1_), channel_id=1, source_target_pairs={{0,1},{1,0},{2,3},{3,2},{4,5},{5,4},{6,7},{7,6},{8,9},{9,8},{10,11... | collective-permute-start | bytes 56 | tf_op jit(solution)/shard_map/ppermute | solution.py:237
  3.8 2.6 %collective-permute-start.1 = (f32[2,2]{1,0:T(2,128)S(1)}, f32[2,2]{1,0:T(2,128)S(1)}, u32[]{:S(2)}, u32[]{:S(2)}) collective-permute-start(f32[2,2]{1,0:T(2,128)S(1)} %pad_maximum_fusion.1.refs_1_), channel_id=1, source_target_pairs={{0,2},{1,3},{2,0},{3,1},{4,6},{5,7},{6,4},{7,5},{8,10},{9,11},{10,... | collective-permute-start | bytes 56 | tf_op jit(solution)/shard_map/ppermute | solution.py:237
  6.4 0.0 collective-permute-start.2
  6.4 1.0 %dynamic-slice_bitcast_fusion = f32[2,128,256]{2,1,0:T(8,128)S(1)} fusion(f32[1,2,256,256]{3,2,1,0:T(8,128)} %refs_4_.1, s32[]{:T(128)S(6)} %select_n.28), kind=kLoop, calls=%fused_computation.2 | loop fusion | bytes 524292 | tf_op jit(solution)/shard_map/dynamic_slice | solution.py:248
  7.4 0.0 copy-done.1
  7.4 0.0 copy-start.3
  7.4 0.1 fusion
  7.5 0.0 copy-start.4
  7.5 1.8 %collective-permute-start.3 = (f32[3,128,256]{2,1,0:T(8,128)S(1)}, f32[3,128,256]{2,1,0:T(8,128)S(1)}, u32[]{:S(2)}, u32[]{:S(2)}) collective-permute-start(f32[3,128,256]{2,1,0:T(8,128)S(1)} %pad_maximum_fusion), channel_id=1, source_target_pairs={{0,8},{8,0},{16,24},{24,16},{1,9},{9,1},{17,25},{25,17},{2,10},{10... | collective-permute-start | bytes 1179656 | tf_op jit(solution)/shard_map/ppermute | solution.py:231
  9.3 1.5 %collective-permute-start.5 = (f32[3,128,256]{2,1,0:T(8,128)S(1)}, f32[3,128,256]{2,1,0:T(8,128)S(1)}, u32[]{:S(2)}, u32[]{:S(2)}) collective-permute-start(f32[3,128,256]{2,1,0:T(8,128)S(1)} %pad_maximum_fusion), channel_id=1, source_target_pairs={{0,16},{8,24},{16,0},{24,8},{1,17},{9,25},{17,1},{25,9},{2,18},{10... | collective-permute-start | bytes 1179656 | tf_op jit(solution)/shard_map/ppermute | solution.py:231
  10.8 0.0 copy-done.4
  10.8 0.1 iota_compare_fusion.1
  10.9 0.0 copy-done.3
  10.9 0.0 copy-start.2
  10.9 6.9 %collective-permute-done.3.refs_3_.refs_5_ = f32[3,128,256]{2,1,0:T(8,128)S(1)} collective-permute-done((f32[3,128,256]{2,1,0:T(8,128)S(1)}, f32[3,128,256]{2,1,0:T(8,128)S(1)}, u32[]{:S(2)}, u32[]{:S(2)}) %collective-permute-start.3) | collective-permute-done | bytes 393248 | tf_op jit(solution)/shard_map/ppermute | solution.py:231
  17.9 0.6 collective-permute-start.9
  18.5 0.6 collective-permute-done.5.refs_7_.refs_9_
  19.1 2.9 %collective-permute-start.10 = (f32[2,2,128,128]{3,2,1,0:T(8,128)S(1)}, f32[2,2,128,128]{3,2,1,0:T(8,128)S(1)}, u32[]{:S(2)}, u32[]{:S(2)}) collective-permute-start(f32[2,2,128,128]{3,2,1,0:T(8,128)S(1)} %bitcast_select_fusion.refs_1_), channel_id=1, source_target_pairs={{0,2},{1,3},{2,0},{3,1},{4,6},{5,7},{6,4},{7,5},{8,10},{9,11},{10,... | collective-permute-start | bytes 786440 | tf_op jit(solution)/shard_map/ppermute | solution.py:237
  22.0 0.0 copy-start
  22.1 0.0 collective-permute-done.refs_2_
  22.1 0.7 %collective-permute-start.11 = (f32[2,2,128,128]{3,2,1,0:T(8,128)S(1)}, f32[2,2,128,128]{3,2,1,0:T(8,128)S(1)}, u32[]{:S(2)}, u32[]{:S(2)}) collective-permute-start(f32[2,2,128,128]{3,2,1,0:T(8,128)S(1)} %bitcast_select_fusion.refs_1_), channel_id=1, source_target_pairs={{0,3},{1,2},{2,1},{3,0},{4,7},{5,6},{6,5},{7,4},{8,11},{9,10},{10,... | collective-permute-start | bytes 786440 | tf_op jit(solution)/shard_map/ppermute | solution.py:237
  22.8 0.0 collective-permute-done.1.refs_3_
  22.8 1.1 %collective-permute-start.7 = (f32[3,128,256]{2,1,0:T(8,128)S(1)}, f32[3,128,256]{2,1,0:T(8,128)S(1)}, u32[]{:S(2)}, u32[]{:S(2)}) collective-permute-start(f32[3,128,256]{2,1,0:T(8,128)S(1)} %broadcast_select_fusion), channel_id=1, source_target_pairs={{0,8},{8,0},{16,24},{24,16},{4,20},{12,28},{20,4},{28,12},{1,9},{9... | collective-permute-start | bytes 1179656 | tf_op jit(solution)/shard_map/ppermute | solution.py:288
  23.9 0.0 collective-permute-done.2.refs_4_
  23.9 0.0 collective-permute-start.4
  23.9 0.0 copy-done.2
  23.9 4.7 %shard_map.73 = (bf16[256,1024]{1,0:T(8,128)(2,1)S(1)}, f32[4]{0:T(128)S(1)}) custom-call(s32[8]{0:T(128)S(1)} %copy-done.2, f32[2,2]{1,0:T(2,128)S(1)} %pad_maximum_fusion.1.refs_1_, f32[2,2]{1,0:T(2,128)S(1)} %collective-permute-done.refs_2_, f32[2,2]{1,0:T(2,128)S(1)} %collective-permute-done.1.refs_3_, f32[2,2]{1,0:T(2,128)S(1)} %collective-permute-done.2.refs_4_, ...), custom_call_target="tpu_custom_call" | custom-call | flops 6000000000 | bytes 6000000 | tf_op jit(solution)/shard_map/pallas_call | solution.py:283
  28.6 0.0 collective-permute-done.4.refs_4_.refs_6_
  28.6 0.6 collective-permute-start.6
  29.2 1.4 %collective-permute-done.7.refs_11_ = f32[3,128,256]{2,1,0:T(8,128)S(1)} collective-permute-done((f32[3,128,256]{2,1,0:T(8,128)S(1)}, f32[3,128,256]{2,1,0:T(8,128)S(1)}, u32[]{:S(2)}, u32[]{:S(2)}) %collective-permute-start.7) | collective-permute-done | bytes 393248 | tf_op jit(solution)/shard_map/ppermute | solution.py:288
  30.6 0.0 collective-permute-start.8
  30.6 0.0 copy-done
  30.6 5.2 %shard_map.74 = (bf16[256,1024]{1,0:T(8,128)(2,1)S(1)}, bf16[256,1024]{1,0:T(8,128)(2,1)S(1)}, bf16[256,1024]{1,0:T(8,128)(2,1)S(1)}) custom-call(f32[4]{0:T(128)S(1)} %get-tuple-element.32.refs_0_, bf16[256,1024]{1,0:T(8,128)(2,1)S(1)} %get-tuple-element.33.refs_1_, f32[1,2,256,256]{3,2,1,0:T(8,128)S(1)} %copy-done, ...), custom_call_target="tpu_custom_call" | custom-call | flops 8000000000 | bytes 8000000 | tf_op jit(solution)/shard_map/pallas_call | solution.py:328
  35.8 0.0 collective-permute-done.6.refs_8_.refs_10_
  35.8 6.2 %shard_map.75 = (bf16[256,1024]{1,0:T(8,128)(2,1)S(1)}, bf16[256,1024]{1,0:T(8,128)(2,1)S(1)}, bf16[256,1024]{1,0:T(8,128)(2,1)S(1)}, f32[256,512]{1,0:T(8,128)S(1)}, f32[4]{0:T(128)S(1)}) custom-call(f32[4]{0:T(128)S(1)} %get-tuple-element.32.refs_0_, bf16[256,1024]{1,0:T(8,128)(2,1)S(1)} %get-tuple-element.33.refs_1_, ...), custom_call_target="tpu_custom_call" | custom-call | flops 8000000000 | bytes 8000000 | tf_op jit(solution)/shard_map/pallas_call | solution.py:379
  42.0 0.0 collective-permute-done.9.refs_2_
  42.0 0.0 collective-permute-done.10.refs_3_
  42.0 0.0 collective-permute-done.11.refs_4_
  42.0 1.1 %shard_map.77.mine = f32[4,128,128]{2,1,0:T(8,128)S(1)} custom-call(s32[8]{0:T(128)S(1)} %copy-done.2, f32[2,2,128,128]{3,2,1,0:T(8,128)S(1)} %bitcast_select_fusion.refs_1_, f32[2,2,128,128]{3,2,1,0:T(8,128)S(1)} %collective-permute-done.9.refs_2_, f32[2,2,128,128]{3,2,1,0:T(8,128)S(1)} %collective-permute-done.10.refs_3_, ...), custom_call_target="tpu_custom_call" | custom-call | flops 2000000000 | bytes 2000000 | tf_op jit(solution)/shard_map/pallas_call | solution.py:413
  43.1 0.6 collective-permute-start.12
  43.7 1.2 %collective-permute-done.12.other = f32[4,128,128]{2,1,0:T(8,128)S(1)} collective-permute-done((f32[4,128,128]{2,1,0:T(8,128)S(1)}, f32[4,128,128]{2,1,0:T(8,128)S(1)}, u32[]{:S(2)}, u32[]{:S(2)}) %collective-permute-start.12) | collective-permute-done | bytes 262176 | tf_op jit(solution)/shard_map/ppermute | solution.py:234
  44.9 1.0 %collective-permute-start.13 = (f32[256,128]{1,0:T(8,128)S(1)}, f32[256,128]{1,0:T(8,128)S(1)}, u32[]{:S(2)}, u32[]{:S(2)}) collective-permute-start(f32[256,128]{1,0:T(8,128)S(1)} %get-tuple-element.50), channel_id=1, source_target_pairs={{0,8},{8,0},{16,24},{24,16},{1,9},{9,1},{17,25},{25,17},{2,10},{10... | collective-permute-start | bytes 393224 | tf_op jit(solution)/shard_map/ppermute | solution.py:231
  45.9 1.7 %collective-permute-start.14 = (f32[256,128]{1,0:T(8,128)S(1)}, f32[256,128]{1,0:T(8,128)S(1)}, u32[]{:S(2)}, u32[]{:S(2)}) collective-permute-start(f32[256,128]{1,0:T(8,128)S(1)} %get-tuple-element.51), channel_id=1, source_target_pairs={{0,16},{8,24},{16,0},{24,8},{1,17},{9,25},{17,1},{25,9},{2,18},{10... | collective-permute-start | bytes 393224 | tf_op jit(solution)/shard_map/ppermute | solution.py:231
  47.6 0.9 %collective-permute-start.15 = (f32[256,128]{1,0:T(8,128)S(1)}, f32[256,128]{1,0:T(8,128)S(1)}, u32[]{:S(2)}, u32[]{:S(2)}) collective-permute-start(f32[256,128]{1,0:T(8,128)S(1)} %get-tuple-element.52), channel_id=1, source_target_pairs={{0,24},{8,16},{16,8},{24,0},{1,25},{9,17},{17,9},{25,1},{2,26},{10... | collective-permute-start | bytes 393224 | tf_op jit(solution)/shard_map/ppermute | solution.py:231
  48.5 0.0 collective-permute-done.8.refs_12_
  48.5 5.6 %shard_map.76 = (bf16[256,1024]{1,0:T(8,128)(2,1)S(1)}, bf16[256,1024]{1,0:T(8,128)(2,1)S(1)}, bf16[256,1024]{1,0:T(8,128)(2,1)S(1)}, bf16[256,1024]{1,0:T(8,128...) custom-call(f32[4]{0:T(128)S(1)} %get-tuple-element.32.refs_0_, ...), custom_call_target="tpu_custom_call" | custom-call | flops 10000000000 | bytes 10000000 | tf_op jit(solution)/shard_map/pallas_call | solution.py:503
  54.0 0.0 collective-permute-done.13.refs_14_
  54.1 0.1 collective-permute-done.14.refs_15_
  54.2 0.0 collective-permute-done.15.refs_16_
  54.2 3.7 %shard_map.79 = (f32[4,128,128]{2,1,0:T(8,128)S(1)}, f32[4,128,128]{2,1,0:T(8,128)S(1)}) custom-call(f32[4]{0:T(128)S(1)} %get-tuple-element.32.refs_0_, bf16[256,1024]{1,0:T(8,128)(2,1)S(1)} %get-tuple-element.33.refs_1_, bf16[256,1024]{1,0:T(8,128)(2,1)S(1)} %get-tuple-element.34.refs_2_, bf16[256,1024]{1,0:T(8,128)(2,1)S(1)} %get-tuple-element.36.refs_3_, ...), custom_call_target="tpu_custom_call" | custom-call | flops 8000000000 | bytes 8000000 | tf_op jit(solution)/shard_map/pallas_call | solution.py:547
  57.9 0.1 collective-permute-start.16
  58.0 1.5 %collective-permute-done.16.send = f32[4,128,128]{2,1,0:T(8,128)S(1)} collective-permute-done((f32[4,128,128]{2,1,0:T(8,128)S(1)}, f32[4,128,128]{2,1,0:T(8,128)S(1)}, u32[]{:S(2)}, u32[]{:S(2)}) %collective-permute-start.16) | collective-permute-done | bytes 262176 | tf_op jit(solution)/shard_map/ppermute | solution.py:234
  59.5 2.5 %collective-permute-start.17 = (f32[128,128]{1,0:T(8,128)S(1)}, f32[128,128]{1,0:T(8,128)S(1)}, u32[]{:S(2)}, u32[]{:S(2)}) collective-permute-start(f32[128,128]{1,0:T(8,128)S(1)} %get-tuple-element.56), channel_id=1, source_target_pairs={{0,8},{8,0},{16,24},{24,16},{1,9},{9,1},{17,25},{25,17},{2,10},{10... | collective-permute-start | bytes 196616 | tf_op jit(solution)/shard_map/ppermute | solution.py:231
  62.1 0.0 collective-permute-start.18
  62.1 1.5 %collective-permute-start.19 = (f32[128,128]{1,0:T(8,128)S(1)}, f32[128,128]{1,0:T(8,128)S(1)}, u32[]{:S(2)}, u32[]{:S(2)}) collective-permute-start(f32[128,128]{1,0:T(8,128)S(1)} %get-tuple-element.58), channel_id=1, source_target_pairs={{0,24},{8,16},{16,8},{24,0},{1,25},{9,17},{17,9},{25,1},{2,26},{10... | collective-permute-start | bytes 196616 | tf_op jit(solution)/shard_map/ppermute | solution.py:231
  63.6 0.9 %collective-permute-done.17.refs_1_ = f32[128,128]{1,0:T(8,128)S(1)} collective-permute-done((f32[128,128]{1,0:T(8,128)S(1)}, f32[128,128]{1,0:T(8,128)S(1)}, u32[]{:S(2)}, u32[]{:S(2)}) %collective-permute-start.17) | collective-permute-done | bytes 65568 | tf_op jit(solution)/shard_map/ppermute | solution.py:231
  64.5 3.2 %collective-permute-done.18.refs_2_ = f32[128,128]{1,0:T(8,128)S(1)} collective-permute-done((f32[128,128]{1,0:T(8,128)S(1)}, f32[128,128]{1,0:T(8,128)S(1)}, u32[]{:S(2)}, u32[]{:S(2)}) %collective-permute-start.18) | collective-permute-done | bytes 65568 | tf_op jit(solution)/shard_map/ppermute | solution.py:231
  67.6 0.0 collective-permute-done.19.refs_3_
  67.6 0.8 %shard_map.81 = f32[2,1,2,128,128]{4,3,2,1,0:T(8,128)} custom-call(f32[128,128]{1,0:T(8,128)S(1)} %get-tuple-element.55.refs_0_, f32[128,128]{1,0:T(8,128)S(1)} %collective-permute-done.17.refs_1_, f32[128,128]{1,0:T(8,128)S(1)} %collective-permute-done.18.refs_2_, f32[128,128]{1,0:T(8,128)S(1)} %collective-permute-done.19.refs_3_), custom_call_target="tpu_custom_call" | custom-call | tf_op jit(solution)/shard_map/pallas_call | solution.py:588
  (6 shorter events, 0.2 us)
Async XLA Ops:
  0.0 7.4 %copy-start.1 = (f32[1,2,256,256]{3,2,1,0:T(8,128)S(1)}, f32[1,2,256,256]{3,2,1,0:T(8,128)}, u32[]{:S(2)}) copy-start(f32[1,2,256,256]{3,2,1,0:T(8,128)} %refs_5_.1) | copy-start | bytes 1572868
  0.7 21.3 %collective-permute-start = (f32[2,2]{1,0:T(2,128)S(1)}, f32[2,2]{1,0:T(2,128)S(1)}, u32[]{:S(2)}, u32[]{:S(2)}) collective-permute-start(f32[2,2]{1,0:T(2,128)S(1)} %pad_maximum_fusion.1.refs_1_), channel_id=1, source_target_pairs={{0,1},{1,0},{2,3},{3,2},{4,5},{5,4},{6,7},{7,6},{8,9},{9,8},{10,11... | collective-permute-start | bytes 56 | tf_op jit(solution)/shard_map/ppermute | solution.py:237
  3.8 19.0 %collective-permute-start.1 = (f32[2,2]{1,0:T(2,128)S(1)}, f32[2,2]{1,0:T(2,128)S(1)}, u32[]{:S(2)}, u32[]{:S(2)}) collective-permute-start(f32[2,2]{1,0:T(2,128)S(1)} %pad_maximum_fusion.1.refs_1_), channel_id=1, source_target_pairs={{0,2},{1,3},{2,0},{3,1},{4,6},{5,7},{6,4},{7,5},{8,10},{9,11},{10,... | collective-permute-start | bytes 56 | tf_op jit(solution)/shard_map/ppermute | solution.py:237
  6.4 17.5 %collective-permute-start.2 = (f32[2,2]{1,0:T(2,128)S(1)}, f32[2,2]{1,0:T(2,128)S(1)}, u32[]{:S(2)}, u32[]{:S(2)}) collective-permute-start(f32[2,2]{1,0:T(2,128)S(1)} %pad_maximum_fusion.1.refs_1_), channel_id=1, source_target_pairs={{0,3},{1,2},{2,1},{3,0},{4,7},{5,6},{6,5},{7,4},{8,11},{9,10},{10,... | collective-permute-start | bytes 56 | tf_op jit(solution)/shard_map/ppermute | solution.py:237
  7.4 3.5 %copy-start.3 = (f32[2,1,2,256,128]{4,3,2,1,0:T(8,128)S(1)}, f32[2,1,2,256,128]{4,3,2,1,0:T(8,128)}, u32[]{:S(2)}) copy-start(f32[2,1,2,256,128]{4,3,2,1,0:T(8,128)} %param.9) | copy-start | bytes 1572868
  7.5 3.3 %copy-start.4 = (s32[2]{0:T(128)S(1)}, s32[2]{0:T(128)}, u32[]{:S(2)}) copy-start(s32[2]{0:T(128)} %param.10) | copy-start | bytes 28
  7.5 10.4 %collective-permute-start.3 = (f32[3,128,256]{2,1,0:T(8,128)S(1)}, f32[3,128,256]{2,1,0:T(8,128)S(1)}, u32[]{:S(2)}, u32[]{:S(2)}) collective-permute-start(f32[3,128,256]{2,1,0:T(8,128)S(1)} %pad_maximum_fusion), channel_id=1, source_target_pairs={{0,8},{8,0},{16,24},{24,16},{1,9},{9,1},{17,25},{25,17},{2,10},{10... | collective-permute-start | bytes 1179656 | tf_op jit(solution)/shard_map/ppermute | solution.py:231
  9.3 9.8 %collective-permute-start.5 = (f32[3,128,256]{2,1,0:T(8,128)S(1)}, f32[3,128,256]{2,1,0:T(8,128)S(1)}, u32[]{:S(2)}, u32[]{:S(2)}) collective-permute-start(f32[3,128,256]{2,1,0:T(8,128)S(1)} %pad_maximum_fusion), channel_id=1, source_target_pairs={{0,16},{8,24},{16,0},{24,8},{1,17},{9,25},{17,1},{25,9},{2,18},{10... | collective-permute-start | bytes 1179656 | tf_op jit(solution)/shard_map/ppermute | solution.py:231
  10.9 13.0 %copy-start.2 = (s32[8]{0:T(128)S(1)}, s32[8]{0:T(128)}, u32[]{:S(2)}) copy-start(s32[8]{0:T(128)} %refs_0_.3) | copy-start | bytes 100
  17.9 24.1 %collective-permute-start.9 = (f32[2,2,128,128]{3,2,1,0:T(8,128)S(1)}, f32[2,2,128,128]{3,2,1,0:T(8,128)S(1)}, u32[]{:S(2)}, u32[]{:S(2)}) collective-permute-start(f32[2,2,128,128]{3,2,1,0:T(8,128)S(1)} %bitcast_select_fusion.refs_1_), channel_id=1, source_target_pairs={{0,1},{1,0},{2,3},{3,2},{4,5},{5,4},{6,7},{7,6},{8,9},{9,8},{10,11... | collective-permute-start | bytes 786440 | tf_op jit(solution)/shard_map/ppermute | solution.py:237
  19.1 22.9 %collective-permute-start.10 = (f32[2,2,128,128]{3,2,1,0:T(8,128)S(1)}, f32[2,2,128,128]{3,2,1,0:T(8,128)S(1)}, u32[]{:S(2)}, u32[]{:S(2)}) collective-permute-start(f32[2,2,128,128]{3,2,1,0:T(8,128)S(1)} %bitcast_select_fusion.refs_1_), channel_id=1, source_target_pairs={{0,2},{1,3},{2,0},{3,1},{4,6},{5,7},{6,4},{7,5},{8,10},{9,11},{10,... | collective-permute-start | bytes 786440 | tf_op jit(solution)/shard_map/ppermute | solution.py:237
  22.0 8.5 %copy-start = (f32[1,2,256,256]{3,2,1,0:T(8,128)S(1)}, f32[1,2,256,256]{3,2,1,0:T(8,128)}, u32[]{:S(2)}) copy-start(f32[1,2,256,256]{3,2,1,0:T(8,128)} %refs_4_.1) | copy-start | bytes 1572868
  22.1 19.9 %collective-permute-start.11 = (f32[2,2,128,128]{3,2,1,0:T(8,128)S(1)}, f32[2,2,128,128]{3,2,1,0:T(8,128)S(1)}, u32[]{:S(2)}, u32[]{:S(2)}) collective-permute-start(f32[2,2,128,128]{3,2,1,0:T(8,128)S(1)} %bitcast_select_fusion.refs_1_), channel_id=1, source_target_pairs={{0,3},{1,2},{2,1},{3,0},{4,7},{5,6},{6,5},{7,4},{8,11},{9,10},{10,... | collective-permute-start | bytes 786440 | tf_op jit(solution)/shard_map/ppermute | solution.py:237
  22.8 7.8 %collective-permute-start.7 = (f32[3,128,256]{2,1,0:T(8,128)S(1)}, f32[3,128,256]{2,1,0:T(8,128)S(1)}, u32[]{:S(2)}, u32[]{:S(2)}) collective-permute-start(f32[3,128,256]{2,1,0:T(8,128)S(1)} %broadcast_select_fusion), channel_id=1, source_target_pairs={{0,8},{8,0},{16,24},{24,16},{4,20},{12,28},{20,4},{28,12},{1,9},{9... | collective-permute-start | bytes 1179656 | tf_op jit(solution)/shard_map/ppermute | solution.py:288
  23.9 4.7 %collective-permute-start.4 = (f32[3,128,256]{2,1,0:T(8,128)S(1)}, f32[3,128,256]{2,1,0:T(8,128)S(1)}, u32[]{:S(2)}, u32[]{:S(2)}) collective-permute-start(f32[3,128,256]{2,1,0:T(8,128)S(1)} %collective-permute-done.3.refs_3_.refs_5_), channel_id=1, source_target_pairs={{0,4},{4,0},{1,5},{5,1},{2,6},{6,2},{3,7},{7,3},{8,12},{12,8},{9,1... | collective-permute-start | bytes 1179656 | tf_op jit(solution)/shard_map/ppermute | solution.py:234
  28.6 7.2 %collective-permute-start.6 = (f32[3,128,256]{2,1,0:T(8,128)S(1)}, f32[3,128,256]{2,1,0:T(8,128)S(1)}, u32[]{:S(2)}, u32[]{:S(2)}) collective-permute-start(f32[3,128,256]{2,1,0:T(8,128)S(1)} %collective-permute-done.5.refs_7_.refs_9_), channel_id=1, source_target_pairs={{0,4},{4,0},{1,5},{5,1},{2,6},{6,2},{3,7},{7,3},{8,12},{12,8},{9,1... | collective-permute-start | bytes 1179656 | tf_op jit(solution)/shard_map/ppermute | solution.py:234
  30.6 17.9 %collective-permute-start.8 = (f32[3,128,256]{2,1,0:T(8,128)S(1)}, f32[3,128,256]{2,1,0:T(8,128)S(1)}, u32[]{:S(2)}, u32[]{:S(2)}) collective-permute-start(f32[3,128,256]{2,1,0:T(8,128)S(1)} %collective-permute-done.7.refs_11_), channel_id=1, source_target_pairs={{0,4},{4,0},{1,5},{5,1},{2,6},{6,2},{3,7},{7,3},{8,12},{12,8},{9,1... | collective-permute-start | bytes 1179656 | tf_op jit(solution)/shard_map/ppermute | solution.py:234
  43.1 1.7 %collective-permute-start.12 = (f32[4,128,128]{2,1,0:T(8,128)S(1)}, f32[4,128,128]{2,1,0:T(8,128)S(1)}, u32[]{:S(2)}, u32[]{:S(2)}) collective-permute-start(f32[4,128,128]{2,1,0:T(8,128)S(1)} %shard_map.77.mine), channel_id=1, source_target_pairs={{0,4},{4,0},{1,5},{5,1},{2,6},{6,2},{3,7},{7,3},{8,12},{12,8},{9,1... | collective-permute-start | bytes 786440 | tf_op jit(solution)/shard_map/ppermute | solution.py:234
  44.9 9.2 %collective-permute-start.13 = (f32[256,128]{1,0:T(8,128)S(1)}, f32[256,128]{1,0:T(8,128)S(1)}, u32[]{:S(2)}, u32[]{:S(2)}) collective-permute-start(f32[256,128]{1,0:T(8,128)S(1)} %get-tuple-element.50), channel_id=1, source_target_pairs={{0,8},{8,0},{16,24},{24,16},{1,9},{9,1},{17,25},{25,17},{2,10},{10... | collective-permute-start | bytes 393224 | tf_op jit(solution)/shard_map/ppermute | solution.py:231
  45.9 8.3 %collective-permute-start.14 = (f32[256,128]{1,0:T(8,128)S(1)}, f32[256,128]{1,0:T(8,128)S(1)}, u32[]{:S(2)}, u32[]{:S(2)}) collective-permute-start(f32[256,128]{1,0:T(8,128)S(1)} %get-tuple-element.51), channel_id=1, source_target_pairs={{0,16},{8,24},{16,0},{24,8},{1,17},{9,25},{17,1},{25,9},{2,18},{10... | collective-permute-start | bytes 393224 | tf_op jit(solution)/shard_map/ppermute | solution.py:231
  47.6 6.6 %collective-permute-start.15 = (f32[256,128]{1,0:T(8,128)S(1)}, f32[256,128]{1,0:T(8,128)S(1)}, u32[]{:S(2)}, u32[]{:S(2)}) collective-permute-start(f32[256,128]{1,0:T(8,128)S(1)} %get-tuple-element.52), channel_id=1, source_target_pairs={{0,24},{8,16},{16,8},{24,0},{1,25},{9,17},{17,9},{25,1},{2,26},{10... | collective-permute-start | bytes 393224 | tf_op jit(solution)/shard_map/ppermute | solution.py:231
  57.9 1.6 %collective-permute-start.16 = (f32[4,128,128]{2,1,0:T(8,128)S(1)}, f32[4,128,128]{2,1,0:T(8,128)S(1)}, u32[]{:S(2)}, u32[]{:S(2)}) collective-permute-start(f32[4,128,128]{2,1,0:T(8,128)S(1)} %get-tuple-element.54), channel_id=1, source_target_pairs={{0,4},{4,0},{1,5},{5,1},{2,6},{6,2},{3,7},{7,3},{8,12},{12,8},{9,1... | collective-permute-start | bytes 786440 | tf_op jit(solution)/shard_map/ppermute | solution.py:234
  59.5 4.9 %collective-permute-start.17 = (f32[128,128]{1,0:T(8,128)S(1)}, f32[128,128]{1,0:T(8,128)S(1)}, u32[]{:S(2)}, u32[]{:S(2)}) collective-permute-start(f32[128,128]{1,0:T(8,128)S(1)} %get-tuple-element.56), channel_id=1, source_target_pairs={{0,8},{8,0},{16,24},{24,16},{1,9},{9,1},{17,25},{25,17},{2,10},{10... | collective-permute-start | bytes 196616 | tf_op jit(solution)/shard_map/ppermute | solution.py:231
  62.1 5.6 %collective-permute-start.18 = (f32[128,128]{1,0:T(8,128)S(1)}, f32[128,128]{1,0:T(8,128)S(1)}, u32[]{:S(2)}, u32[]{:S(2)}) collective-permute-start(f32[128,128]{1,0:T(8,128)S(1)} %get-tuple-element.57), channel_id=1, source_target_pairs={{0,16},{8,24},{16,0},{24,8},{1,17},{9,25},{17,1},{25,9},{2,18},{10... | collective-permute-start | bytes 196616 | tf_op jit(solution)/shard_map/ppermute | solution.py:231
  62.1 5.6 %collective-permute-start.19 = (f32[128,128]{1,0:T(8,128)S(1)}, f32[128,128]{1,0:T(8,128)S(1)}, u32[]{:S(2)}, u32[]{:S(2)}) collective-permute-start(f32[128,128]{1,0:T(8,128)S(1)} %get-tuple-element.58), channel_id=1, source_target_pairs={{0,24},{8,16},{16,8},{24,0},{1,25},{9,17},{17,9},{25,1},{2,26},{10... | collective-permute-start | bytes 196616 | tf_op jit(solution)/shard_map/ppermute | solution.py:231

commit v5 on v4

--- a/solution.py
+++ b/solution.py
@@ -33,11 +33,10 @@
     return jnp.concatenate([jnp.concatenate([re, im], 1), jnp.concatenate([-im, re], 1)], 0)
 
 
-def embed_triple(re, im):
+def embed_double(re, im):
     re_high, re_low = hi_lo(re)
     im_high, im_low = hi_lo(im)
-    high = embed(re_high, im_high)
-    return jnp.concatenate([high, high, embed(re_low, im_low)], 0)
+    return jnp.concatenate([embed(re_high, im_high), embed(re_low, im_low)], 0)
 
 
 def whole(pair):
@@ -74,14 +73,27 @@
     return (row == col).astype(F32)
 
 
-def invert(s_re, s_im, zeta_im, s_emb, x_ref, work):
+def planes(re, im):
+    return re.astype(BF16), im.astype(BF16), (re + im).astype(BF16)
+
+
+def coarse_product(left, right):
+    first, second, third = [dot(a, b) for a, b in zip(left, right)]
+    return first - second, third - first - second
+
+
+def invert(s_re, s_im, zeta_im, s_emb, x_ref, work, s_planes):
     n = s_re.shape[0]
     eye = eye_of(n)
-    s_emb[...] = embed_triple(s_re, s_im)
+    for k, plane in enumerate(planes(s_re, s_im)):
+        s_planes[k] = plane
+    s_emb[...] = embed_double(s_re, s_im)
     adj_re, adj_im = s_re.T, -s_im.T
-    gram = dot(jnp.concatenate([adj_re, adj_im], 1).astype(BF16), s_emb[0 : 2 * n, :])
+    gram_re, gram_im = coarse_product(planes(adj_re, adj_im), [s_planes[k] for k in range(3)])
     total_sq = jnp.sum(jnp.sum(s_re * s_re + s_im * s_im, 0, keepdims=True), 1, keepdims=True)
-    total_4th = jnp.sum(jnp.sum(gram * gram, 0, keepdims=True), 1, keepdims=True)
+    total_4th = jnp.sum(
+        jnp.sum(gram_re * gram_re + gram_im * gram_im, 0, keepdims=True), 1, keepdims=True
+    )
     bound_sq = ROOM * total_4th / total_sq
     bound = jnp.sqrt(bound_sq)
     ratio = jnp.abs(zeta_im) / bound
@@ -90,34 +102,42 @@
     beta = shrink / bound * jnp.where(zeta_im > 0, 1.0, -1.0)
     x_re = alpha * adj_re
     x_im = alpha * adj_im - beta * eye
-    x_ref[...] = jnp.concatenate([x_re, x_im], 1)
-    work[:, 0 : 2 * n] = embed(
-        eye - alpha * gram[:, :n] - beta * s_im, beta * s_re - alpha * gram[:, n:]
-    ).astype(BF16)
-    work[:, 2 * n :] = embed(x_re, x_im).astype(BF16)
+    x_ref[:, :n] = x_re
+    x_ref[:, n:] = x_im
+
+    def keep(first, re, im):
+        for k, plane in enumerate(planes(re, im)):
+            work[k, :, first : first + n] = plane
+
+    keep(0, eye - alpha * gram_re - beta * s_im, beta * s_re - alpha * gram_im)
+    keep(n, x_re, x_im)
 
     def double(size):
-        both = dot(work[0:n, 0 : 2 * n], work[...])
-        work[:, 0 : 2 * n] = embed(both[:, :n], both[:, n : 2 * n]).astype(BF16)
-        x_now = x_ref[...] + both[:, 2 * n :]
-        x_ref[...] = x_now
-        work[:, 2 * n :] = embed(x_now[:, :n], x_now[:, n:]).astype(BF16)
+        re, im = coarse_product([work[k, :, :n] for k in range(3)], [work[k] for k in range(3)])
+        keep(0, re[:, :n], im[:, :n])
+        x_re = x_ref[:, :n] + re[:, n:]
+        x_im = x_ref[:, n:] + im[:, n:]
+        x_ref[:, :n] = x_re
+        x_ref[:, n:] = x_im
+        keep(n, x_re, x_im)
         return size * size
 
     lax.while_loop(lambda size: size * size > COARSE, double, shrink[0, 0])
-    x_now = x_ref[...] + dot(work[0:n, 0 : 2 * n], work[:, 2 * n :])
+    re, im = coarse_product([work[k, :, :n] for k in range(3)], [work[k, :, n:] for k in range(3)])
+    x_re = x_ref[:, :n] + re
+    x_im = x_ref[:, n:] + im
+    x_planes = planes(x_re, x_im)
+    re = dot(x_planes[0], s_planes[0]) - dot(x_planes[1], s_planes[1])
+    im = dot(x_planes[0], s_planes[1]) + dot(x_planes[1], s_planes[0])
+    re, im = coarse_product(planes(eye - re, -im), x_planes)
+    x_now = jnp.concatenate([x_re + re, x_im + im], 1)
     wide_eye = jnp.concatenate([eye, jnp.zeros((n, n), F32)], 1)
-    x_emb = embed(x_now[:, :n], x_now[:, n:]).astype(BF16)
-    work[:, 2 * n :] = x_emb
-    rest = wide_eye - dot(x_emb[0:n, :], s_emb[0 : 2 * n, :])
-    x_now = x_now + dot(rest.astype(BF16), work[:, 2 * n :])
 
     def correct(value):
         rounded = embed(value[:, :n], value[:, n:]).astype(BF16)
-        work[:, 2 * n :] = rounded
         left = rounded[0:n, :]
-        rest = wide_eye - dot(jnp.concatenate([left, left], 1), s_emb[2 * n :, :])
-        x_ref[...] = left.astype(F32) + dot(rest.astype(BF16), work[:, 2 * n :])
+        rest = wide_eye - dot(jnp.concatenate([left, left], 1), s_emb[...])
+        x_ref[...] = left.astype(F32) + dot(rest.astype(BF16), rounded)
         return jnp.sum(jnp.sum(rest * rest, 0, keepdims=True), 1, keepdims=True)[0, 0]
 
     size = correct(x_now)
@@ -222,9 +242,10 @@
     grant = pltpu.CompilerParams(vmem_limit_bytes=20 * 1024 * 1024)
     pair_shape = jax.ShapeDtypeStruct((n, 4 * n), BF16)
     scratch = [
-        pltpu.VMEM((6 * n, 2 * n), BF16),
+        pltpu.VMEM((4 * n, 2 * n), BF16),
         pltpu.VMEM((n, 2 * n), F32),
-        pltpu.VMEM((2 * n, 4 * n), BF16),
+        pltpu.VMEM((3, n, 2 * n), BF16),
+        pltpu.VMEM((3, n, n), BF16),
     ]
 
     def exchange(value, distance):
@@ -260,13 +281,13 @@
     def first_body(*refs):
         scal, owner = position(), refs[0]
         tables = refs[1 : 1 + win_count]
-        diag, x_out, prm, s_emb, x_ref, work = refs[1 + win_count :]
+        diag, x_out, prm, s_emb, x_ref, work, s_planes = refs[1 + win_count :]
         z_re, z_im, weight_re, weight_im = contour(scal, owner, tables, dims, point_count)
         for k, value in enumerate((z_re, z_im, weight_re, weight_im)):
             prm[k] = value
         eye = eye_of(n)
         x_out[...] = packed_pair(
-            invert(z_re * eye - diag[0, 0], z_im * eye - diag[0, 1], z_im, s_emb, x_ref, work)
+            invert(z_re * eye - diag[0, 0], z_im * eye - diag[0, 1], z_im, s_emb, x_ref, work, s_planes)
         )
 
     head = [owner_order] + tables
@@ -292,7 +313,7 @@
 
     def second_body(*refs):
         scal, prm = position(), refs[0]
-        (x_own, own_c, x_dir, x_swp, x_out, w_out, l_out, s_emb, x_ref, work) = refs[1:]
+        (x_own, own_c, x_dir, x_swp, x_out, w_out, l_out, s_emb, x_ref, work, s_planes) = refs[1:]
         z_re, z_im = prm[0], prm[1]
         p = scal[2]
         near = [rows_of(x_dir, x_swp, k, p) for k in range(3)]
@@ -313,6 +334,7 @@
                 s_emb,
                 x_ref,
                 work,
+                s_planes,
             )
         )
 
@@ -330,7 +352,7 @@
     def third_body(*refs):
         scal, prm = position(), refs[0]
         (x_own, x_near, l_near, own_c, x_dir, x_swp, y_dir, y_swp) = refs[1:9]
-        (x_out, w_out, l_out, ahead, later, s_emb, x_ref, work, s_ref) = refs[9:]
+        (x_out, w_out, l_out, ahead, later, s_emb, x_ref, work, s_planes, s_ref) = refs[9:]
         for k in range(4):
             later[k] = prm[k]
         z_re, z_im = prm[0], prm[1]
@@ -363,7 +385,7 @@
             l_out[...] = packed_pair(jnp.concatenate([own_c[0, 0].T, -own_c[0, 1].T], 1))
             ahead[...] = product(l_near[...], cross)
 
-        x_pair = packed_pair(invert(s_ref[:, :n], s_ref[:, n:], z_im, s_emb, x_ref, work))
+        x_pair = packed_pair(invert(s_ref[:, :n], s_ref[:, n:], z_im, s_emb, x_ref, work, s_planes))
         x_out[...] = x_pair
 
         @pl.when(even_fork)
@@ -437,7 +459,7 @@
     def fourth_body(*refs):
         scal, prm = position(), refs[0]
         (x_own, x_near, x_side, w_near, l_near, w_mid, l_mid, ahead, y_dir, y_swp, f_dir, f_swp) = refs[1:13]
-        (x_out, w_far, l_far, w_cross, l_cross, w_last, l_last, s_emb, x_ref, work, s_ref, fill) = refs[13:]
+        (x_out, w_far, l_far, w_cross, l_cross, w_last, l_last, s_emb, x_ref, work, s_planes, s_ref, fill) = refs[13:]
         z_re, z_im = prm[0], prm[1]
         p = scal[2]
         even = lax.rem(scal[1], 2) == 0
@@ -498,7 +520,7 @@
             s_ref[...] = s_ref[...] - product(left, solved)
 
         s_now = s_ref[...]
-        x_out[...] = packed_pair(invert(s_now[:, :n], s_now[:, n:], z_im, s_emb, x_ref, work))
+        x_out[...] = packed_pair(invert(s_now[:, :n], s_now[:, n:], z_im, s_emb, x_ref, work, s_planes))
 
     x_far, w_far, l_far, w_cross, l_cross, w_last, l_last = pl.pallas_call(
         fourth_body,

time: 68.6 us -> 68.1 us (level)
  the two profiles are of different devices: /device:TPU:0 before, /device:TPU:10 now
where the time goes in v5:
time: 68.1 us; the launch traced here: 67.9 us
  Pallas kernels  26 us (38%)
  waiting for transfers between devices  20.9 us (31%)
  starting transfers between devices  18.8 us (28%)
  local copies, waits for them, and re-layouts  1 us (1%)
  other arithmetic  1 us (1%)
    ppermute x8, waiting for transfers between devices, exchange(): lax.ppermute(value, 'slab', [(i, i ^ distance) for i in range(slab_count)])  12.5 us
    ppermute x8, starting transfers between devices, exchange(): lax.ppermute(value, 'slab', [(i, i ^ distance) for i in range(slab_count)])  9.23 us
    ppermute x6, starting transfers between devices, along_win(): lax.ppermute(value, 'win', [(i, i ^ shift) for i in range(win_count)])  7.61 us
    pallas_call x1, Pallas kernels, per_device(): pl.pallas_call(fourth_body, out_shape=[pair_shape] * 7, in_specs=[smem] +...  6.51 us
    pallas_call x1, Pallas kernels, per_device(): pl.pallas_call(third_body, out_shape=[pair_shape] * 3 + [wide_shape, jax....  5.27 us
    pallas_call x1, Pallas kernels, per_device(): x_near, w_near, l_near = second(prm, x_own, couplings, *from_x)  4.51 us
    pallas_call x1, Pallas kernels, per_device(): x_own, prm = first(*head, diag_blocks)  3.98 us
    pallas_call x1, Pallas kernels, per_device(): pl.pallas_call(solve_body, out_shape=[quad] * 2, in_specs=[smem] + [vmem]...  3.69 us
  transfers between devices with their start and end apart: 20, of which 8 were waited for; matrix products, arithmetic and copies ran while one was open for 2% of the time, Pallas kernels for 32%

profile of v5, /device:TPU:10, one launch (start us, length us, event | category | flops | bytes accessed | tf_op | source)
XLA Modules:
  0.0 67.9 jit_solution(5675391278459229785)
XLA Ops:
  0.0 0.0 copy-start.1
  0.0 0.7 %pad_maximum_fusion.1.refs_1_ = f32[2,2]{1,0:T(2,128)S(1)} fusion(f32[1,2]{1,0:T(1,128)} %bitcast.14, f32[1,2]{1,0:T(1,128)} %bitcast.15), kind=kLoop, calls=%fused_computation.8 | loop fusion | flops 4 | bytes 32 | tf_op jit(solution)/shard_map/stack | solution.py:260
  0.7 0.4 collective-permute-start
  1.2 2.6 %collective-permute-start.1 = (f32[2,2]{1,0:T(2,128)S(1)}, f32[2,2]{1,0:T(2,128)S(1)}, u32[]{:S(2)}, u32[]{:S(2)}) collective-permute-start(f32[2,2]{1,0:T(2,128)S(1)} %pad_maximum_fusion.1.refs_1_), channel_id=1, source_target_pairs={{0,2},{1,3},{2,0},{3,1},{4,6},{5,7},{6,4},{7,5},{8,10},{9,11},{10,... | collective-permute-start | bytes 56 | tf_op jit(solution)/shard_map/ppermute | solution.py:258
  3.8 0.5 collective-permute-start.2
  4.2 1.0 %dynamic-slice_bitcast_fusion = f32[2,128,256]{2,1,0:T(8,128)S(1)} fusion(f32[1,2,256,256]{3,2,1,0:T(8,128)} %refs_4_.1, s32[]{:T(128)S(6)} %select_n.28), kind=kLoop, calls=%fused_computation.2 | loop fusion | bytes 524292 | tf_op jit(solution)/shard_map/dynamic_slice | solution.py:269
  5.2 0.0 copy-done.1
  5.2 0.0 copy-start.3
  5.2 0.1 fusion
  5.4 0.0 copy-start.4
  5.4 0.6 collective-permute-start.3
  6.0 1.5 %collective-permute-start.5 = (f32[3,128,256]{2,1,0:T(8,128)S(1)}, f32[3,128,256]{2,1,0:T(8,128)S(1)}, u32[]{:S(2)}, u32[]{:S(2)}) collective-permute-start(f32[3,128,256]{2,1,0:T(8,128)S(1)} %pad_maximum_fusion), channel_id=1, source_target_pairs={{0,16},{8,24},{16,0},{24,8},{1,17},{9,25},{17,1},{25,9},{2,18},{10... | collective-permute-start | bytes 1179656 | tf_op jit(solution)/shard_map/ppermute | solution.py:252
  7.5 0.0 copy-done.4
  7.5 0.1 iota_compare_fusion.1
  7.6 0.0 copy-done.3
  7.6 0.0 copy-start.2
  7.6 7.8 %collective-permute-done.3.refs_3_.refs_5_ = f32[3,128,256]{2,1,0:T(8,128)S(1)} collective-permute-done((f32[3,128,256]{2,1,0:T(8,128)S(1)}, f32[3,128,256]{2,1,0:T(8,128)S(1)}, u32[]{:S(2)}, u32[]{:S(2)}) %collective-permute-start.3) | collective-permute-done | bytes 393248 | tf_op jit(solution)/shard_map/ppermute | solution.py:252
  15.4 1.4 %collective-permute-start.9 = (f32[2,2,128,128]{3,2,1,0:T(8,128)S(1)}, f32[2,2,128,128]{3,2,1,0:T(8,128)S(1)}, u32[]{:S(2)}, u32[]{:S(2)}) collective-permute-start(f32[2,2,128,128]{3,2,1,0:T(8,128)S(1)} %bitcast_select_fusion.refs_1_), channel_id=1, source_target_pairs={{0,1},{1,0},{2,3},{3,2},{4,5},{5,4},{6,7},{7,6},{8,9},{9,8},{10,11... | collective-permute-start | bytes 786440 | tf_op jit(solution)/shard_map/ppermute | solution.py:258
  16.9 0.0 collective-permute-done.5.refs_7_.refs_9_
  16.9 2.3 %collective-permute-start.10 = (f32[2,2,128,128]{3,2,1,0:T(8,128)S(1)}, f32[2,2,128,128]{3,2,1,0:T(8,128)S(1)}, u32[]{:S(2)}, u32[]{:S(2)}) collective-permute-start(f32[2,2,128,128]{3,2,1,0:T(8,128)S(1)} %bitcast_select_fusion.refs_1_), channel_id=1, source_target_pairs={{0,2},{1,3},{2,0},{3,1},{4,6},{5,7},{6,4},{7,5},{8,10},{9,11},{10,... | collective-permute-start | bytes 786440 | tf_op jit(solution)/shard_map/ppermute | solution.py:258
  19.2 0.0 copy-start
  19.3 0.0 collective-permute-done.refs_2_
  19.3 0.4 collective-permute-start.11
  19.7 0.0 collective-permute-done.1.refs_3_
  19.7 1.3 %collective-permute-start.7 = (f32[3,128,256]{2,1,0:T(8,128)S(1)}, f32[3,128,256]{2,1,0:T(8,128)S(1)}, u32[]{:S(2)}, u32[]{:S(2)}) collective-permute-start(f32[3,128,256]{2,1,0:T(8,128)S(1)} %broadcast_select_fusion), channel_id=1, source_target_pairs={{0,8},{8,0},{16,24},{24,16},{4,20},{12,28},{20,4},{28,12},{1,9},{9... | collective-permute-start | bytes 1179656 | tf_op jit(solution)/shard_map/ppermute | solution.py:309
  20.9 0.0 collective-permute-done.2.refs_4_
  20.9 0.0 collective-permute-start.4
  20.9 0.0 copy-done.2
  20.9 4.0 %shard_map.73 = (bf16[256,1024]{1,0:T(8,128)(2,1)S(1)}, f32[4]{0:T(128)S(1)}) custom-call(s32[8]{0:T(128)S(1)} %copy-done.2, f32[2,2]{1,0:T(2,128)S(1)} %pad_maximum_fusion.1.refs_1_, f32[2,2]{1,0:T(2,128)S(1)} %collective-permute-done.refs_2_, f32[2,2]{1,0:T(2,128)S(1)} %collective-permute-done.1.refs_3_, f32[2,2]{1,0:T(2,128)S(1)} %collective-permute-done.2.refs_4_, ...), custom_call_target="tpu_custom_call" | custom-call | flops 6000000000 | bytes 6000000 | tf_op jit(solution)/shard_map/pallas_call | solution.py:304
  24.9 0.0 collective-permute-done.4.refs_4_.refs_6_
  24.9 0.6 collective-permute-start.6
  25.5 1.9 %collective-permute-done.7.refs_11_ = f32[3,128,256]{2,1,0:T(8,128)S(1)} collective-permute-done((f32[3,128,256]{2,1,0:T(8,128)S(1)}, f32[3,128,256]{2,1,0:T(8,128)S(1)}, u32[]{:S(2)}, u32[]{:S(2)}) %collective-permute-start.7) | collective-permute-done | bytes 393248 | tf_op jit(solution)/shard_map/ppermute | solution.py:309
  27.4 0.0 collective-permute-start.8
  27.4 0.0 copy-done
  27.4 4.5 %shard_map.74 = (bf16[256,1024]{1,0:T(8,128)(2,1)S(1)}, bf16[256,1024]{1,0:T(8,128)(2,1)S(1)}, bf16[256,1024]{1,0:T(8,128)(2,1)S(1)}) custom-call(f32[4]{0:T(128)S(1)} %get-tuple-element.32.refs_0_, bf16[256,1024]{1,0:T(8,128)(2,1)S(1)} %get-tuple-element.33.refs_1_, f32[1,2,256,256]{3,2,1,0:T(8,128)S(1)} %copy-done, ...), custom_call_target="tpu_custom_call" | custom-call | flops 8000000000 | bytes 8000000 | tf_op jit(solution)/shard_map/pallas_call | solution.py:350
  32.0 0.0 collective-permute-done.6.refs_8_.refs_10_
  32.0 5.3 %shard_map.75 = (bf16[256,1024]{1,0:T(8,128)(2,1)S(1)}, bf16[256,1024]{1,0:T(8,128)(2,1)S(1)}, bf16[256,1024]{1,0:T(8,128)(2,1)S(1)}, f32[256,512]{1,0:T(8,128)S(1)}, f32[4]{0:T(128)S(1)}) custom-call(f32[4]{0:T(128)S(1)} %get-tuple-element.32.refs_0_, bf16[256,1024]{1,0:T(8,128)(2,1)S(1)} %get-tuple-element.33.refs_1_, ...), custom_call_target="tpu_custom_call" | custom-call | flops 8000000000 | bytes 8000000 | tf_op jit(solution)/shard_map/pallas_call | solution.py:401
  37.2 0.0 collective-permute-done.9.refs_2_
  37.2 0.0 collective-permute-done.10.refs_3_
  37.3 3.5 %collective-permute-done.11.refs_4_ = f32[2,2,128,128]{3,2,1,0:T(8,128)S(1)} collective-permute-done((f32[2,2,128,128]{3,2,1,0:T(8,128)S(1)}, f32[2,2,128,128]{3,2,1,0:T(8,128)S(1)}, u32[]{:S(2)}, u32[]{:S(2)}) %collective-permute-start.11) | collective-permute-done | bytes 262176 | tf_op jit(solution)/shard_map/ppermute | solution.py:258
  40.7 1.1 %shard_map.77.mine = f32[4,128,128]{2,1,0:T(8,128)S(1)} custom-call(s32[8]{0:T(128)S(1)} %copy-done.2, f32[2,2,128,128]{3,2,1,0:T(8,128)S(1)} %bitcast_select_fusion.refs_1_, f32[2,2,128,128]{3,2,1,0:T(8,128)S(1)} %collective-permute-done.9.refs_2_, f32[2,2,128,128]{3,2,1,0:T(8,128)S(1)} %collective-permute-done.10.refs_3_, ...), custom_call_target="tpu_custom_call" | custom-call | flops 2000000000 | bytes 2000000 | tf_op jit(solution)/shard_map/pallas_call | solution.py:435
  41.8 0.1 collective-permute-start.12
  41.9 1.5 %collective-permute-done.12.other = f32[4,128,128]{2,1,0:T(8,128)S(1)} collective-permute-done((f32[4,128,128]{2,1,0:T(8,128)S(1)}, f32[4,128,128]{2,1,0:T(8,128)S(1)}, u32[]{:S(2)}, u32[]{:S(2)}) %collective-permute-start.12) | collective-permute-done | bytes 262176 | tf_op jit(solution)/shard_map/ppermute | solution.py:255
  43.5 0.6 collective-permute-start.13
  44.1 1.5 %collective-permute-start.14 = (f32[256,128]{1,0:T(8,128)S(1)}, f32[256,128]{1,0:T(8,128)S(1)}, u32[]{:S(2)}, u32[]{:S(2)}) collective-permute-start(f32[256,128]{1,0:T(8,128)S(1)} %get-tuple-element.51), channel_id=1, source_target_pairs={{0,16},{8,24},{16,0},{24,8},{1,17},{9,25},{17,1},{25,9},{2,18},{10... | collective-permute-start | bytes 393224 | tf_op jit(solution)/shard_map/ppermute | solution.py:252
  45.6 1.4 %collective-permute-start.15 = (f32[256,128]{1,0:T(8,128)S(1)}, f32[256,128]{1,0:T(8,128)S(1)}, u32[]{:S(2)}, u32[]{:S(2)}) collective-permute-start(f32[256,128]{1,0:T(8,128)S(1)} %get-tuple-element.52), channel_id=1, source_target_pairs={{0,24},{8,16},{16,8},{24,0},{1,25},{9,17},{17,9},{25,1},{2,26},{10... | collective-permute-start | bytes 393224 | tf_op jit(solution)/shard_map/ppermute | solution.py:252
  47.0 0.0 collective-permute-done.8.refs_12_
  47.0 6.5 %shard_map.76 = (bf16[256,1024]{1,0:T(8,128)(2,1)S(1)}, bf16[256,1024]{1,0:T(8,128)(2,1)S(1)}, bf16[256,1024]{1,0:T(8,128)(2,1)S(1)}, bf16[256,1024]{1,0:T(8,128...) custom-call(f32[4]{0:T(128)S(1)} %get-tuple-element.32.refs_0_, ...), custom_call_target="tpu_custom_call" | custom-call | flops 10000000000 | bytes 10000000 | tf_op jit(solution)/shard_map/pallas_call | solution.py:525
  53.5 0.0 collective-permute-done.13.refs_14_
  53.5 0.0 collective-permute-done.14.refs_15_
  53.6 0.0 collective-permute-done.15.refs_16_
  53.6 3.7 %shard_map.79 = (f32[4,128,128]{2,1,0:T(8,128)S(1)}, f32[4,128,128]{2,1,0:T(8,128)S(1)}) custom-call(f32[4]{0:T(128)S(1)} %get-tuple-element.32.refs_0_, bf16[256,1024]{1,0:T(8,128)(2,1)S(1)} %get-tuple-element.33.refs_1_, bf16[256,1024]{1,0:T(8,128)(2,1)S(1)} %get-tuple-element.34.refs_2_, bf16[256,1024]{1,0:T(8,128)(2,1)S(1)} %get-tuple-element.36.refs_3_, ...), custom_call_target="tpu_custom_call" | custom-call | flops 8000000000 | bytes 8000000 | tf_op jit(solution)/shard_map/pallas_call | solution.py:569
  57.3 0.1 collective-permute-start.16
  57.3 1.5 %collective-permute-done.16.send = f32[4,128,128]{2,1,0:T(8,128)S(1)} collective-permute-done((f32[4,128,128]{2,1,0:T(8,128)S(1)}, f32[4,128,128]{2,1,0:T(8,128)S(1)}, u32[]{:S(2)}, u32[]{:S(2)}) %collective-permute-start.16) | collective-permute-done | bytes 262176 | tf_op jit(solution)/shard_map/ppermute | solution.py:255
  58.9 0.1 collective-permute-start.17
  59.0 2.9 %collective-permute-start.18 = (f32[128,128]{1,0:T(8,128)S(1)}, f32[128,128]{1,0:T(8,128)S(1)}, u32[]{:S(2)}, u32[]{:S(2)}) collective-permute-start(f32[128,128]{1,0:T(8,128)S(1)} %get-tuple-element.57), channel_id=1, source_target_pairs={{0,16},{8,24},{16,0},{24,8},{1,17},{9,25},{17,1},{25,9},{2,18},{10... | collective-permute-start | bytes 196616 | tf_op jit(solution)/shard_map/ppermute | solution.py:252
  61.9 0.5 collective-permute-start.19
  62.5 0.8 %collective-permute-done.17.refs_1_ = f32[128,128]{1,0:T(8,128)S(1)} collective-permute-done((f32[128,128]{1,0:T(8,128)S(1)}, f32[128,128]{1,0:T(8,128)S(1)}, u32[]{:S(2)}, u32[]{:S(2)}) %collective-permute-start.17) | collective-permute-done | bytes 65568 | tf_op jit(solution)/shard_map/ppermute | solution.py:252
  63.2 1.7 %collective-permute-done.18.refs_2_ = f32[128,128]{1,0:T(8,128)S(1)} collective-permute-done((f32[128,128]{1,0:T(8,128)S(1)}, f32[128,128]{1,0:T(8,128)S(1)}, u32[]{:S(2)}, u32[]{:S(2)}) %collective-permute-start.18) | collective-permute-done | bytes 65568 | tf_op jit(solution)/shard_map/ppermute | solution.py:252
  64.9 2.2 %collective-permute-done.19.refs_3_ = f32[128,128]{1,0:T(8,128)S(1)} collective-permute-done((f32[128,128]{1,0:T(8,128)S(1)}, f32[128,128]{1,0:T(8,128)S(1)}, u32[]{:S(2)}, u32[]{:S(2)}) %collective-permute-start.19) | collective-permute-done | bytes 65568 | tf_op jit(solution)/shard_map/ppermute | solution.py:252
  67.1 0.8 %shard_map.81 = f32[2,1,2,128,128]{4,3,2,1,0:T(8,128)} custom-call(f32[128,128]{1,0:T(8,128)S(1)} %get-tuple-element.55.refs_0_, f32[128,128]{1,0:T(8,128)S(1)} %collective-permute-done.17.refs_1_, f32[128,128]{1,0:T(8,128)S(1)} %collective-permute-done.18.refs_2_, f32[128,128]{1,0:T(8,128)S(1)} %collective-permute-done.19.refs_3_), custom_call_target="tpu_custom_call" | custom-call | tf_op jit(solution)/shard_map/pallas_call | solution.py:610
  (6 shorter events, 0.2 us)
Async XLA Ops:
  0.0 5.2 %copy-start.1 = (f32[1,2,256,256]{3,2,1,0:T(8,128)S(1)}, f32[1,2,256,256]{3,2,1,0:T(8,128)}, u32[]{:S(2)}) copy-start(f32[1,2,256,256]{3,2,1,0:T(8,128)} %refs_5_.1) | copy-start | bytes 1572868
  0.7 18.5 %collective-permute-start = (f32[2,2]{1,0:T(2,128)S(1)}, f32[2,2]{1,0:T(2,128)S(1)}, u32[]{:S(2)}, u32[]{:S(2)}) collective-permute-start(f32[2,2]{1,0:T(2,128)S(1)} %pad_maximum_fusion.1.refs_1_), channel_id=1, source_target_pairs={{0,1},{1,0},{2,3},{3,2},{4,5},{5,4},{6,7},{7,6},{8,9},{9,8},{10,11... | collective-permute-start | bytes 56 | tf_op jit(solution)/shard_map/ppermute | solution.py:258
  1.2 18.5 %collective-permute-start.1 = (f32[2,2]{1,0:T(2,128)S(1)}, f32[2,2]{1,0:T(2,128)S(1)}, u32[]{:S(2)}, u32[]{:S(2)}) collective-permute-start(f32[2,2]{1,0:T(2,128)S(1)} %pad_maximum_fusion.1.refs_1_), channel_id=1, source_target_pairs={{0,2},{1,3},{2,0},{3,1},{4,6},{5,7},{6,4},{7,5},{8,10},{9,11},{10,... | collective-permute-start | bytes 56 | tf_op jit(solution)/shard_map/ppermute | solution.py:258
  3.8 17.1 %collective-permute-start.2 = (f32[2,2]{1,0:T(2,128)S(1)}, f32[2,2]{1,0:T(2,128)S(1)}, u32[]{:S(2)}, u32[]{:S(2)}) collective-permute-start(f32[2,2]{1,0:T(2,128)S(1)} %pad_maximum_fusion.1.refs_1_), channel_id=1, source_target_pairs={{0,3},{1,2},{2,1},{3,0},{4,7},{5,6},{6,5},{7,4},{8,11},{9,10},{10,... | collective-permute-start | bytes 56 | tf_op jit(solution)/shard_map/ppermute | solution.py:258
  5.2 2.4 %copy-start.3 = (f32[2,1,2,256,128]{4,3,2,1,0:T(8,128)S(1)}, f32[2,1,2,256,128]{4,3,2,1,0:T(8,128)}, u32[]{:S(2)}) copy-start(f32[2,1,2,256,128]{4,3,2,1,0:T(8,128)} %param.9) | copy-start | bytes 1572868
  5.4 2.1 %copy-start.4 = (s32[2]{0:T(128)S(1)}, s32[2]{0:T(128)}, u32[]{:S(2)}) copy-start(s32[2]{0:T(128)} %param.10) | copy-start | bytes 28
  5.4 10.1 %collective-permute-start.3 = (f32[3,128,256]{2,1,0:T(8,128)S(1)}, f32[3,128,256]{2,1,0:T(8,128)S(1)}, u32[]{:S(2)}, u32[]{:S(2)}) collective-permute-start(f32[3,128,256]{2,1,0:T(8,128)S(1)} %pad_maximum_fusion), channel_id=1, source_target_pairs={{0,8},{8,0},{16,24},{24,16},{1,9},{9,1},{17,25},{25,17},{2,10},{10... | collective-permute-start | bytes 1179656 | tf_op jit(solution)/shard_map/ppermute | solution.py:252
  6.0 10.9 %collective-permute-start.5 = (f32[3,128,256]{2,1,0:T(8,128)S(1)}, f32[3,128,256]{2,1,0:T(8,128)S(1)}, u32[]{:S(2)}, u32[]{:S(2)}) collective-permute-start(f32[3,128,256]{2,1,0:T(8,128)S(1)} %pad_maximum_fusion), channel_id=1, source_target_pairs={{0,16},{8,24},{16,0},{24,8},{1,17},{9,25},{17,1},{25,9},{2,18},{10... | collective-permute-start | bytes 1179656 | tf_op jit(solution)/shard_map/ppermute | solution.py:252
  7.6 13.3 %copy-start.2 = (s32[8]{0:T(128)S(1)}, s32[8]{0:T(128)}, u32[]{:S(2)}) copy-start(s32[8]{0:T(128)} %refs_0_.3) | copy-start | bytes 100
  15.4 21.8 %collective-permute-start.9 = (f32[2,2,128,128]{3,2,1,0:T(8,128)S(1)}, f32[2,2,128,128]{3,2,1,0:T(8,128)S(1)}, u32[]{:S(2)}, u32[]{:S(2)}) collective-permute-start(f32[2,2,128,128]{3,2,1,0:T(8,128)S(1)} %bitcast_select_fusion.refs_1_), channel_id=1, source_target_pairs={{0,1},{1,0},{2,3},{3,2},{4,5},{5,4},{6,7},{7,6},{8,9},{9,8},{10,11... | collective-permute-start | bytes 786440 | tf_op jit(solution)/shard_map/ppermute | solution.py:258
  16.9 20.4 %collective-permute-start.10 = (f32[2,2,128,128]{3,2,1,0:T(8,128)S(1)}, f32[2,2,128,128]{3,2,1,0:T(8,128)S(1)}, u32[]{:S(2)}, u32[]{:S(2)}) collective-permute-start(f32[2,2,128,128]{3,2,1,0:T(8,128)S(1)} %bitcast_select_fusion.refs_1_), channel_id=1, source_target_pairs={{0,2},{1,3},{2,0},{3,1},{4,6},{5,7},{6,4},{7,5},{8,10},{9,11},{10,... | collective-permute-start | bytes 786440 | tf_op jit(solution)/shard_map/ppermute | solution.py:258
  19.2 8.2 %copy-start = (f32[1,2,256,256]{3,2,1,0:T(8,128)S(1)}, f32[1,2,256,256]{3,2,1,0:T(8,128)}, u32[]{:S(2)}) copy-start(f32[1,2,256,256]{3,2,1,0:T(8,128)} %refs_4_.1) | copy-start | bytes 1572868
  19.3 21.5 %collective-permute-start.11 = (f32[2,2,128,128]{3,2,1,0:T(8,128)S(1)}, f32[2,2,128,128]{3,2,1,0:T(8,128)S(1)}, u32[]{:S(2)}, u32[]{:S(2)}) collective-permute-start(f32[2,2,128,128]{3,2,1,0:T(8,128)S(1)} %bitcast_select_fusion.refs_1_), channel_id=1, source_target_pairs={{0,3},{1,2},{2,1},{3,0},{4,7},{5,6},{6,5},{7,4},{8,11},{9,10},{10,... | collective-permute-start | bytes 786440 | tf_op jit(solution)/shard_map/ppermute | solution.py:258
  19.7 7.8 %collective-permute-start.7 = (f32[3,128,256]{2,1,0:T(8,128)S(1)}, f32[3,128,256]{2,1,0:T(8,128)S(1)}, u32[]{:S(2)}, u32[]{:S(2)}) collective-permute-start(f32[3,128,256]{2,1,0:T(8,128)S(1)} %broadcast_select_fusion), channel_id=1, source_target_pairs={{0,8},{8,0},{16,24},{24,16},{4,20},{12,28},{20,4},{28,12},{1,9},{9... | collective-permute-start | bytes 1179656 | tf_op jit(solution)/shard_map/ppermute | solution.py:309
  20.9 4.0 %collective-permute-start.4 = (f32[3,128,256]{2,1,0:T(8,128)S(1)}, f32[3,128,256]{2,1,0:T(8,128)S(1)}, u32[]{:S(2)}, u32[]{:S(2)}) collective-permute-start(f32[3,128,256]{2,1,0:T(8,128)S(1)} %collective-permute-done.3.refs_3_.refs_5_), channel_id=1, source_target_pairs={{0,4},{4,0},{1,5},{5,1},{2,6},{6,2},{3,7},{7,3},{8,12},{12,8},{9,1... | collective-permute-start | bytes 1179656 | tf_op jit(solution)/shard_map/ppermute | solution.py:255
  24.9 7.0 %collective-permute-start.6 = (f32[3,128,256]{2,1,0:T(8,128)S(1)}, f32[3,128,256]{2,1,0:T(8,128)S(1)}, u32[]{:S(2)}, u32[]{:S(2)}) collective-permute-start(f32[3,128,256]{2,1,0:T(8,128)S(1)} %collective-permute-done.5.refs_7_.refs_9_), channel_id=1, source_target_pairs={{0,4},{4,0},{1,5},{5,1},{2,6},{6,2},{3,7},{7,3},{8,12},{12,8},{9,1... | collective-permute-start | bytes 1179656 | tf_op jit(solution)/shard_map/ppermute | solution.py:255
  27.4 19.6 %collective-permute-start.8 = (f32[3,128,256]{2,1,0:T(8,128)S(1)}, f32[3,128,256]{2,1,0:T(8,128)S(1)}, u32[]{:S(2)}, u32[]{:S(2)}) collective-permute-start(f32[3,128,256]{2,1,0:T(8,128)S(1)} %collective-permute-done.7.refs_11_), channel_id=1, source_target_pairs={{0,4},{4,0},{1,5},{5,1},{2,6},{6,2},{3,7},{7,3},{8,12},{12,8},{9,1... | collective-permute-start | bytes 1179656 | tf_op jit(solution)/shard_map/ppermute | solution.py:255
  41.8 1.6 %collective-permute-start.12 = (f32[4,128,128]{2,1,0:T(8,128)S(1)}, f32[4,128,128]{2,1,0:T(8,128)S(1)}, u32[]{:S(2)}, u32[]{:S(2)}) collective-permute-start(f32[4,128,128]{2,1,0:T(8,128)S(1)} %shard_map.77.mine), channel_id=1, source_target_pairs={{0,4},{4,0},{1,5},{5,1},{2,6},{6,2},{3,7},{7,3},{8,12},{12,8},{9,1... | collective-permute-start | bytes 786440 | tf_op jit(solution)/shard_map/ppermute | solution.py:255
  43.5 10.1 %collective-permute-start.13 = (f32[256,128]{1,0:T(8,128)S(1)}, f32[256,128]{1,0:T(8,128)S(1)}, u32[]{:S(2)}, u32[]{:S(2)}) collective-permute-start(f32[256,128]{1,0:T(8,128)S(1)} %get-tuple-element.50), channel_id=1, source_target_pairs={{0,8},{8,0},{16,24},{24,16},{1,9},{9,1},{17,25},{25,17},{2,10},{10... | collective-permute-start | bytes 393224 | tf_op jit(solution)/shard_map/ppermute | solution.py:252
  44.1 9.5 %collective-permute-start.14 = (f32[256,128]{1,0:T(8,128)S(1)}, f32[256,128]{1,0:T(8,128)S(1)}, u32[]{:S(2)}, u32[]{:S(2)}) collective-permute-start(f32[256,128]{1,0:T(8,128)S(1)} %get-tuple-element.51), channel_id=1, source_target_pairs={{0,16},{8,24},{16,0},{24,8},{1,17},{9,25},{17,1},{25,9},{2,18},{10... | collective-permute-start | bytes 393224 | tf_op jit(solution)/shard_map/ppermute | solution.py:252
  45.6 8.0 %collective-permute-start.15 = (f32[256,128]{1,0:T(8,128)S(1)}, f32[256,128]{1,0:T(8,128)S(1)}, u32[]{:S(2)}, u32[]{:S(2)}) collective-permute-start(f32[256,128]{1,0:T(8,128)S(1)} %get-tuple-element.52), channel_id=1, source_target_pairs={{0,24},{8,16},{16,8},{24,0},{1,25},{9,17},{17,9},{25,1},{2,26},{10... | collective-permute-start | bytes 393224 | tf_op jit(solution)/shard_map/ppermute | solution.py:252
  57.3 1.6 %collective-permute-start.16 = (f32[4,128,128]{2,1,0:T(8,128)S(1)}, f32[4,128,128]{2,1,0:T(8,128)S(1)}, u32[]{:S(2)}, u32[]{:S(2)}) collective-permute-start(f32[4,128,128]{2,1,0:T(8,128)S(1)} %get-tuple-element.54), channel_id=1, source_target_pairs={{0,4},{4,0},{1,5},{5,1},{2,6},{6,2},{3,7},{7,3},{8,12},{12,8},{9,1... | collective-permute-start | bytes 786440 | tf_op jit(solution)/shard_map/ppermute | solution.py:255
  58.9 4.3 %collective-permute-start.17 = (f32[128,128]{1,0:T(8,128)S(1)}, f32[128,128]{1,0:T(8,128)S(1)}, u32[]{:S(2)}, u32[]{:S(2)}) collective-permute-start(f32[128,128]{1,0:T(8,128)S(1)} %get-tuple-element.56), channel_id=1, source_target_pairs={{0,8},{8,0},{16,24},{24,16},{1,9},{9,1},{17,25},{25,17},{2,10},{10... | collective-permute-start | bytes 196616 | tf_op jit(solution)/shard_map/ppermute | solution.py:252
  59.0 5.9 %collective-permute-start.18 = (f32[128,128]{1,0:T(8,128)S(1)}, f32[128,128]{1,0:T(8,128)S(1)}, u32[]{:S(2)}, u32[]{:S(2)}) collective-permute-start(f32[128,128]{1,0:T(8,128)S(1)} %get-tuple-element.57), channel_id=1, source_target_pairs={{0,16},{8,24},{16,0},{24,8},{1,17},{9,25},{17,1},{25,9},{2,18},{10... | collective-permute-start | bytes 196616 | tf_op jit(solution)/shard_map/ppermute | solution.py:252
  61.9 5.2 %collective-permute-start.19 = (f32[128,128]{1,0:T(8,128)S(1)}, f32[128,128]{1,0:T(8,128)S(1)}, u32[]{:S(2)}, u32[]{:S(2)}) collective-permute-start(f32[128,128]{1,0:T(8,128)S(1)} %get-tuple-element.58), channel_id=1, source_target_pairs={{0,24},{8,16},{16,8},{24,0},{1,25},{9,17},{17,9},{25,1},{2,26},{10... | collective-permute-start | bytes 196616 | tf_op jit(solution)/shard_map/ppermute | solution.py:252
